TPU v7x, 32 devices: a whole 2x2x4 slice. The times are simulated.
32 devices in a mesh: head: 4 (over x, core), blk: 8 (over z, y).
Axes of the slice: x: 2, y: 2, z: 4, core: 2. Of those that a mesh axis runs over, the one named last changes fastest.
Arguments:
- inputs: bfloat16 [4, 1024, 768], P('head', 'blk'), may hold values from -6 to 6
- segments: int32 [4, 1024], P('head', 'blk'), may hold values from 0 to 10, as said below
- w_query: bfloat16 [768, 768], P(('head', 'blk')), may hold values from -0.109375 to 0.109375
- w_key: bfloat16 [768, 768], P(('head', 'blk')), may hold values from -0.109375 to 0.109375
- w_value: bfloat16 [768, 768], P(('head', 'blk')), may hold values from -0.21875 to 0.21875
- w_out: bfloat16 [768, 768], P(('head', 'blk')), may hold values from -0.875 to 0.875
- w_in: bfloat16 [768, 3072], P(('head', 'blk')), may hold values from -0.21875 to 0.21875
- w_back: bfloat16 [3072, 768], P(('head', 'blk')), may hold values from -0.109375 to 0.109375
- w_proj: bfloat16 [768, 128], P(('head', 'blk')), may hold values from -0.21875 to 0.21875
- gain_attn: bfloat16 [768], P(('head', 'blk')), may hold values from 0.5 to 1.5
- gain_ffn: bfloat16 [768], P(('head', 'blk')), may hold values from 0.5 to 1.5
- gain_final: bfloat16 [768], P(('head', 'blk')), may hold values from 0.5 to 1.5
- rel_table: bfloat16 [32, 12], replicated, may hold values from -4 to 4
- cotangent: bfloat16 [4, 1024, 128], P('head', 'blk'), may hold values from -6 to 6
Outputs:
- states: bfloat16 [4, 1024, 128], P('head', 'blk')
- input_gradient_rows: float32 [4, 1024, 768], P('head', 'blk')
- grad_query: float32 [768, 768], P(('head', 'blk'))
- grad_key: float32 [768, 768], P(('head', 'blk'))
- grad_value: float32 [768, 768], P(('head', 'blk'))
- grad_out: float32 [768, 768], P(('head', 'blk'))
- grad_in: float32 [768, 3072], P(('head', 'blk'))
- grad_back: float32 [3072, 768], P(('head', 'blk'))
- grad_proj: float32 [768, 128], P(('head', 'blk'))
- grad_gain_attn: float32 [768], P(('head', 'blk'))
- grad_gain_ffn: float32 [768], P(('head', 'blk'))
- grad_gain_final: float32 [768], P(('head', 'blk'))
- grad_table: float32 [32, 12], replicated
Inputs may be any that keep to these rules, and one draw needn't show every extreme that they name: `segments`: within each of the 4 sequences the numbers start at 0 at the first position and never fall; equal numbers mark one document. In one sequence, drawn from the seed, a single document covers all positions from 127 to 896.
All inputs are finite; a program needn't handle non-finite values.
Results may differ from a plain program's by a relative error of at most 0.014.
The roundings to bfloat16 on the way count: a program that leaves them out, or rounds other values in their place, can miss the bound.
Values may be sent and summed in bfloat16 or wider, within the bound.
No kernel may reach another device: no remote copies, remote signals or barrier semaphores. Data moves between devices by JAX's collectives and lax.ppermute only.
A program may use at most 192 MiB of HBM per device.

v0:
```python
import jax
import jax.numpy as jnp
from jax import lax
from jax.sharding import PartitionSpec as P

bucket_borders = (12, 16, 23, 32, 46, 64, 91)
masked_value = -1e30


def bucket_of(offset):
    distance = jnp.abs(offset)
    beyond = 8 + sum(((distance >= border).astype(jnp.int32) for border in bucket_borders))
    within = jnp.minimum(jnp.where(distance < 8, distance, beyond), 15)
    return within + 16 * (offset > 0).astype(jnp.int32)


def norm_gain(value_vectors, weights):
    factor = lax.rsqrt(jnp.mean(value_vectors * value_vectors, axis=-1, keepdims=True) + 1e-06)
    return value_vectors * factor * weights


def tile_scores(queries, keys_tile, query_pos, key_pos, query_seg, key_seg, head_table):
    products = jnp.einsum("sihe,sjhe->shij", queries, keys_tile, preferred_element_type=jnp.float32)
    buckets = bucket_of(key_pos[None, :] - query_pos[:, None])
    bucket_ids = jnp.arange(head_table.shape[1], dtype=jnp.int32)
    onehot = (buckets[None] == bucket_ids[:, None, None]).astype(jnp.float32)
    rel_bias = jnp.einsum("hb,bij->hij", head_table, onehot, precision=lax.Precision.HIGHEST)
    allowed = query_seg[:, None, :, None] == key_seg[:, None, None, :]
    return (products + rel_bias[None], allowed, onehot)


def tile_probs(logit_scores, allowed, logsum):
    return jnp.where(allowed, jnp.exp(logit_scores - logsum[..., None]), 0.0)


def body(
    inputs,
    segments,
    w_query,
    w_key,
    w_value,
    w_out,
    w_in,
    w_back,
    w_proj,
    gain_attn,
    gain_ffn,
    gain_final,
    rel_table,
    cotangent,
):
    tokens = inputs.shape[1]
    model_width = inputs.shape[2]
    groups = lax.axis_size("head")
    blocks = lax.axis_size("blk")
    head_count = rel_table.shape[1]
    bucket_total = rel_table.shape[0]
    local_heads = head_count // groups
    head_size = model_width // head_count
    lane_width = local_heads * head_size
    seq_length = tokens * blocks
    key_block = min(512, seq_length)
    key_count = seq_length // key_block
    head_shape = (groups, tokens, local_heads, head_size)
    document = lax.all_gather(segments, ("head", "blk"), axis=0, tiled=True).reshape(
        groups, seq_length
    )
    gathered = (
        lax.all_gather(w_query, ("head", "blk"), axis=0, tiled=True),
        lax.all_gather(w_key, ("head", "blk"), axis=0, tiled=True),
        lax.all_gather(w_value, ("head", "blk"), axis=0, tiled=True),
        lax.all_gather(w_out, ("head", "blk"), axis=0, tiled=True),
        lax.all_gather(w_in, ("head", "blk"), axis=0, tiled=True),
        lax.all_gather(w_back, ("head", "blk"), axis=0, tiled=True),
        lax.all_gather(w_proj, ("head", "blk"), axis=0, tiled=True),
        lax.all_gather(gain_attn, ("head", "blk"), axis=0, tiled=True),
        lax.all_gather(gain_ffn, ("head", "blk"), axis=0, tiled=True),
        lax.all_gather(gain_final, ("head", "blk"), axis=0, tiled=True),
    )
    (
        full_query,
        full_key,
        full_value,
        full_out,
        full_in,
        full_back,
        full_proj,
        gain_one,
        gain_two,
        gain_three,
    ) = gathered
    states_in = inputs[0].astype(jnp.float32)
    normed_one, back_one = jax.vjp(norm_gain, states_in, gain_one.astype(jnp.float32))
    hidden_one = normed_one.astype(jnp.bfloat16)
    query_rows = jnp.dot(hidden_one, full_query, preferred_element_type=jnp.float32).astype(
        jnp.bfloat16
    )
    key_rows = jnp.dot(hidden_one, full_key, preferred_element_type=jnp.float32).astype(
        jnp.bfloat16
    )
    value_rows = jnp.dot(hidden_one, full_value, preferred_element_type=jnp.float32).astype(
        jnp.bfloat16
    )
    query_heads, key_heads, value_heads = (
        lax.all_to_all(query_rows[None], "head", split_axis=2, concat_axis=0, tiled=True),
        lax.all_to_all(key_rows[None], "head", split_axis=2, concat_axis=0, tiled=True),
        lax.all_to_all(value_rows[None], "head", split_axis=2, concat_axis=0, tiled=True),
    )
    key_all, value_all = (
        lax.all_gather(key_heads, "blk", axis=1, tiled=True),
        lax.all_gather(value_heads, "blk", axis=1, tiled=True),
    )
    first_pos = lax.axis_index("blk") * tokens
    query_pos = first_pos + jnp.arange(tokens, dtype=jnp.int32)
    query_seg = lax.dynamic_slice_in_dim(document, first_pos, tokens, 1)
    head_table = lax.dynamic_slice_in_dim(
        rel_table.astype(jnp.float32).T, lax.axis_index("head") * local_heads, local_heads, 0
    )
    query_view = query_heads.reshape(head_shape)

    def key_tile(first_key, length):
        keys_tile = lax.dynamic_slice_in_dim(key_all, first_key, length, 1).reshape(
            groups, length, local_heads, head_size
        )
        values_tile = lax.dynamic_slice_in_dim(value_all, first_key, length, 1).reshape(
            groups, length, local_heads, head_size
        )
        key_pos = first_key + jnp.arange(length, dtype=jnp.int32)
        key_seg = lax.dynamic_slice_in_dim(document, first_key, length, 1)
        return (keys_tile, values_tile, key_pos, key_seg)

    def stats_step(carried, block_index):
        running_high, running_sum = carried
        keys_tile, values_tile, key_pos, key_seg = key_tile(block_index * key_block, key_block)
        logit_scores, allowed, onehot = tile_scores(
            query_view, keys_tile, query_pos, key_pos, query_seg, key_seg, head_table
        )
        masked = jnp.where(allowed, logit_scores, masked_value)
        new_high = jnp.maximum(running_high, jnp.max(masked, axis=-1))
        expsum = jnp.sum(jnp.where(allowed, jnp.exp(masked - new_high[..., None]), 0.0), axis=-1)
        return ((new_high, running_sum * jnp.exp(running_high - new_high) + expsum), None)

    start_high = jnp.full((groups, local_heads, tokens), masked_value, jnp.float32)
    (highest, summed), unused = lax.scan(
        stats_step, (start_high, jnp.zeros_like(start_high)), jnp.arange(key_count)
    )
    logsum = highest + jnp.log(summed)

    def value_step(carried, block_index):
        keys_tile, values_tile, key_pos, key_seg = key_tile(block_index * key_block, key_block)
        logit_scores, allowed, onehot = tile_scores(
            query_view, keys_tile, query_pos, key_pos, query_seg, key_seg, head_table
        )
        softmax = tile_probs(logit_scores, allowed, logsum).astype(jnp.bfloat16)
        return (
            carried
            + jnp.einsum(
                "shij,sjhe->sihe", softmax, values_tile, preferred_element_type=jnp.float32
            ),
            None,
        )

    attended, unused = lax.scan(
        value_step, jnp.zeros(head_shape, jnp.float32), jnp.arange(key_count)
    )
    attended_low = attended.astype(jnp.bfloat16).reshape(groups, tokens, lane_width)
    mixed_rows = lax.all_to_all(attended_low, "head", split_axis=0, concat_axis=2, tiled=True)[0]
    attention_row_block = jnp.dot(mixed_rows, full_out, preferred_element_type=jnp.float32)
    resid_one = states_in + attention_row_block
    normed_two, back_two = jax.vjp(norm_gain, resid_one, gain_two.astype(jnp.float32))
    hidden_two = normed_two.astype(jnp.bfloat16)
    upward = jnp.dot(hidden_two, full_in, preferred_element_type=jnp.float32)
    active, back_gelu = jax.vjp(
        lambda value_vectors: jax.nn.gelu(value_vectors, approximate=True), upward
    )
    active_low = active.astype(jnp.bfloat16)
    resid_two = resid_one + jnp.dot(active_low, full_back, preferred_element_type=jnp.float32)
    normed_three, back_three = jax.vjp(norm_gain, resid_two, gain_three.astype(jnp.float32))
    final_low = normed_three.astype(jnp.bfloat16)
    states = jnp.dot(final_low, full_proj, preferred_element_type=jnp.float32).astype(jnp.bfloat16)
    full_query, full_key, full_value, full_out, full_in, full_back, full_proj = (
        lax.all_gather(w_query, ("head", "blk"), axis=0, tiled=True),
        lax.all_gather(w_key, ("head", "blk"), axis=0, tiled=True),
        lax.all_gather(w_value, ("head", "blk"), axis=0, tiled=True),
        lax.all_gather(w_out, ("head", "blk"), axis=0, tiled=True),
        lax.all_gather(w_in, ("head", "blk"), axis=0, tiled=True),
        lax.all_gather(w_back, ("head", "blk"), axis=0, tiled=True),
        lax.all_gather(w_proj, ("head", "blk"), axis=0, tiled=True),
    )
    incoming_cotangent = cotangent[0]
    grad_proj = jnp.einsum(
        "td,tp->dp", final_low, incoming_cotangent, preferred_element_type=jnp.float32
    )
    grad_final = jnp.dot(incoming_cotangent, full_proj.T, preferred_element_type=jnp.float32)
    grad_two, grad_gain_three = back_three(grad_final)
    grad_branch = grad_two.astype(jnp.bfloat16)
    grad_back = jnp.einsum("tf,td->fd", active_low, grad_branch, preferred_element_type=jnp.float32)
    grad_active = jnp.dot(grad_branch, full_back.T, preferred_element_type=jnp.float32)
    grad_upward = back_gelu(grad_active)[0].astype(jnp.bfloat16)
    grad_in = jnp.einsum("td,tf->df", hidden_two, grad_upward, preferred_element_type=jnp.float32)
    grad_hidden_two = jnp.dot(grad_upward, full_in.T, preferred_element_type=jnp.float32)
    grad_norm_two, grad_gain_two = back_two(grad_hidden_two)
    grad_one = grad_two + grad_norm_two
    grad_attn = grad_one.astype(jnp.bfloat16)
    grad_out = jnp.einsum("td,te->de", mixed_rows, grad_attn, preferred_element_type=jnp.float32)
    grad_mixed = jnp.dot(grad_attn, full_out.T, preferred_element_type=jnp.float32).astype(
        jnp.bfloat16
    )
    grad_heads = lax.all_to_all(grad_mixed[None], "head", split_axis=2, concat_axis=0, tiled=True)
    grad_view = grad_heads.reshape(head_shape)
    row_delta = jnp.einsum("sihe,sihe->shi", grad_view.astype(jnp.float32), attended)

    def query_terms(first_key, length):
        keys_tile, values_tile, key_pos, key_seg = key_tile(first_key, length)
        logit_scores, allowed, onehot = tile_scores(
            query_view, keys_tile, query_pos, key_pos, query_seg, key_seg, head_table
        )
        softmax = tile_probs(logit_scores, allowed, logsum)
        grad_probs = jnp.einsum(
            "sihe,sjhe->shij", grad_view, values_tile, preferred_element_type=jnp.float32
        )
        grad_scores = (softmax * (grad_probs - row_delta[..., None])).astype(jnp.bfloat16)
        table_term = jnp.einsum(
            "shij,bij->hb",
            grad_scores,
            onehot.astype(jnp.bfloat16),
            preferred_element_type=jnp.float32,
        )
        query_term = jnp.einsum(
            "shij,sjhe->sihe", grad_scores, keys_tile, preferred_element_type=jnp.float32
        )
        return (softmax, grad_scores, table_term, query_term)

    start_grads = (
        jnp.zeros(head_shape, jnp.float32),
        jnp.zeros((local_heads, bucket_total), jnp.float32),
    )

    def query_step(carried, block_index):
        softmax, grad_scores, table_term, query_term = query_terms(
            block_index * key_block, key_block
        )
        return ((carried[0] + query_term, carried[1] + table_term), None)

    (grad_query_acc, grad_table_acc), unused = lax.scan(
        query_step, start_grads, jnp.arange(key_count)
    )
    query_all, grad_all = (
        lax.all_gather(query_heads, "blk", axis=1, tiled=True),
        lax.all_gather(grad_heads, "blk", axis=1, tiled=True),
    )
    logsum_all, delta_all = (
        lax.all_gather(logsum, "blk", axis=2, tiled=True),
        lax.all_gather(row_delta, "blk", axis=2, tiled=True),
    )
    key_view = key_heads.reshape(head_shape)
    value_view = value_heads.reshape(head_shape)

    def owner_step(carried, block_index):
        first_query = block_index * key_block
        queries_tile = lax.dynamic_slice_in_dim(query_all, first_query, key_block, 1).reshape(
            groups, key_block, local_heads, head_size
        )
        grads_tile = lax.dynamic_slice_in_dim(grad_all, first_query, key_block, 1).reshape(
            groups, key_block, local_heads, head_size
        )
        tile_pos = first_query + jnp.arange(key_block, dtype=jnp.int32)
        tile_seg = lax.dynamic_slice_in_dim(document, first_query, key_block, 1)
        logit_scores, allowed, onehot = tile_scores(
            queries_tile, key_view, tile_pos, query_pos, tile_seg, query_seg, head_table
        )
        softmax = tile_probs(
            logit_scores, allowed, lax.dynamic_slice_in_dim(logsum_all, first_query, key_block, 2)
        )
        grad_probs = jnp.einsum(
            "sihe,sjhe->shij", grads_tile, value_view, preferred_element_type=jnp.float32
        )
        tile_delta = lax.dynamic_slice_in_dim(delta_all, first_query, key_block, 2)
        grad_scores = (softmax * (grad_probs - tile_delta[..., None])).astype(jnp.bfloat16)
        grad_keys = jnp.einsum(
            "shij,sihe->sjhe", grad_scores, queries_tile, preferred_element_type=jnp.float32
        )
        grad_values = jnp.einsum(
            "shij,sihe->sjhe",
            softmax.astype(jnp.bfloat16),
            grads_tile,
            preferred_element_type=jnp.float32,
        )
        return ((carried[0] + grad_keys, carried[1] + grad_values), None)

    start_owner = (jnp.zeros(head_shape, jnp.float32), jnp.zeros(head_shape, jnp.float32))
    (grad_key_acc, grad_value_acc), unused = lax.scan(
        owner_step, start_owner, jnp.arange(key_count)
    )
    grad_key_low = grad_key_acc.astype(jnp.bfloat16).reshape(groups, tokens, lane_width)
    grad_value_low = grad_value_acc.astype(jnp.bfloat16).reshape(groups, tokens, lane_width)
    grad_query_low = grad_query_acc.astype(jnp.bfloat16).reshape(groups, tokens, lane_width)
    back_query, back_key, back_value = (
        lax.all_to_all(grad_query_low, "head", split_axis=0, concat_axis=2, tiled=True),
        lax.all_to_all(grad_key_low, "head", split_axis=0, concat_axis=2, tiled=True),
        lax.all_to_all(grad_value_low, "head", split_axis=0, concat_axis=2, tiled=True),
    )
    back_query = back_query[0]
    back_key = back_key[0]
    back_value = back_value[0]
    grad_query = jnp.einsum("td,te->de", hidden_one, back_query, preferred_element_type=jnp.float32)
    grad_key = jnp.einsum("td,te->de", hidden_one, back_key, preferred_element_type=jnp.float32)
    grad_value = jnp.einsum("td,te->de", hidden_one, back_value, preferred_element_type=jnp.float32)
    grad_hidden_one = jnp.dot(back_query, full_query.T, preferred_element_type=jnp.float32)
    grad_hidden_one = grad_hidden_one + jnp.dot(
        back_key, full_key.T, preferred_element_type=jnp.float32
    )
    grad_hidden_one = grad_hidden_one + jnp.dot(
        back_value, full_value.T, preferred_element_type=jnp.float32
    )
    grad_norm_one, grad_gain_one = back_one(grad_hidden_one)
    input_gradient_rows = (grad_one + grad_norm_one)[None]
    sharded = (
        lax.psum_scatter(grad_query, ("head", "blk"), scatter_dimension=0, tiled=True),
        lax.psum_scatter(grad_key, ("head", "blk"), scatter_dimension=0, tiled=True),
        lax.psum_scatter(grad_value, ("head", "blk"), scatter_dimension=0, tiled=True),
        lax.psum_scatter(grad_out, ("head", "blk"), scatter_dimension=0, tiled=True),
        lax.psum_scatter(grad_in, ("head", "blk"), scatter_dimension=0, tiled=True),
        lax.psum_scatter(grad_back, ("head", "blk"), scatter_dimension=0, tiled=True),
        lax.psum_scatter(grad_proj, ("head", "blk"), scatter_dimension=0, tiled=True),
        lax.psum_scatter(grad_gain_one, ("head", "blk"), scatter_dimension=0, tiled=True),
        lax.psum_scatter(grad_gain_two, ("head", "blk"), scatter_dimension=0, tiled=True),
        lax.psum_scatter(grad_gain_three, ("head", "blk"), scatter_dimension=0, tiled=True),
    )
    table_rows = lax.dynamic_update_slice_in_dim(
        jnp.zeros((head_count, bucket_total), jnp.float32),
        grad_table_acc,
        lax.axis_index("head") * local_heads,
        0,
    )
    grad_table = lax.psum(table_rows.T, ("head", "blk"))
    return (
        states[None],
        input_gradient_rows,
        sharded[0],
        sharded[1],
        sharded[2],
        sharded[3],
        sharded[4],
        sharded[5],
        sharded[6],
        sharded[7],
        sharded[8],
        sharded[9],
        grad_table,
    )


def solution(mesh):
    in_specs = (
        P("head", "blk", None),
        P("head", "blk"),
        P(("head", "blk"), None),
        P(("head", "blk"), None),
        P(("head", "blk"), None),
        P(("head", "blk"), None),
        P(("head", "blk"), None),
        P(("head", "blk"), None),
        P(("head", "blk"), None),
        P(("head", "blk")),
        P(("head", "blk")),
        P(("head", "blk")),
        P(),
        P("head", "blk", None),
    )
    out_specs = (
        P("head", "blk", None),
        P("head", "blk", None),
        P(("head", "blk"), None),
        P(("head", "blk"), None),
        P(("head", "blk"), None),
        P(("head", "blk"), None),
        P(("head", "blk"), None),
        P(("head", "blk"), None),
        P(("head", "blk"), None),
        P(("head", "blk")),
        P(("head", "blk")),
        P(("head", "blk")),
        P(),
    )
    return jax.shard_map(body, mesh=mesh, in_specs=in_specs, out_specs=out_specs, check_vma=False)
```

profile of v0, /device:TPU:0, one launch (start us, length us, event | category | flops | bytes accessed | tf_op | source)
XLA Modules:
  0.0 1356.5 jit_solution(1026312289091275732)
XLA Ops:
  12.0 42.1 %all-reduce.8 = (bf16[768]{0:T(1024)(128)(2,1)S(1)}, bf16[768]{0:T(1024)(128)(2,1)S(1)}, bf16[768]{0:T(1024)(128)(2,1)S(1)}) all-reduce(bf16[768]{0:T(1024)(128)(2,1)S(1)} %dynamic-update-slice, bf16[768]{0:T(1024)(128)(2,1)S(1)} %dynamic-update-slice.1, ...), channel_id=1, replica_groups=mesh['head'=4,'blk'=8] {'head','blk'}, use_global_device_ids=true, to_apply=%add | all-reduce | flops 2304 | bytes 9216
  55.2 12.7 all-gather.18.cloned.1.call-done
  72.4 7.8 all_to_all.132
  81.2 42.7 %all-gather.16.cloned.1.call-done = bf16[768,768]{1,0:T(8,128)(2,1)} async-done(((bf16[24,768]{1,0:T(8,128)(2,1)}), bf16[768,768]{1,0:T(8,128)(2,1)}) %all-gather.16.cloned.1.call-update) | async-done | bytes 1179664 | tf_op jit(solution)/shard_map/all_gather | solution.py:71
  127.8 7.8 all_to_all.133
  138.6 65.1 %all-gather.4 = s32[32,1,128]{2,1,0:T(1,128)S(1)} all-gather(s32[1,1,128]{2,1,0:T(1,128)S(1)} %bitcast.388), channel_id=1, replica_groups=mesh['head'=4,'blk'=8] {'head','blk'}, dimensions={0}, use_global_device_ids=true | all-gather | bytes 16896 | tf_op jit(solution)/shard_map/all_gather | solution.py:65
  209.5 3.9 all-to-all-start.2
  214.2 4.5 all-to-all-done.2
  219.6 6.4 all-gather.30.cloned.1.call-done
  226.0 21.0 %while.50 = (s32[]{:T(128)}, f32[4,3,128]{2,1,0:T(4,128)S(1)}, f32[4,3,128]{2,1,0:T(4,128)S(1)}, s32[4,128]{1,0:T(4,128)S(1)}, s32[2]{0:T(128)S(1)}, /*index=5*/...) while((s32[]{:T(128)}, f32[4,3,128]{2,1,0:T(4,128)S(1)}, ...), condition=%wide.region_4.5_spmd.clone, body=%wide.region_1.4_spmd.clone.sunk | while | flops 186720384 | bytes 23639704 | solution.py:144
  227.6 2.6 fusion.243
  234.5 2.0 select_reduce_fusion.2
  238.1 2.6 fusion.243
  245.0 1.9 select_reduce_fusion.2
  247.0 25.0 %all-gather.28.cloned.1.call-done = bf16[4,1,1024,192]{2,3,0,1:T(8,128)(2,1)} async-done(((bf16[4,1,128,192]{2,3,0,1:T(8,128)(2,1)}), bf16[4,1,1024,192]{2,3,0,1:T(8,128)(2,1)}) %all-gather.28.cloned.1.call-update) | async-done | bytes 1572880 | tf_op jit(solution)/shard_map/all_gather | solution.py:111
  272.0 21.0 %while.51 = (s32[]{:T(128)}, f32[4,128,3,64]{1,3,2,0:T(8,128)}, s32[2]{0:T(128)S(1)}, bf16[4,1024,192]{1,2,0:T(8,128)(2,1)}, s32[4,128]{1,0:T(4,128)S(1)}, /*ind...) while((s32[]{:T(128)}, f32[4,128,3,64]{1,3,2,0:T(8,128)}, ...), condition=%wide.region_6.7_spmd.clone, body=%wide.region_5.6_spmd.clone.sunk | while | flops 284426880 | bytes 10720901 | solution.py:163
  273.3 2.4 constant_dynamic-slice_fusion.25
  276.0 2.6 fusion.251
  279.4 3.1 fusion.252
  283.7 2.4 constant_dynamic-slice_fusion.25
  286.5 2.6 fusion.251
  289.9 3.2 fusion.252
  294.8 3.4 all-to-all-start.3
  298.2 67.5 %all_gather.70 = bf16[768,128]{1,0:T(8,128)(2,1)S(1)} all-gather(bf16[24,128]{1,0:T(8,128)(2,1)S(1)} %copy-done.39), channel_id=1, replica_groups=mesh['head'=4,'blk'=8] {'head','blk'}, dimensions={0}, use_global_device_ids=true | all-gather | bytes 202752 | tf_op jit(solution)/shard_map/all_gather | solution.py:75
  367.7 25.3 %all-gather.24.cloned.1.call-done = bf16[768,3072]{1,0:T(8,128)(2,1)} async-done(((bf16[24,3072]{1,0:T(8,128)(2,1)}), bf16[768,3072]{1,0:T(8,128)(2,1)}) %all-gather.24.cloned.1.call-update) | async-done | bytes 4718608 | tf_op jit(solution)/shard_map/all_gather | solution.py:73
  393.0 3.2 fusion.144
  396.2 62.2 %all-gather.26.cloned.1.call-done = bf16[3072,768]{1,0:T(8,128)(2,1)} async-done(((bf16[96,768]{1,0:T(8,128)(2,1)}), bf16[3072,768]{1,0:T(8,128)(2,1)}) %all-gather.26.cloned.1.call-update) | async-done | bytes 4718608 | tf_op jit(solution)/shard_map/all_gather | solution.py:74
  458.4 3.6 multiply_reduce_fusion.4
  469.7 7.8 all_to_all.134
  483.3 39.2 %while.52 = (s32[]{:T(128)}, f32[4,128,3,64]{1,3,2,0:T(8,128)}, f32[3,32]{1,0:T(4,128)S(1)}, s32[2]{0:T(128)S(1)}, bf16[4,1024,192]{1,2,0:T(8,128)(2,1)S(1)}, /*...) while((s32[]{:T(128)}, f32[4,128,3,64]{1,3,2,0:T(8,128)}, ...), condition=%wide.region_13.14_spmd.clone, body=%wide.region_11.13_spmd.clone.sunk | while | flops 406913856 | bytes 29012464 | solution.py:245
  484.5 2.2 constant_dynamic-slice_fusion.27
  487.8 3.6 fusion.262
  494.1 4.5 convert_reduce_fusion.2
  498.6 2.7 fusion.264
  504.1 2.2 constant_dynamic-slice_fusion.27
  507.3 3.6 fusion.262
  513.6 4.5 convert_reduce_fusion.2
  518.1 2.7 fusion.264
  524.2 3.4 all-to-all-start.5
  527.7 26.5 %all_gather.72 = f32[4,3,1024]{2,1,0:T(4,128)S(1)} all-gather(f32[4,3,128]{2,1,0:T(4,128)S(1)} %get-tuple-element.1204), channel_id=1, replica_groups=mesh['head'=4,'blk'=8] {'blk'}, dimensions={2}, use_global_device_ids=true | all-gather | bytes 55296 | tf_op jit(solution)/shard_map/all_gather | solution.py:253
  554.1 27.0 %all_gather.74 = f32[4,3,1024]{2,1,0:T(4,128)} all-gather(f32[4,3,128]{2,1,0:T(4,128)S(1)} %get-tuple-element.1202), channel_id=1, replica_groups=mesh['head'=4,'blk'=8] {'blk'}, dimensions={2}, use_global_device_ids=true | all-gather | bytes 55296 | tf_op jit(solution)/shard_map/all_gather | solution.py:254
  581.2 3.0 fusion.149
  584.6 35.5 %while.53 = (s32[]{:T(128)}, f32[4,128,3,64]{1,3,2,0:T(8,128)}, f32[4,128,3,64]{1,3,2,0:T(8,128)}, s32[2]{0:T(128)S(1)}, bf16[4,1024,192]{1,2,0:T(8,128)(2,1)}, ...) while((s32[]{:T(128)}, f32[4,128,3,64]{1,3,2,0:T(8,128)}, ...), condition=%wide.region_15.16_spmd.clone, body=%wide.region_14.15_spmd.clone.sunk | while | flops 490668672 | bytes 27270872 | solution.py:292
  585.9 2.4 constant_dynamic-slice_fusion.29
  589.6 2.6 fusion.276
  594.2 4.8 fusion.277
  599.0 3.3 fusion.278
  603.5 2.4 constant_dynamic-slice_fusion.29
  607.2 2.6 fusion.276
  611.8 4.9 fusion.277
  616.7 3.4 fusion.278
  621.2 8.2 all_to_all.135
  629.4 2.1 fusion.147
  631.5 7.8 all_to_all.136
  639.3 2.0 fusion.145
  641.4 5.1 fusion.143
  648.0 5.2 fusion.130
  659.2 38.6 %all-reduce.7 = (f32[768]{0:T(1024)S(1)}, f32[768]{0:T(1024)S(1)}, f32[768]{0:T(1024)S(1)}, f32[32,12]{0,1:T(8,128)}) all-reduce(f32[768]{0:T(1024)S(1)} %get-tuple-element.487, f32[768]{0:T(1024)S(1)} %get-tuple-element.485, f32[768]{0:T(1024)S(1)} %get-tuple-element.483, ...), channel_id=13, replica_groups=mesh['head'=4,'blk'=8] {'head','blk'}, use_global_device_ids=true, to_apply=%region_25.26.clone | all-reduce | flops 2688 | bytes 21504
  700.5 53.8 %reduce-scatter.16.cloned.1.call-done = f32[24,768]{1,0:T(8,128)} async-done(((f32[768,768]{1,0:T(8,128)}), f32[24,768]{1,0:T(8,128)}) %reduce-scatter.16.cloned.1.call-update) | async-done | bytes 73744 | tf_op jit(solution)/shard_map/reduce_scatter | solution.py:322
  754.3 103.9 %reduce-scatter.10.cloned.1.call-done = f32[24,768]{1,0:T(8,128)} async-done(((f32[768,768]{1,0:T(8,128)}), f32[24,768]{1,0:T(8,128)}) %reduce-scatter.10.cloned.1.call-update) | async-done | bytes 73744 | tf_op jit(solution)/shard_map/reduce_scatter | solution.py:319
  858.2 104.6 %reduce-scatter.12.cloned.1.call-done = f32[24,768]{1,0:T(8,128)} async-done(((f32[768,768]{1,0:T(8,128)}), f32[24,768]{1,0:T(8,128)}) %reduce-scatter.12.cloned.1.call-update) | async-done | bytes 73744 | tf_op jit(solution)/shard_map/reduce_scatter | solution.py:320
  962.8 103.7 %reduce-scatter.14.cloned.1.call-done = f32[24,768]{1,0:T(8,128)} async-done(((f32[768,768]{1,0:T(8,128)}), f32[24,768]{1,0:T(8,128)}) %reduce-scatter.14.cloned.1.call-update) | async-done | bytes 73744 | tf_op jit(solution)/shard_map/reduce_scatter | solution.py:321
  1066.5 141.9 %reduce-scatter.18.cloned.1.call-done = f32[24,3072]{1,0:T(8,128)} async-done(((f32[768,3072]{1,0:T(8,128)}), f32[24,3072]{1,0:T(8,128)}) %reduce-scatter.18.cloned.1.call-update) | async-done | bytes 294928 | tf_op jit(solution)/shard_map/reduce_scatter | solution.py:323
  1208.4 141.1 %reduce-scatter.20.cloned.1.call-done = f32[96,768]{1,0:T(8,128)} async-done(((f32[3072,768]{1,0:T(8,128)}), f32[96,768]{1,0:T(8,128)}) %reduce-scatter.20.cloned.1.call-update) | async-done | bytes 294928 | tf_op jit(solution)/shard_map/reduce_scatter | solution.py:324
  (315 shorter events, 88.8 us)
Async XLA Ops:
  7.2 454.9 %copy-start = (bf16[1,128,128]{2,1,0:T(8,128)(2,1)S(1)}, bf16[1,128,128]{2,1,0:T(8,128)(2,1)}, u32[]{:S(2)}) copy-start(bf16[1,128,128]{2,1,0:T(8,128)(2,1)} %param.35) | copy-start | bytes 98308
  7.2 60.7 %all-gather.18.cloned.1.call-start = ((), (), s32[]{:S(2)}) async-start(), calls=%async_computation.16 | async-start | bytes 1216512 | tf_op jit(solution)/shard_map/all_gather | solution.py:70
  7.9 115.9 %all-gather.16.cloned.1.call-start = ((), (), s32[]{:S(2)}) async-start(), calls=%async_computation.15 | async-start | bytes 1216512 | tf_op jit(solution)/shard_map/all_gather | solution.py:71
  8.7 196.2 %all-gather.20.cloned.1.call-start = ((), (), s32[]{:S(2)}) async-start(), calls=%async_computation.17 | async-start | bytes 1216512 | tf_op jit(solution)/shard_map/all_gather | solution.py:69
  9.4 216.6 %all-gather.30.cloned.1.call-start = ((), (), s32[]{:S(2)}) async-start(), calls=%async_computation.28 | async-start | bytes 1769472 | tf_op jit(solution)/shard_map/all_gather | solution.py:110
  55.1 26.0 %copy-start.42 = (f32[128]{0:T(128)}, f32[128]{0:T(128)S(1)}, u32[]{:S(2)}) copy-start(f32[128]{0:T(128)S(1)} %fusion.118) | copy-start | bytes 1540
  55.1 68.7 %copy-start.8 = (bf16[1,128,768]{2,1,0:T(8,128)(2,1)S(1)}, bf16[1,128,768]{2,1,0:T(8,128)(2,1)}, u32[]{:S(2)}) copy-start(bf16[1,128,768]{2,1,0:T(8,128)(2,1)} %param.22) | copy-start | bytes 589828
  81.1 190.9 %all-gather.28.cloned.1.call-start = ((), (), s32[]{:S(2)}) async-start(), calls=%async_computation.27 | async-start | bytes 1769472 | tf_op jit(solution)/shard_map/all_gather | solution.py:111
  125.5 13.1 copy-start.44
  136.5 229.5 %all-gather.22.cloned.1.call-start = ((), (), s32[]{:S(2)}) async-start(), calls=%async_computation.18 | async-start | bytes 1216512 | tf_op jit(solution)/shard_map/all_gather | solution.py:72
  137.1 255.9 %all-gather.24.cloned.1.call-start = ((), (), s32[]{:S(2)}) async-start(), calls=%async_computation.19 | async-start | bytes 4866048 | tf_op jit(solution)/shard_map/all_gather | solution.py:73
  137.8 320.6 %all-gather.26.cloned.1.call-start = ((), (), s32[]{:S(2)}) async-start(), calls=%async_computation.20 | async-start | bytes 4866048 | tf_op jit(solution)/shard_map/all_gather | solution.py:74
  209.5 9.2 all-to-all-start.2
  227.6 4.2 copy-start.3
  238.1 4.2 copy-start.3
  272.0 26.2 %copy-start.39 = (bf16[24,128]{1,0:T(8,128)(2,1)S(1)}, bf16[24,128]{1,0:T(8,128)(2,1)}, u32[]{:S(2)}) copy-start(bf16[24,128]{1,0:T(8,128)(2,1)} %param.30) | copy-start | bytes 18436
  272.0 94.0 %copy-start.9 = (bf16[1,128,768]{2,1,0:T(8,128)(2,1)S(1)}, bf16[1,128,768]{2,1,0:T(8,128)(2,1)}, u32[]{:S(2)}) copy-start(bf16[1,128,768]{2,1,0:T(8,128)(2,1)} %param.22) | copy-start | bytes 589828
  276.0 3.3 copy-start.6
  286.5 3.3 copy-start.6
  294.8 71.2 %all-to-all-start.3 = ((bf16[4,128,192]{1,2,0:T(8,128)(2,1)}), bf16[4,128,192]{1,2,0:T(8,128)(2,1)S(1)}, u32[]{:S(2)}, u32[]{:S(2)}) async-start(bf16[4,128,192]{1,2,0:T(8,128)(2,1)} %bitcast.15), calls=%async_computation.3 | async-start | bytes 393216 | tf_op jit(solution)/shard_map/all_to_all | solution.py:167
  298.1 286.4 %all-gather.32.cloned.1.call-start = ((), (), s32[]{:S(2)}) async-start(), calls=%async_computation.29 | async-start | bytes 1769472 | tf_op jit(solution)/shard_map/all_gather | solution.py:249
  365.7 96.4 %copy-start.34 = (bf16[768,128]{1,0:T(8,128)(2,1)}, bf16[768,128]{1,0:T(8,128)(2,1)S(1)}, u32[]{:S(2)}) copy-start(bf16[768,128]{1,0:T(8,128)(2,1)S(1)} %all_gather.70) | copy-start | bytes 589828
  365.7 218.8 %all-gather.34.cloned.1.call-start = ((), (), s32[]{:S(2)}) async-start(), calls=%async_computation.30 | async-start | bytes 1769472 | tf_op jit(solution)/shard_map/all_gather | solution.py:250
  367.7 99.0 %copy-start.13 = (f32[128,768]{1,0:T(8,128)}, f32[128,768]{1,0:T(8,128)S(1)}, u32[]{:S(2)}) copy-start(f32[128,768]{1,0:T(8,128)S(1)} %get-tuple-element.607) | copy-start | bytes 1179652
  396.2 66.4 %copy-start.16 = (f32[128,3072]{1,0:T(8,128)}, f32[128,3072]{1,0:T(8,128)S(1)}, u32[]{:S(2)}) copy-start(f32[128,3072]{1,0:T(8,128)S(1)} %fusion.144) | copy-start | bytes 4718596
  458.4 4.2 copy-start.45
  462.0 16.4 %copy-start.20 = (f32[128,768]{1,0:T(8,128)}, f32[128,768]{1,0:T(8,128)S(1)}, u32[]{:S(2)}) copy-start(f32[128,768]{1,0:T(8,128)S(1)} %get-tuple-element.609) | copy-start | bytes 1179652
  462.4 2.3 slice-start
  462.6 4.1 copy-start.27
  462.6 2.3 slice-start.1
  464.9 1.8 copy-start.29
  464.9 2.0 copy-start.26
  466.9 13.0 copy-start.22
  478.4 222.1 %reduce-scatter.22.cloned.1.call-start = ((), (), s32[]{:S(2)}) async-start(), calls=%async_computation.31 | async-start | bytes 405504
  479.6 274.7 %reduce-scatter.16.cloned.1.call-start = ((), (), s32[]{:S(2)}) async-start(), calls=%async_computation.24 | async-start | bytes 2433024 | tf_op jit(solution)/shard_map/reduce_scatter | solution.py:322
  479.9 1.9 copy-start.36
  481.8 1.5 copy-start.4
  481.8 1.5 copy-start.7
  498.6 2.7 copy-start.12
  498.6 3.1 copy-start.19
  518.1 2.7 copy-start.12
  518.1 3.1 copy-start.19
  522.5 61.7 %copy-start.40 = (f32[3,32]{1,0:T(4,128)}, f32[3,32]{1,0:T(4,128)S(1)}, u32[]{:S(2)}) copy-start(f32[3,32]{1,0:T(4,128)S(1)} %get-tuple-element.275) | copy-start | bytes 1156
  524.2 57.0 %all-to-all-start.5 = ((bf16[4,128,192]{1,2,0:T(8,128)(2,1)}), bf16[4,128,192]{1,2,0:T(8,128)(2,1)S(1)}, u32[]{:S(2)}, u32[]{:S(2)}) async-start(bf16[4,128,192]{1,2,0:T(8,128)(2,1)} %bitcast.26), calls=%async_computation.5 | async-start | bytes 393216 | tf_op jit(solution)/shard_map/all_to_all | solution.py:299
  527.6 330.6 %reduce-scatter.10.cloned.1.call-start = ((), (), s32[]{:S(2)}) async-start(), calls=%async_computation.21 | async-start | bytes 2433024 | tf_op jit(solution)/shard_map/reduce_scatter | solution.py:319
  581.2 3.0 copy-start.31
  584.2 378.6 %reduce-scatter.12.cloned.1.call-start = ((), (), s32[]{:S(2)}) async-start(), calls=%async_computation.22 | async-start | bytes 2433024 | tf_op jit(solution)/shard_map/reduce_scatter | solution.py:320
  584.6 44.8 %copy-start.10 = (bf16[1,128,768]{2,1,0:T(8,128)(2,1)S(1)}, bf16[1,128,768]{2,1,0:T(8,128)(2,1)}, u32[]{:S(2)}) copy-start(bf16[1,128,768]{2,1,0:T(8,128)(2,1)} %param.22) | copy-start | bytes 589828
  585.8 2.4 copy-start.15
  603.5 2.4 copy-start.15
  629.4 2.1 copy-start.38
  631.4 435.1 %reduce-scatter.14.cloned.1.call-start = ((), (), s32[]{:S(2)}) async-start(), calls=%async_computation.23 | async-start | bytes 2433024 | tf_op jit(solution)/shard_map/reduce_scatter | solution.py:321
  639.3 2.0 copy-start.33
  639.3 2.1 copy-start.14
  639.3 2.1 copy-start.30
  641.3 567.1 %reduce-scatter.18.cloned.1.call-start = ((), (), s32[]{:S(2)}) async-start(), calls=%async_computation.25 | async-start | bytes 9732096 | tf_op jit(solution)/shard_map/reduce_scatter | solution.py:323
  646.5 702.9 %reduce-scatter.20.cloned.1.call-start = ((), (), s32[]{:S(2)}) async-start(), calls=%async_computation.26 | async-start | bytes 9732096 | tf_op jit(solution)/shard_map/reduce_scatter | solution.py:324
  653.2 1.9 copy-start.41
  653.2 2.0 copy-start.32
  653.2 3.9 copy-start.24
  655.1 2.6 copy-start.25
  657.1 42.5 %copy-start.43 = (f32[128]{0:T(128)S(1)}, f32[128]{0:T(128)}, u32[]{:S(2)}) copy-start(f32[128]{0:T(128)} %copy-done.42) | copy-start | bytes 1540
  657.1 42.5 %copy-start.23 = (f32[128,768]{1,0:T(8,128)S(1)}, f32[128,768]{1,0:T(8,128)}, u32[]{:S(2)}) copy-start(f32[128,768]{1,0:T(8,128)} %copy-done.22) | copy-start | bytes 1179652
  657.1 692.3 %copy-start.1 = (bf16[1,128,128]{2,1,0:T(8,128)(2,1)S(1)}, bf16[1,128,128]{2,1,0:T(8,128)(2,1)}, u32[]{:S(2)}) copy-start(bf16[1,128,128]{2,1,0:T(8,128)(2,1)} %param.35) | copy-start | bytes 98308
  (14 other events, 14.5 us)
Sparse Core Ops, SparseCore 0:
  10.9 56.8 all-gather.17
  70.8 53.0 all-gather.15
  126.8 52.9 all-gather.19
  181.7 44.2 all-gather.29
  228.5 43.4 all-gather.27
  274.8 52.6 all-gather.21
  330.4 62.5 all-gather.23
  395.9 62.4 all-gather.25
  460.5 44.1 all-gather.31
  506.5 44.1 all-gather.33
  556.2 93.2 reduce-scatter.21
  656.1 98.1 reduce-scatter.15
  760.1 98.0 reduce-scatter.9
  864.7 98.0 reduce-scatter.11
  968.5 97.9 reduce-scatter.13
  1073.8 134.4 reduce-scatter.17
  1214.7 134.6 reduce-scatter.19
where the time goes:
time: 1360 us
  waiting for transfers between devices  832 us (61%)
  blocking collectives  306 us (22%)
  matrix products  112 us (8%)
  local copies, waits for them, and re-layouts  45.9 us (3%)
  other arithmetic  27.4 us (2%)
  between operations  15.3 us (1%)
    reduce_scatter x1, waiting for transfers between devices, body(): lax.psum_scatter(grad_in, ('head', 'blk'), scatter_dimension=0, tiled=True)  142 us
    reduce_scatter x1, waiting for transfers between devices, body(): lax.psum_scatter(grad_back, ('head', 'blk'), scatter_dimension=0, tiled=T...  141 us
    reduce_scatter x1, waiting for transfers between devices, body(): lax.psum_scatter(grad_key, ('head', 'blk'), scatter_dimension=0, tiled=True)  105 us
    reduce_scatter x1, waiting for transfers between devices, body(): lax.psum_scatter(grad_query, ('head', 'blk'), scatter_dimension=0, tiled=...  104 us
    reduce_scatter x1, waiting for transfers between devices, body(): lax.psum_scatter(grad_value, ('head', 'blk'), scatter_dimension=0, tiled=...  104 us
    unnamed x2, blocking collectives  80.7 us
    all_gather x1, blocking collectives, body(): lax.all_gather(w_proj, ('head', 'blk'), axis=0, tiled=True)  67.5 us
    all_gather x1, blocking collectives, body(): lax.all_gather(segments, ('head', 'blk'), axis=0, tiled=True)  65.1 us
  transfers between devices with their start and end apart: 20, of which 13 were waited for; matrix products, arithmetic and copies ran while one was open for 13% of the time, Pallas kernels for 0%

commit v1 on v0

v1 whole, which is shorter than its diff:
```python
import functools
import math

import jax
import jax.numpy as jnp
import numpy as np
from jax import lax
from jax.experimental import pallas as pl
from jax.experimental.pallas import tpu as pltpu
from jax.sharding import PartitionSpec as P

BORDERS = (12, 16, 23, 32, 46, 64, 91)
MASKED = -1e30
EPS = 1e-6
TILE = 128
WIN = 512
BF16 = jnp.bfloat16
F32 = jnp.float32
AXES = ("head", "blk")
VMEM_LIMIT = 56 * 1024 * 1024


def bucket_np(offset):
    distance = np.abs(offset)
    beyond = 8 + sum((distance >= border).astype(np.int64) for border in BORDERS)
    within = np.minimum(np.where(distance < 8, distance, beyond), 15)
    return within + 16 * (offset > 0)


def window_offsets():
    k = np.arange(WIN)
    return np.where(k < WIN - TILE, k - TILE, k - WIN - TILE)


def dot(a, b):
    return jnp.dot(a, b, preferred_element_type=F32)


def dot_nt(a, b):
    return lax.dot_general(a, b, (((1,), (1,)), ((), ())), preferred_element_type=F32)


def dot_tn(a, b):
    return lax.dot_general(a, b, (((0,), (0,)), ((), ())), preferred_element_type=F32)


class Links:
    def __init__(self):
        self.blocks = lax.axis_size("blk")
        self.total = lax.axis_size("head") * self.blocks
        self.me = lax.axis_index("head") * self.blocks + lax.axis_index("blk")
        self.bits = [1 << k for k in range(int(math.log2(self.total)))]
        self.blk_bits = [bit for bit in self.bits if bit < self.blocks]
        self.head_bits = [bit for bit in self.bits if bit >= self.blocks]

    def swap(self, value, bit):
        return lax.ppermute(value, AXES, [(i, i ^ bit) for i in range(self.total)])

    def mine(self, bit):
        return (self.me & bit) != 0


def gather_rows(links, shard, order, all_bits):
    high_first = sorted(all_bits, reverse=True)
    value = shard.reshape((1,) * len(high_first) + shard.shape)
    for bit in order:
        axis = high_first.index(bit)
        other = links.swap(value, bit)
        value = jnp.where(
            links.mine(bit),
            jnp.concatenate([other, value], axis),
            jnp.concatenate([value, other], axis),
        )
    return value.reshape((-1,) + shard.shape[1:])


def scatter_sum(links, whole, order, all_bits):
    high_first = sorted(all_bits, reverse=True)
    count = len(high_first)
    rows = whole.shape[0] >> count
    value = whole.reshape((2,) * count + (rows,) + whole.shape[1:])
    for bit in order:
        axis = high_first.index(bit)
        side = links.mine(bit).astype(jnp.int32)
        sent = lax.dynamic_slice_in_dim(value, 1 - side, 1, axis).astype(BF16)
        kept = lax.dynamic_slice_in_dim(value, side, 1, axis)
        value = kept.astype(F32) + links.swap(sent, bit).astype(F32)
    return value.reshape((rows,) + whole.shape[1:])


def bias_tiles(bias_ref, tiles_ref, head_row, side):
    row = bias_ref[pl.ds(head_row, 1), :]
    near = pltpu.roll(jnp.broadcast_to(row[:, :WIN], (TILE, WIN)), 0, 1, stride=1, stride_axis=0)
    rows = pl.ds(side * TILE, TILE)
    tiles_ref[0, rows, :] = jnp.broadcast_to(row[:, WIN : WIN + 1], (TILE, TILE))
    for t in range(3):
        tiles_ref[1 + t, rows, :] = near[:, t * TILE : (t + 1) * TILE]
    tiles_ref[4, rows, :] = jnp.broadcast_to(row[:, WIN + 1 : WIN + 2], (TILE, TILE))


def stacked(pair):
    lane = lax.broadcasted_iota(jnp.int32, pair.shape, 1)
    zero = jnp.zeros_like(pair)
    half = pair.shape[1] // 2
    return jnp.concatenate([jnp.where(lane < half, pair, zero), jnp.where(lane < half, zero, pair)], 0)


def unstacked(both):
    rows = both.shape[0] // 2
    lane = lax.broadcasted_iota(jnp.int32, (rows, both.shape[1]), 1)
    return jnp.where(lane < both.shape[1] // 2, both[:rows], both[rows:])


def tile_kind(key_tile, own_tile):
    return jnp.clip(key_tile - own_tile, -2, 2) + 2


def scores_into(chunk, chunk_tiles, own, q2, k_ref, qseg, kseg_ref, tiles_ref, s_ref):
    base = chunk * chunk_tiles * TILE
    raw = dot_nt(q2, k_ref[pl.ds(base, chunk_tiles * TILE), :])
    parts = []
    for t in range(chunk_tiles):
        at = base + t * TILE
        near = tiles_ref[tile_kind(chunk * chunk_tiles + t, own)]
        allowed = qseg == kseg_ref[:, pl.ds(at, TILE)]
        tile = jnp.where(allowed, raw[:, t * TILE : (t + 1) * TILE] + near, MASKED)
        s_ref[:, pl.ds(at, TILE)] = tile
        parts.append(tile)
    return parts


def attend_kernel(own_ref, q_ref, k_ref, v_ref, qseg_ref, kseg_ref, bias_ref, o_ref, low_ref, lse_ref, tiles_ref, s_ref, *, chunks, chunk_tiles):
    pair = pl.program_id(0)
    own = own_ref[0]
    for side in range(2):
        bias_tiles(bias_ref, tiles_ref, pair * 2 + side, side)
    q2 = stacked(q_ref[...])
    qseg = jnp.concatenate([qseg_ref[...], qseg_ref[...]], 0)

    def first(chunk, high):
        parts = scores_into(chunk, chunk_tiles, own, q2, k_ref, qseg, kseg_ref, tiles_ref, s_ref)
        return functools.reduce(jnp.maximum, parts, high)

    def second(chunk, total):
        for t in range(chunk_tiles):
            at = pl.ds((chunk * chunk_tiles + t) * TILE, TILE)
            powers = jnp.exp(s_ref[:, at] - high)
            s_ref[:, at] = powers
            total = total + powers
        return total

    def third(chunk, acc):
        base = chunk * chunk_tiles * TILE
        at = pl.ds(base, chunk_tiles * TILE)
        low = (s_ref[:, at] * inverse).astype(BF16)
        return acc + dot(low, v_ref[at, :])

    def loop(body, start):
        return body(0, start) if chunks == 1 else lax.fori_loop(0, chunks, body, start)

    high = loop(first, jnp.full((2 * TILE, TILE), MASKED, F32))
    high = jnp.max(high, axis=1, keepdims=True)
    total = jnp.sum(loop(second, jnp.zeros((2 * TILE, TILE), F32)), axis=1, keepdims=True)
    inverse = 1.0 / total
    out = unstacked(loop(third, jnp.zeros((2 * TILE, TILE), F32)))
    o_ref[...] = out
    low_ref[...] = out.astype(BF16)
    lse_ref[...] = jnp.broadcast_to(high + jnp.log(total), (2 * TILE, TILE))


def attend_back_kernel(own_ref, q_ref, k_ref, v_ref, do_ref, o_ref, lse_ref, qseg_ref, kseg_ref, bias_ref, dq_ref, dk_ref, dv_ref, sums_ref, tiles_ref, s_ref, near_ref, *, chunks, chunk_tiles):
    pair = pl.program_id(0)
    own = own_ref[0]
    for side in range(2):
        bias_tiles(bias_ref, tiles_ref, pair * 2 + side, side)
    q2 = stacked(q_ref[...])
    do2 = stacked(do_ref[...])
    delta = jnp.sum(stacked(do_ref[...].astype(F32) * o_ref[...]), axis=1, keepdims=True)
    lse = lse_ref[:, :1]
    qseg = jnp.concatenate([qseg_ref[...], qseg_ref[...]], 0)
    near_ref[...] = jnp.zeros_like(near_ref)

    def step(chunk, carried):
        acc, left, right = carried
        base = chunk * chunk_tiles * TILE
        at = pl.ds(base, chunk_tiles * TILE)
        scores_into(chunk, chunk_tiles, own, q2, k_ref, qseg, kseg_ref, tiles_ref, s_ref)
        probs = jnp.exp(s_ref[:, at] - lse)
        grad_probs = dot_nt(do2, v_ref[at, :])
        grads = (probs * (grad_probs - delta)).astype(BF16)
        acc = acc + dot(grads, k_ref[at, :])
        dk_ref[at, :] = dot_tn(grads, q2).astype(BF16)
        dv_ref[at, :] = dot_tn(probs.astype(BF16), do2).astype(BF16)
        wide = grads.astype(F32)
        for t in range(chunk_tiles):
            gap = chunk * chunk_tiles + t - own
            tile = wide[:, t * TILE : (t + 1) * TILE]
            left = left + jnp.where(gap < -1, tile, 0.0)
            right = right + jnp.where(gap > 1, tile, 0.0)

            @pl.when(jnp.abs(gap) <= 1)
            def _():
                near_ref[jnp.clip(gap + 1, 0, 2)] = tile

        return acc, left, right

    zero = jnp.zeros((2 * TILE, TILE), F32)
    start = (zero, zero, zero)
    acc, left, right = step(0, start) if chunks == 1 else lax.fori_loop(0, chunks, step, start)
    dq_ref[...] = unstacked(acc).astype(BF16)
    flip = (
        lax.broadcasted_iota(jnp.int32, (TILE, TILE), 0) + lax.broadcasted_iota(jnp.int32, (TILE, TILE), 1) == TILE - 1
    ).astype(BF16)
    for side in range(2):
        rows = slice(side * TILE, (side + 1) * TILE)
        window = jnp.concatenate([near_ref[t, rows, :] for t in range(4)], 1).astype(BF16)
        turned = pltpu.roll(dot(flip, window), 0, 1, stride=1, stride_axis=0)
        near_sum = jnp.sum(turned, axis=0, keepdims=True)
        far = [jnp.sum(jnp.sum(part[rows], axis=0, keepdims=True), axis=1, keepdims=True) for part in (left, right)]
        sums_ref[0, side : side + 1, :WIN] = near_sum
        lane = lax.broadcasted_iota(jnp.int32, (1, TILE), 1)
        sums_ref[0, side : side + 1, WIN:] = jnp.where(lane == 0, far[0], jnp.where(lane == 1, far[1], 0.0))


def attention_calls(length, width, heads):
    pairs = heads // 2
    tiles = length // TILE
    chunk_tiles = min(8, tiles)
    chunks = tiles // chunk_tiles
    wide = WIN + TILE
    lanes = width // pairs
    own_spec = pl.BlockSpec(memory_space=pltpu.SMEM)
    q_spec = pl.BlockSpec((TILE, lanes), lambda p: (0, p))
    k_spec = pl.BlockSpec((length, lanes), lambda p: (0, p))
    qseg_spec = pl.BlockSpec((TILE, 1), lambda p: (0, 0))
    kseg_spec = pl.BlockSpec((1, length), lambda p: (0, 0))
    bias_spec = pl.BlockSpec((heads, wide), lambda p: (0, 0))
    lse_spec = pl.BlockSpec((2 * TILE, TILE), lambda p: (p, 0))
    sums_spec = pl.BlockSpec((1, 2, wide), lambda p: (p, 0, 0))
    scratch = [pltpu.VMEM((5, 2 * TILE, TILE), F32), pltpu.VMEM((2 * TILE, length), F32)]
    params = pltpu.CompilerParams(vmem_limit_bytes=VMEM_LIMIT)

    def shape(dims, kind):
        return jax.ShapeDtypeStruct(dims, kind)

    forward = pl.pallas_call(
        functools.partial(attend_kernel, chunks=chunks, chunk_tiles=chunk_tiles),
        grid=(pairs,),
        in_specs=[own_spec, q_spec, k_spec, k_spec, qseg_spec, kseg_spec, bias_spec],
        out_specs=[q_spec, q_spec, lse_spec],
        out_shape=[shape((TILE, width), F32), shape((TILE, width), BF16), shape((pairs * 2 * TILE, TILE), F32)],
        scratch_shapes=scratch,
        compiler_params=params,
        name="attend",
    )
    backward = pl.pallas_call(
        functools.partial(attend_back_kernel, chunks=chunks, chunk_tiles=chunk_tiles),
        grid=(pairs,),
        in_specs=[own_spec, q_spec, k_spec, k_spec, q_spec, q_spec, lse_spec, qseg_spec, kseg_spec, bias_spec],
        out_specs=[q_spec, k_spec, k_spec, sums_spec],
        out_shape=[
            shape((TILE, width), BF16),
            shape((length, width), BF16),
            shape((length, width), BF16),
            shape((pairs, 2, wide), F32),
        ],
        scratch_shapes=scratch + [pltpu.VMEM((4, 2 * TILE, TILE), F32)],
        compiler_params=params,
        name="attend_back",
    )
    return forward, backward


def normed(rows):
    scale = lax.rsqrt(jnp.mean(rows * rows, axis=-1, keepdims=True) + EPS)
    return rows * scale, scale


def norm_back(grad, gain, unit, scale):
    scaled = grad * gain
    return (scaled - unit * jnp.mean(scaled * unit, axis=-1, keepdims=True)) * scale


def body(inputs, segments, w_query, w_key, w_value, w_out, w_in, w_back, w_proj, gain_attn, gain_ffn, gain_final, rel_table, cotangent):
    links = Links()
    bits = links.bits
    tokens, width = inputs.shape[1:]
    ff = w_in.shape[1]
    proj = w_proj.shape[1]
    buckets, heads = rel_table.shape
    length = tokens * links.blocks
    rows = w_query.shape[0]
    own = lax.axis_index("blk").reshape(1).astype(jnp.int32)

    gains = jnp.stack([gain_attn, gain_ffn, gain_final], 1)
    gains = jnp.pad(gains, ((0, 0), (0, TILE - gains.shape[1])))
    pack_qkv = jnp.concatenate([w_query, w_key, w_value, gains], 1)
    pack_mid = jnp.concatenate([w_out, w_in, w_proj], 1)
    blk_down = [b for b in links.blk_bits if b > 1] + [1]
    order_a = blk_down + links.head_bits[::-1]
    own_rows = inputs[0]
    all_rows = gather_rows(links, own_rows, blk_down, links.blk_bits)
    seg_all = gather_rows(links, segments, blk_down, links.blk_bits)
    full_qkv = gather_rows(links, pack_qkv, order_a, bits)
    full_mid = gather_rows(links, pack_mid, order_a, bits)
    full_back = gather_rows(links, w_back, order_a, bits)
    full_query, full_key, full_value = (full_qkv[:, i * width : (i + 1) * width] for i in range(3))
    gain_rows = full_qkv[:, 3 * width :].astype(F32).T
    gain_one, gain_two, gain_three = gain_rows[0], gain_rows[1], gain_rows[2]
    full_out = full_mid[:, :width]
    full_in = full_mid[:, width : width + ff]
    full_proj = full_mid[:, width + ff :]

    offsets = bucket_np(window_offsets())
    onehot = np.zeros((WIN + TILE, buckets), np.float32)
    onehot[np.arange(WIN), offsets] = 1.0
    onehot[WIN, 15] = 1.0
    onehot[WIN + 1, 31] = 1.0
    bias = lax.dot_general(
        rel_table, jnp.asarray(onehot, BF16), (((0,), (1,)), ((), ())), preferred_element_type=F32
    )

    states_in = own_rows.astype(F32)
    unit_all, scale_all = normed(all_rows.astype(F32))
    hidden_all = (unit_all * gain_one).astype(BF16)
    unit_one, scale_one = normed(states_in)
    hidden_one = (unit_one * gain_one).astype(BF16)
    query = dot(hidden_one, full_query).astype(BF16)
    key = dot(hidden_all, full_key).astype(BF16)
    value = dot(hidden_all, full_value).astype(BF16)
    attend, attend_back = attention_calls(length, width, heads)
    qseg = segments.reshape(tokens, 1)
    kseg = seg_all.reshape(1, length)
    attended, attended_low, lse = attend(own, query, key, value, qseg, kseg, bias)
    resid_one = states_in + dot(attended_low, full_out)
    unit_two, scale_two = normed(resid_one)
    hidden_two = (unit_two * gain_two).astype(BF16)
    upward = dot(hidden_two, full_in)
    active, back_gelu = jax.vjp(lambda u: jax.nn.gelu(u, approximate=True), upward)
    active_low = active.astype(BF16)
    resid_two = resid_one + dot(active_low, full_back)
    unit_three, scale_three = normed(resid_two)
    final_low = (unit_three * gain_three).astype(BF16)
    states = dot(final_low, full_proj).astype(BF16)

    arriving = cotangent[0]
    grad_proj = dot_tn(final_low, arriving)
    grad_final = dot_nt(arriving, full_proj)
    grad_gain_three = jnp.sum(grad_final * unit_three, axis=0)
    grad_two = norm_back(grad_final, gain_three, unit_three, scale_three)
    grad_branch = grad_two.astype(BF16)
    grad_back = dot_tn(active_low, grad_branch)
    grad_up = back_gelu(dot_nt(grad_branch, full_back))[0].astype(BF16)
    grad_in = dot_tn(hidden_two, grad_up)
    grad_hidden_two = dot_nt(grad_up, full_in)
    grad_gain_two = jnp.sum(grad_hidden_two * unit_two, axis=0)
    grad_one = grad_two + norm_back(grad_hidden_two, gain_two, unit_two, scale_two)
    grad_attn = grad_one.astype(BF16)
    grad_out = dot_tn(attended_low, grad_attn)
    grad_attended = dot_nt(grad_attn, full_out).astype(BF16)
    grad_q, grad_k, grad_v, sums = attend_back(
        own, query, key, value, grad_attended, attended, lse, qseg, kseg, bias
    )
    grad_query = dot_tn(hidden_one, grad_q)
    grad_key = dot_tn(hidden_all, grad_k)
    grad_value = dot_tn(hidden_all, grad_v)
    grad_rows = dot_nt(grad_k, full_key) + dot_nt(grad_v, full_value)
    own_part = dot_nt(grad_q, full_query)
    first = lax.axis_index("blk") * tokens
    grad_rows = lax.dynamic_update_slice_in_dim(
        grad_rows, lax.dynamic_slice_in_dim(grad_rows, first, tokens, 0) + own_part, first, 0
    )
    grad_gain_one = jnp.sum(grad_rows * unit_all, axis=0)

    up_order = links.head_bits + [1] + [b for b in links.blk_bits if b > 1][::-1]
    blk_up = [1] + [b for b in links.blk_bits if b > 1][::-1]
    reduced_back = scatter_sum(links, grad_back, up_order, bits)
    reduced_mid = scatter_sum(links, jnp.concatenate([grad_out, grad_in, grad_proj], 1), up_order, bits)
    gain_grads = jnp.stack([grad_gain_one, grad_gain_two, grad_gain_three], 1)
    gain_grads = jnp.pad(gain_grads, ((0, 0), (0, TILE - 3)))
    reduced_qkv = scatter_sum(
        links, jnp.concatenate([grad_query, grad_key, grad_value, gain_grads], 1), up_order, bits
    )
    grad_hidden_one = scatter_sum(links, grad_rows, blk_up, links.blk_bits)
    input_gradient_rows = grad_one + norm_back(grad_hidden_one, gain_one, unit_one, scale_one)

    per_head = sums.reshape(heads, WIN + TILE)
    lane = np.arange(WIN)
    diagonal = np.zeros((WIN + TILE, buckets), np.float32)
    reach = lane - (TILE - 1) - TILE
    diagonal[lane, bucket_np(reach)] = 1.0
    diagonal[WIN, 15] = 1.0
    diagonal[WIN + 1, 31] = 1.0
    table = lax.dot_general(
        jnp.asarray(diagonal), per_head, (((0,), (1,)), ((), ())), precision=lax.Precision.HIGHEST
    )
    table = jnp.pad(table, ((0, 0), (0, TILE - heads)))
    for bit in bits:
        table = table + links.swap(table, bit)
    return (
        states[None],
        input_gradient_rows[None],
        reduced_qkv[:, :width],
        reduced_qkv[:, width : 2 * width],
        reduced_qkv[:, 2 * width : 3 * width],
        reduced_mid[:, :width],
        reduced_mid[:, width : width + ff],
        reduced_back,
        reduced_mid[:, width + ff :],
        reduced_qkv[:, 3 * width],
        reduced_qkv[:, 3 * width + 1],
        reduced_qkv[:, 3 * width + 2],
        table[:, :heads],
    )


def solution(mesh):
    rows = P(("head", "blk"), None)
    line = P(("head", "blk"))
    tokens = P("head", "blk", None)
    in_specs = (tokens, P("head", "blk")) + (rows,) * 7 + (line,) * 3 + (P(), tokens)
    out_specs = (tokens, tokens) + (rows,) * 7 + (line,) * 3 + (P(),)
    return jax.shard_map(body, mesh=mesh, in_specs=in_specs, out_specs=out_specs, check_vma=False)
```

time: 1360 us -> 427 us (0.31)
  waiting for transfers between devices: 832 us -> 234 us
  blocking collectives: 306 us -> 0 us
  matrix products: 112 us -> 40.8 us
  starting transfers between devices: 12.2 us -> 48.2 us
  Pallas kernels: 0 us -> 20.8 us
  other arithmetic: 27.4 us -> 46.4 us
  local copies, waits for them, and re-layouts: 45.9 us -> 29.1 us
    reduce_scatter x6 -> x0, waiting for transfers between devices: 649 us -> none  [the longest x1 142 us: body(): lax.psum_scatter(grad_in, ('head', 'blk'), scatter_dimension=0, tiled=True)]
    ppermute x0 -> x44, waiting for transfers between devices: none -> 234 us  [swap(): return lax.ppermute(value, AXES, [(i, i ^ bit) for i in range(self.total)])]
    all_gather x4 -> x0, blocking collectives: 186 us -> none  [the longest x1 67.5 us: body(): lax.all_gather(w_proj, ('head', 'blk'), axis=0, tiled=True)]
    all_gather x10 -> x0, waiting for transfers between devices: 174 us -> none  [the longest x1 62.2 us: body(): lax.all_gather(w_back, ('head', 'blk'), axis=0, tiled=True)]
    unnamed x2 -> x0, blocking collectives: 80.7 us -> none
    dot_general x47 -> x23, matrix products: 112 us -> 40.8 us  [the longest x7 16.7 us: dot_tn(): lax.dot_general(a, b, (((0,), (0,)), ((), ())), preferred_element_type=F32)]
    ppermute x0 -> x44, starting transfers between devices: none -> 48.2 us  [swap(): return lax.ppermute(value, AXES, [(i, i ^ bit) for i in range(self.total)])]
    all_to_all x5 -> x0, blocking collectives: 39.4 us -> none  [the longest x1 8.19 us: body(): lax.all_to_all(grad_key_low, 'head', split_axis=0, concat_axis=2, tiled=T...]
  transfers between devices with their start and end apart: 20 -> 44, of which waited for: 13 -> 24; matrix products, arithmetic and copies ran while one was open for 13% -> 18% of each run, Pallas kernels for 0% -> 2%
where the time goes in v1:
time: 427 us; the launch traced here: 421 us
  waiting for transfers between devices  234 us (55%)
  starting transfers between devices  48.2 us (11%)
  other arithmetic  46.4 us (11%)
  matrix products  40.8 us (10%)
  local copies, waits for them, and re-layouts  29.1 us (7%)
  Pallas kernels  20.8 us (5%)
    ppermute x44, waiting for transfers between devices, swap(): return lax.ppermute(value, AXES, [(i, i ^ bit) for i in range(self.total)])  234 us
    ppermute x44, starting transfers between devices, swap(): return lax.ppermute(value, AXES, [(i, i ^ bit) for i in range(self.total)])  48.2 us
    dot_general x7, matrix products, dot_tn(): lax.dot_general(a, b, (((0,), (0,)), ((), ())), preferred_element_type=F32)  16.7 us
    select_n x21, other arithmetic, gather_rows(): jnp.where(links.mine(bit), jnp.concatenate([other, value], axis), jnp.con...  15.6 us
    add x14, other arithmetic, scatter_sum(): value = kept.astype(F32) + links.swap(sent, bit).astype(F32)  14.3 us
    pallas_call x1, Pallas kernels, body(): attend_back(own, query, key, value, grad_attended, attended, lse, qseg, k...  13 us
    convert_element_type x18, local copies, waits for them, and re-layouts, scatter_sum(): sent = lax.dynamic_slice_in_dim(value, 1 - side, 1, axis).astype(BF16)  10.6 us
    dot_general x7, matrix products, dot(): return jnp.dot(a, b, preferred_element_type=F32)  10.6 us
  transfers between devices with their start and end apart: 44, of which 24 were waited for; matrix products, arithmetic and copies ran while one was open for 18% of the time, Pallas kernels for 2%

profile of v1, /device:TPU:0, one launch (start us, length us, event | category | flops | bytes accessed | tf_op | source)
XLA Modules:
  0.0 421.2 jit_solution(10330906223352826322)
XLA Ops:
  3.1 3.0 collective-permute-start.11
  7.8 2.0 collective-permute-start.5
  9.9 1.9 collective-permute-start.16
  12.9 1.7 convolution_bitcast_fusion.1.bias_ref
  14.7 3.8 collective-permute-done.8
  19.2 3.0 collective-permute-start.9
  23.7 1.9 collective-permute-start.10
  25.6 1.4 copy.106.qseg_ref
  28.0 3.0 collective-permute-start.1
  31.4 3.0 collective-permute-start.12
  34.8 27.0 %collective-permute-done.1 = bf16[1,1,1,2,1,24,2432]{6,5,3,2,4,1,0:T(8,128)(2,1)S(1)} collective-permute-done((bf16[1,1,1,2,1,24,2432]{6,5,3,2,4,1,0:T(8,128)(2,1)S(1)}, bf16[1,1,1,2,1,24,2432]{6,5,3,2,4,1,0:T(8,128)(2,1)S(1)}, u32[]{:S(2)}, u32[]{:S(2)}) %collective-permute-start.1) | collective-permute-done | bytes 233504 | tf_op jit(solution)/shard_map/ppermute | solution.py:57
  61.9 1.4 collective-permute-start.2
  63.4 4.8 %collective-permute-done.17 = bf16[1,1,1,2,1,96,768]{6,5,3,2,4,1,0:T(8,128)(2,1)S(1)} collective-permute-done((bf16[1,1,1,2,1,96,768]{6,5,3,2,4,1,0:T(8,128)(2,1)S(1)}, bf16[1,1,1,2,1,96,768]{6,5,3,2,4,1,0:T(8,128)(2,1)S(1)}, u32[]{:S(2)}, u32[]{:S(2)}) %collective-permute-start.17) | collective-permute-done | bytes 294944 | tf_op jit(solution)/shard_map/ppermute | solution.py:57
  69.8 6.6 %collective-permute-done.12 = bf16[1,1,1,2,1,24,3968]{6,5,3,2,4,1,0:T(8,128)(2,1)S(1)} collective-permute-done((bf16[1,1,1,2,1,24,3968]{6,5,3,2,4,1,0:T(8,128)(2,1)S(1)}, bf16[1,1,1,2,1,24,3968]{6,5,3,2,4,1,0:T(8,128)(2,1)S(1)}, u32[]{:S(2)}, u32[]{:S(2)}) %collective-permute-start.12) | collective-permute-done | bytes 380960 | tf_op jit(solution)/shard_map/ppermute | solution.py:57
  78.0 5.7 %collective-permute-done.6 = bf16[1,2,1,128,768]{4,3,1,2,0:T(8,128)(2,1)S(1)} collective-permute-done((bf16[1,2,1,128,768]{4,3,1,2,0:T(8,128)(2,1)S(1)}, bf16[1,2,1,128,768]{4,3,1,2,0:T(8,128)(2,1)S(1)}, u32[]{:S(2)}, u32[]{:S(2)}) %collective-permute-start.6) | collective-permute-done | bytes 393248 | tf_op jit(solution)/shard_map/ppermute | solution.py:57
  85.4 1.6 collective-permute-start.3
  87.2 17.4 %collective-permute-done.13 = bf16[1,1,2,2,1,24,3968]{6,5,3,2,4,1,0:T(8,128)(2,1)S(1)} collective-permute-done((bf16[1,1,2,2,1,24,3968]{6,5,3,2,4,1,0:T(8,128)(2,1)S(1)}, bf16[1,1,2,2,1,24,3968]{6,5,3,2,4,1,0:T(8,128)(2,1)S(1)}, u32[]{:S(2)}, u32[]{:S(2)}) %collective-permute-start.13) | collective-permute-done | bytes 761888 | tf_op jit(solution)/shard_map/ppermute | solution.py:57
  105.0 1.6 collective-permute-start.14
  107.4 1.7 collective-permute-done.3
  110.1 8.4 %collective-permute-done.7 = bf16[2,2,1,128,768]{4,3,1,2,0:T(8,128)(2,1)S(1)} collective-permute-done((bf16[2,2,1,128,768]{4,3,1,2,0:T(8,128)(2,1)S(1)}, bf16[2,2,1,128,768]{4,3,1,2,0:T(8,128)(2,1)S(1)}, u32[]{:S(2)}, u32[]{:S(2)}) %collective-permute-start.7) | collective-permute-done | bytes 786464 | tf_op jit(solution)/shard_map/ppermute | solution.py:57
  119.7 22.1 %collective-permute-done.14 = bf16[1,1,2,2,2,24,3968]{6,5,4,3,2,1,0:T(8,128)(2,1)S(1)} collective-permute-done((bf16[1,1,2,2,2,24,3968]{6,5,4,3,2,1,0:T(8,128)(2,1)S(1)}, bf16[1,1,2,2,2,24,3968]{6,5,4,3,2,1,0:T(8,128)(2,1)S(1)}, u32[]{:S(2)}, u32[]{:S(2)}) %collective-permute-start.14) | collective-permute-done | bytes 1523744 | tf_op jit(solution)/shard_map/ppermute | solution.py:57
  142.6 22.1 %collective-permute-done.19 = bf16[1,1,2,2,2,96,768]{6,5,4,3,2,1,0:T(8,128)(2,1)S(1)} collective-permute-done((bf16[1,1,2,2,2,96,768]{6,5,4,3,2,1,0:T(8,128)(2,1)S(1)}, bf16[1,1,2,2,2,96,768]{6,5,4,3,2,1,0:T(8,128)(2,1)S(1)}, u32[]{:S(2)}, u32[]{:S(2)}) %collective-permute-start.19) | collective-permute-done | bytes 1179680 | tf_op jit(solution)/shard_map/ppermute | solution.py:57
  164.7 1.8 maximum_select_fusion.4
  169.5 2.6 convolution_convert_fusion.1.k_ref
  172.1 2.5 convolution_convert_fusion.v_ref
  174.7 7.8 %attend.1 = (f32[128,768]{1,0:T(8,128)}, bf16[128,768]{1,0:T(8,128)(2,1)}, f32[1536,128]{1,0:T(8,128)}) custom-call(s32[1]{0:T(128)} %bitcast.1.own_ref, bf16[128,768]{1,0:T(8,128)(2,1)} %convolution_convert_fusion.3.q_ref, bf16[1024,768]{1,0:T(8,128)(2,1)} %convolution_convert_fusion.1.k_ref, bf16[1024,768]{1,0:T(8,128)(2,1)} %convolution_convert_fusion.v_ref, ...), custom_call_target="tpu_custom_call" | custom-call | tf_op jit(solution)/shard_map/attend/pallas_call | solution.py:334
  182.5 4.5 %maximum_select_fusion.1 = bf16[2,2,2,2,2,96,768]{6,5,4,3,2,1,0:T(8,128)(2,1)S(1)} fusion(bf16[2,1,2,2,2,96,768]{6,5,4,3,2,1,0:T(8,128)(2,1)} %maximum_select_fusion.4, bf16[2,1,2,2,2,96,768]{6,5,4,3,2,1,0:T(8,128)(2,1)} %collective-permute-done.20, pred[]{:T(512)S(6)} %ne.10), kind=kLoop, calls=%fused_computation.5 | loop fusion | flops 7077888 | bytes 9437185 | tf_op jit(solution)/shard_map/jit(_where)/select_n | solution.py:69
  187.1 4.0 maximum_select_fusion
  194.0 1.9 fusion.10
  195.9 1.7 multiply_reduce_fusion.3
  199.0 13.0 %attend_back.1 = (bf16[128,768]{1,0:T(8,128)(2,1)}, bf16[1024,768]{1,0:T(8,128)(2,1)}, bf16[1024,768]{1,0:T(8,128)(2,1)}, f32[6,2,640]{2,1,0:T(2,128)}) custom-call(s32[1]{0:T(128)} %bitcast.1.own_ref, bf16[128,768]{1,0:T(8,128)(2,1)} %convolution_convert_fusion.3.q_ref, bf16[1024,768]{1,0:T(8,128)(2,1)} %convolution_convert_fusion.1.k_ref, ...), custom_call_target="tpu_custom_call" | custom-call | tf_op jit(solution)/shard_map/attend_back/pallas_call | solution.py:361
  212.1 3.3 fusion.17
  215.4 1.4 fusion.85
  217.9 5.1 %fusion.73 = f32[768,3072]{1,0:T(8,128)} fusion(bf16[128,3072]{1,0:T(8,128)(2,1)S(1)} %copy-done.21, f32[128,768]{1,0:T(8,128)S(1)} %get-tuple-element.58, f32[768]{0:T(1024)S(1)} %get-tuple-element.32, f32[128]{0:T(128)S(1)} %add_rsqrt_fusion.2), kind=kOutput, calls=%fused_computation.196 | convolution fusion | flops 604274688 | bytes 10620416 | tf_op jit(solution)/shard_map/dot_general | solution.py:44
  223.0 1.9 fusion.54
  225.0 5.2 %fusion.57 = f32[3072,768]{1,0:T(8,128)} fusion(f32[128,768]{1,0:T(8,128)S(1)} %subtract_multiply_fusion, f32[128,3072]{1,0:T(8,128)S(1)} %fusion.2), kind=kOutput, calls=%fused_computation.164 | convolution fusion | flops 607617024 | bytes 11403264 | tf_op jit(solution)/shard_map/dot_general | solution.py:44
  230.2 1.4 fusion.84
  232.2 1.5 convolution_add_fusion
  237.3 3.3 pad_maximum_fusion.1
  240.6 8.8 %copy.123 = f32[768,2432]{1,0:T(8,128)} copy(f32[768,2432]{0,1:T(8,128)} %pad_maximum_fusion.1) | data formatting | bytes 14942208 | tf_op jit(solution)/shard_map/concatenate | solution.py:382
  249.5 3.5 dynamic-slice_convert_fusion.2
  255.6 2.8 dynamic-slice_convert_fusion.1
  258.9 1.5 collective-permute-start.40
  260.4 4.5 %pad_maximum_fusion = f32[768,3968]{1,0:T(8,128)S(1)} fusion(f32[768,128]{1,0:T(8,128)S(1)} %copy-done.16, f32[768,3072]{1,0:T(8,128)} %fusion.73, f32[768,768]{1,0:T(8,128)S(1)} %copy-done.7), kind=kLoop, calls=%fused_computation | loop fusion | flops 6094848 | bytes 24379392 | tf_op jit(solution)/shard_map/concatenate | solution.py:378
  264.9 3.4 collective-permute-start.41
  270.2 1.8 collective-permute-done.41
  272.1 1.8 fusion.14
  274.3 1.5 collective-permute-start.43
  275.9 14.0 %collective-permute-done.22 = bf16[1,2,1,128,768]{4,3,2,1,0:T(8,128)(2,1)S(1)} collective-permute-done((bf16[1,2,1,128,768]{4,3,2,1,0:T(8,128)(2,1)S(1)}, bf16[1,2,1,128,768]{4,3,2,1,0:T(8,128)(2,1)S(1)}, u32[]{:S(2)}, u32[]{:S(2)}) %collective-permute-start.22) | collective-permute-done | bytes 393248 | tf_op jit(solution)/shard_map/ppermute | solution.py:57
  290.1 3.3 convert_add_fusion.2
  294.4 1.5 collective-permute-start.25
  297.6 2.3 convert_add_fusion.1
  301.2 1.5 collective-permute-start.35
  302.7 15.6 %collective-permute-done.25 = bf16[1,1,2,2,2,24,2432]{6,5,4,3,2,1,0:T(8,128)(2,1)} collective-permute-done((bf16[1,1,2,2,2,24,2432]{6,5,4,3,2,1,0:T(8,128)(2,1)}, bf16[1,1,2,2,2,24,2432]{6,5,4,3,2,1,0:T(8,128)(2,1)}, u32[]{:S(2)}, u32[]{:S(2)}) %collective-permute-start.25) | collective-permute-done | bytes 933920 | tf_op jit(solution)/shard_map/ppermute | solution.py:57
  320.3 2.4 convert_add_fusion
  322.9 1.6 collective-permute-start.30
  324.5 6.2 %collective-permute-done.26 = bf16[1,1,2,2,1,24,2432]{6,5,4,3,2,1,0:T(8,128)(2,1)} collective-permute-done((bf16[1,1,2,2,1,24,2432]{6,5,4,3,2,1,0:T(8,128)(2,1)S(1)}, bf16[1,1,2,2,1,24,2432]{6,5,4,3,2,1,0:T(8,128)(2,1)}, u32[]{:S(2)}, u32[]{:S(2)}) %collective-permute-start.26) | collective-permute-done | bytes 466976 | tf_op jit(solution)/shard_map/ppermute | solution.py:57
  334.0 8.7 %collective-permute-done.27 = bf16[1,1,1,2,1,24,2432]{6,5,4,3,2,1,0:T(8,128)(2,1)S(1)} collective-permute-done((bf16[1,1,1,2,1,24,2432]{6,5,4,3,2,1,0:T(8,128)(2,1)S(1)}, bf16[1,1,1,2,1,24,2432]{6,5,4,3,2,1,0:T(8,128)(2,1)S(1)}, u32[]{:S(2)}, u32[]{:S(2)}) %collective-permute-start.27) | collective-permute-done | bytes 233504 | tf_op jit(solution)/shard_map/ppermute | solution.py:57
  343.5 1.6 convert_add_fusion.4
  345.9 29.3 %collective-permute-done.30 = bf16[1,1,2,2,2,24,3968]{6,5,4,3,2,1,0:T(8,128)(2,1)S(1)} collective-permute-done((bf16[1,1,2,2,2,24,3968]{6,5,4,3,2,1,0:T(8,128)(2,1)S(1)}, bf16[1,1,2,2,2,24,3968]{6,5,4,3,2,1,0:T(8,128)(2,1)S(1)}, u32[]{:S(2)}, u32[]{:S(2)}) %collective-permute-start.30) | collective-permute-done | bytes 1523744 | tf_op jit(solution)/shard_map/ppermute | solution.py:57
  377.1 1.5 collective-permute-start.37
  378.5 15.1 %collective-permute-done.31 = bf16[1,1,2,2,1,24,3968]{6,5,4,3,2,1,0:T(8,128)(2,1)S(1)} collective-permute-done((bf16[1,1,2,2,1,24,3968]{6,5,4,3,2,1,0:T(8,128)(2,1)S(1)}, bf16[1,1,2,2,1,24,3968]{6,5,4,3,2,1,0:T(8,128)(2,1)S(1)}, u32[]{:S(2)}, u32[]{:S(2)}) %collective-permute-start.31) | collective-permute-done | bytes 761888 | tf_op jit(solution)/shard_map/ppermute | solution.py:57
  396.8 15.2 %collective-permute-done.32 = bf16[1,1,1,2,1,24,3968]{6,5,4,3,2,1,0:T(8,128)(2,1)S(1)} collective-permute-done((bf16[1,1,1,2,1,24,3968]{6,5,4,3,2,1,0:T(8,128)(2,1)S(1)}, bf16[1,1,1,2,1,24,3968]{6,5,4,3,2,1,0:T(8,128)(2,1)S(1)}, u32[]{:S(2)}, u32[]{:S(2)}) %collective-permute-start.32) | collective-permute-done | bytes 380960 | tf_op jit(solution)/shard_map/ppermute | solution.py:57
  413.0 5.7 %collective-permute-done.33 = bf16[1,1,1,1,1,24,3968]{6,5,4,3,2,1,0:T(8,128)(2,1)S(1)} collective-permute-done((bf16[1,1,1,1,1,24,3968]{6,5,4,3,2,1,0:T(8,128)(2,1)S(1)}, bf16[1,1,1,1,1,24,3968]{6,5,4,3,2,1,0:T(8,128)(2,1)S(1)}, u32[]{:S(2)}, u32[]{:S(2)}) %collective-permute-start.33) | collective-permute-done | bytes 190496 | tf_op jit(solution)/shard_map/ppermute | solution.py:57
  (225 shorter events, 56.2 us)
Async XLA Ops:
  0.6 192.9 %copy-start = (bf16[1,128,128]{2,1,0:T(8,128)(2,1)S(1)}, bf16[1,128,128]{2,1,0:T(8,128)(2,1)}, u32[]{:S(2)}) copy-start(bf16[1,128,128]{2,1,0:T(8,128)(2,1)} %param.29) | copy-start | bytes 98308
  0.7 30.4 %copy-start.22 = (bf16[96,768]{1,0:T(8,128)(2,1)S(1)}, bf16[96,768]{1,0:T(8,128)(2,1)}, u32[]{:S(2)}) copy-start(bf16[96,768]{1,0:T(8,128)(2,1)} %param.23) | copy-start | bytes 442372
  3.1 28.2 %collective-permute-start.11 = (bf16[1,1,1,1,1,24,3968]{6,5,4,3,2,1,0:T(8,128)(2,1)S(1)}, bf16[1,1,1,1,1,24,3968]{6,5,4,3,2,1,0:T(8,128)(2,1)S(1)}, u32[]{:S(2)}, u32[]{:S(2)}) collective-permute-start(bf16[1,1,1,1,1,24,3968]{6,5,4,3,2,1,0:T(8,128)(2,1)S(1)} %bitcast.249), channel_id=1, source_target_pairs={{0,2},{1,3},{2,0},{3,1},{4,6},{5,7},{6,4},{7,5},{8,10},{9,11},{10,... | collective-permute-start | bytes 571400 | tf_op jit(solution)/shard_map/ppermute | solution.py:57
  7.8 20.2 %collective-permute-start = (bf16[1,1,1,1,1,24,2432]{6,5,4,3,2,1,0:T(8,128)(2,1)S(1)}, bf16[1,1,1,1,1,24,2432]{6,5,4,3,2,1,0:T(8,128)(2,1)S(1)}, u32[]{:S(2)}, u32[]{:S(2)}) collective-permute-start(bf16[1,1,1,1,1,24,2432]{6,5,4,3,2,1,0:T(8,128)(2,1)S(1)} %get-tuple-element.56), channel_id=1, source_target_pairs={{0,2},{1,3},{2,0},{3,1},{4,6},{5,7},{6,4},{7,5},{8,10},{9,11},{10,... | collective-permute-start | bytes 350216 | tf_op jit(solution)/shard_map/ppermute | solution.py:57
  7.8 26.7 %collective-permute-start.5 = (bf16[1,1,1,128,768]{4,3,1,2,0:T(8,128)(2,1)}, bf16[1,1,1,128,768]{4,3,1,2,0:T(8,128)(2,1)S(1)}, u32[]{:S(2)}, u32[]{:S(2)}) collective-permute-start(bf16[1,1,1,128,768]{4,3,1,2,0:T(8,128)(2,1)} %bitcast.235), channel_id=1, source_target_pairs={{0,2},{1,3},{2,0},{3,1},{4,6},{5,7},{6,4},{7,5},{8,10},{9,11},{10,... | collective-permute-start | bytes 589832 | tf_op jit(solution)/shard_map/ppermute | solution.py:57
  9.8 8.7 %collective-permute-start.8 = (s32[1,1,1,1,128]{4,3,2,1,0:T(1,128)}, s32[1,1,1,1,128]{4,3,2,1,0:T(1,128)S(1)}, u32[]{:S(2)}, u32[]{:S(2)}) collective-permute-start(s32[1,1,1,1,128]{4,3,2,1,0:T(1,128)} %bitcast.263), channel_id=1, source_target_pairs={{0,2},{1,3},{2,0},{3,1},{4,6},{5,7},{6,4},{7,5},{8,10},{9,11},{10,... | collective-permute-start | bytes 1544 | tf_op jit(solution)/shard_map/ppermute | solution.py:57
  9.9 21.1 %collective-permute-start.16 = (bf16[1,1,1,1,1,96,768]{6,5,4,3,2,1,0:T(8,128)(2,1)}, bf16[1,1,1,1,1,96,768]{6,5,4,3,2,1,0:T(8,128)(2,1)S(1)}, u32[]{:S(2)}, u32[]{:S(2)}) collective-permute-start(bf16[1,1,1,1,1,96,768]{6,5,4,3,2,1,0:T(8,128)(2,1)} %bitcast.254), channel_id=1, source_target_pairs={{0,2},{1,3},{2,0},{3,1},{4,6},{5,7},{6,4},{7,5},{8,10},{9,11},{10,... | collective-permute-start | bytes 442376 | tf_op jit(solution)/shard_map/ppermute | solution.py:57
  19.2 4.5 %collective-permute-start.9 = (s32[1,2,1,1,128]{4,3,2,1,0:T(1,128)S(1)}, s32[1,2,1,1,128]{4,3,2,1,0:T(1,128)S(1)}, u32[]{:S(2)}, u32[]{:S(2)}) collective-permute-start(s32[1,2,1,1,128]{4,3,2,1,0:T(1,128)S(1)} %broadcast_select_fusion.2), channel_id=1, source_target_pairs={{0,4},{1,5},{2,6},{3,7},{4,0},{5,1},{6,2},{7,3},{8,12},{9,13},{10,... | collective-permute-start | bytes 3080 | tf_op jit(solution)/shard_map/ppermute | solution.py:57
  23.7 3.6 collective-permute-start.10
  28.0 33.8 %collective-permute-start.1 = (bf16[1,1,1,2,1,24,2432]{6,5,3,2,4,1,0:T(8,128)(2,1)S(1)}, bf16[1,1,1,2,1,24,2432]{6,5,3,2,4,1,0:T(8,128)(2,1)S(1)}, u32[]{:S(2)}, u32[]{:S(2)}) collective-permute-start(bf16[1,1,1,2,1,24,2432]{6,5,3,2,4,1,0:T(8,128)(2,1)S(1)} %fusion.45), channel_id=1, source_target_pairs={{0,4},{1,5},{2,6},{3,7},{4,0},{5,1},{6,2},{7,3},{8,12},{9,13},{10,... | collective-permute-start | bytes 700424 | tf_op jit(solution)/shard_map/ppermute | solution.py:57
  31.1 37.0 %collective-permute-start.17 = (bf16[1,1,1,2,1,96,768]{6,5,3,2,4,1,0:T(8,128)(2,1)S(1)}, bf16[1,1,1,2,1,96,768]{6,5,3,2,4,1,0:T(8,128)(2,1)S(1)}, u32[]{:S(2)}, u32[]{:S(2)}) collective-permute-start(bf16[1,1,1,2,1,96,768]{6,5,3,2,4,1,0:T(8,128)(2,1)S(1)} %fusion.44), channel_id=1, source_target_pairs={{0,4},{1,5},{2,6},{3,7},{4,0},{5,1},{6,2},{7,3},{8,12},{9,13},{10,... | collective-permute-start | bytes 884744 | tf_op jit(solution)/shard_map/ppermute | solution.py:57
  31.4 44.9 %collective-permute-start.12 = (bf16[1,1,1,2,1,24,3968]{6,5,3,2,4,1,0:T(8,128)(2,1)S(1)}, bf16[1,1,1,2,1,24,3968]{6,5,3,2,4,1,0:T(8,128)(2,1)S(1)}, u32[]{:S(2)}, u32[]{:S(2)}) collective-permute-start(bf16[1,1,1,2,1,24,3968]{6,5,3,2,4,1,0:T(8,128)(2,1)S(1)} %fusion.43), channel_id=1, source_target_pairs={{0,4},{1,5},{2,6},{3,7},{4,0},{5,1},{6,2},{7,3},{8,12},{9,13},{10,... | collective-permute-start | bytes 1142792 | tf_op jit(solution)/shard_map/ppermute | solution.py:57
  34.6 49.1 %collective-permute-start.6 = (bf16[1,2,1,128,768]{4,3,1,2,0:T(8,128)(2,1)S(1)}, bf16[1,2,1,128,768]{4,3,1,2,0:T(8,128)(2,1)S(1)}, u32[]{:S(2)}, u32[]{:S(2)}) collective-permute-start(bf16[1,2,1,128,768]{4,3,1,2,0:T(8,128)(2,1)S(1)} %maximum_select_fusion.14), channel_id=1, source_target_pairs={{0,4},{1,5},{2,6},{3,7},{4,0},{5,1},{6,2},{7,3},{8,12},{9,13},{10,... | collective-permute-start | bytes 1179656 | tf_op jit(solution)/shard_map/ppermute | solution.py:57
  61.9 23.2 %collective-permute-start.2 = (bf16[1,1,2,2,1,24,2432]{6,5,3,2,4,1,0:T(8,128)(2,1)S(1)}, bf16[1,1,2,2,1,24,2432]{6,5,3,2,4,1,0:T(8,128)(2,1)S(1)}, u32[]{:S(2)}, u32[]{:S(2)}) collective-permute-start(bf16[1,1,2,2,1,24,2432]{6,5,3,2,4,1,0:T(8,128)(2,1)S(1)} %fusion.33), channel_id=1, source_target_pairs={{0,1},{1,0},{2,3},{3,2},{4,5},{5,4},{6,7},{7,6},{8,9},{9,8},{10,11... | collective-permute-start | bytes 1400840 | tf_op jit(solution)/shard_map/ppermute | solution.py:57
  68.3 38.3 %collective-permute-start.18 = (bf16[1,1,2,2,1,96,768]{6,5,3,2,4,1,0:T(8,128)(2,1)S(1)}, bf16[1,1,2,2,1,96,768]{6,5,3,2,4,1,0:T(8,128)(2,1)S(1)}, u32[]{:S(2)}, u32[]{:S(2)}) collective-permute-start(bf16[1,1,2,2,1,96,768]{6,5,3,2,4,1,0:T(8,128)(2,1)S(1)} %fusion.28), channel_id=1, source_target_pairs={{0,1},{1,0},{2,3},{3,2},{4,5},{5,4},{6,7},{7,6},{8,9},{9,8},{10,11... | collective-permute-start | bytes 1769480 | tf_op jit(solution)/shard_map/ppermute | solution.py:57
  76.5 28.1 %collective-permute-start.13 = (bf16[1,1,2,2,1,24,3968]{6,5,3,2,4,1,0:T(8,128)(2,1)S(1)}, bf16[1,1,2,2,1,24,3968]{6,5,3,2,4,1,0:T(8,128)(2,1)S(1)}, u32[]{:S(2)}, u32[]{:S(2)}) collective-permute-start(bf16[1,1,2,2,1,24,3968]{6,5,3,2,4,1,0:T(8,128)(2,1)S(1)} %fusion.26), channel_id=1, source_target_pairs={{0,1},{1,0},{2,3},{3,2},{4,5},{5,4},{6,7},{7,6},{8,9},{9,8},{10,11... | collective-permute-start | bytes 2285576 | tf_op jit(solution)/shard_map/ppermute | solution.py:57
  83.9 34.6 %collective-permute-start.7 = (bf16[2,2,1,128,768]{4,3,1,2,0:T(8,128)(2,1)S(1)}, bf16[2,2,1,128,768]{4,3,1,2,0:T(8,128)(2,1)S(1)}, u32[]{:S(2)}, u32[]{:S(2)}) collective-permute-start(bf16[2,2,1,128,768]{4,3,1,2,0:T(8,128)(2,1)S(1)} %maximum_select_fusion.13), channel_id=1, source_target_pairs={{0,1},{1,0},{2,3},{3,2},{4,5},{5,4},{6,7},{7,6},{8,9},{9,8},{10,11... | collective-permute-start | bytes 2359304 | tf_op jit(solution)/shard_map/ppermute | solution.py:57
  85.4 23.7 %collective-permute-start.3 = (bf16[1,1,2,2,2,24,2432]{6,5,4,3,2,1,0:T(8,128)(2,1)S(1)}, bf16[1,1,2,2,2,24,2432]{6,5,4,3,2,1,0:T(8,128)(2,1)S(1)}, u32[]{:S(2)}, u32[]{:S(2)}) collective-permute-start(bf16[1,1,2,2,2,24,2432]{6,5,4,3,2,1,0:T(8,128)(2,1)S(1)} %copy.103), channel_id=1, source_target_pairs={{0,16},{1,17},{2,18},{3,19},{4,20},{5,21},{6,22},{7,23},{8,24},{9,... | collective-permute-start | bytes 2801672 | tf_op jit(solution)/shard_map/ppermute | solution.py:57
  105.0 36.8 %collective-permute-start.14 = (bf16[1,1,2,2,2,24,3968]{6,5,4,3,2,1,0:T(8,128)(2,1)S(1)}, bf16[1,1,2,2,2,24,3968]{6,5,4,3,2,1,0:T(8,128)(2,1)S(1)}, u32[]{:S(2)}, u32[]{:S(2)}) collective-permute-start(bf16[1,1,2,2,2,24,3968]{6,5,4,3,2,1,0:T(8,128)(2,1)S(1)} %copy.113), channel_id=1, source_target_pairs={{0,16},{1,17},{2,18},{3,19},{4,20},{5,21},{6,22},{7,23},{8,24},{9,... | collective-permute-start | bytes 4571144 | tf_op jit(solution)/shard_map/ppermute | solution.py:57
  106.8 57.9 %collective-permute-start.19 = (bf16[1,1,2,2,2,96,768]{6,5,4,3,2,1,0:T(8,128)(2,1)S(1)}, bf16[1,1,2,2,2,96,768]{6,5,4,3,2,1,0:T(8,128)(2,1)S(1)}, u32[]{:S(2)}, u32[]{:S(2)}) collective-permute-start(bf16[1,1,2,2,2,96,768]{6,5,4,3,2,1,0:T(8,128)(2,1)S(1)} %copy.120), channel_id=1, source_target_pairs={{0,16},{1,17},{2,18},{3,19},{4,20},{5,21},{6,22},{7,23},{8,24},{9,... | collective-permute-start | bytes 3538952 | tf_op jit(solution)/shard_map/ppermute | solution.py:57
  109.4 57.1 %collective-permute-start.4 = (bf16[2,1,2,2,2,24,2432]{6,5,4,3,2,1,0:T(8,128)(2,1)S(1)}, bf16[2,1,2,2,2,24,2432]{6,5,4,3,2,1,0:T(8,128)(2,1)S(1)}, u32[]{:S(2)}, u32[]{:S(2)}) collective-permute-start(bf16[2,1,2,2,2,24,2432]{6,5,4,3,2,1,0:T(8,128)(2,1)S(1)} %maximum_select_fusion.5), channel_id=1, source_target_pairs={{0,8},{1,9},{2,10},{3,11},{4,12},{5,13},{6,14},{7,15},{8,0},{9,1},... | collective-permute-start | bytes 5603336 | tf_op jit(solution)/shard_map/ppermute | solution.py:57
  142.5 44.6 %collective-permute-start.15 = (bf16[2,1,2,2,2,24,3968]{6,5,4,3,2,1,0:T(8,128)(2,1)S(1)}, bf16[2,1,2,2,2,24,3968]{6,5,4,3,2,1,0:T(8,128)(2,1)}, u32[]{:S(2)}, u32[]{:S(2)}) collective-permute-start(bf16[2,1,2,2,2,24,3968]{6,5,4,3,2,1,0:T(8,128)(2,1)S(1)} %maximum_select_fusion.3), channel_id=1, source_target_pairs={{0,8},{1,9},{2,10},{3,11},{4,12},{5,13},{6,14},{7,15},{8,0},{9,1},... | collective-permute-start | bytes 9142280 | tf_op jit(solution)/shard_map/ppermute | solution.py:57
  166.5 16.1 %collective-permute-start.20 = (bf16[2,1,2,2,2,96,768]{6,5,4,3,2,1,0:T(8,128)(2,1)}, bf16[2,1,2,2,2,96,768]{6,5,4,3,2,1,0:T(8,128)(2,1)}, u32[]{:S(2)}, u32[]{:S(2)}) collective-permute-start(bf16[2,1,2,2,2,96,768]{6,5,4,3,2,1,0:T(8,128)(2,1)} %maximum_select_fusion.4), channel_id=1, source_target_pairs={{0,8},{1,9},{2,10},{3,11},{4,12},{5,13},{6,14},{7,15},{8,0},{9,1},... | collective-permute-start | bytes 7077896 | tf_op jit(solution)/shard_map/ppermute | solution.py:57
  167.3 4.9 %copy-start.5 = (bf16[2,2,2,2,2,24,2432]{6,5,4,3,2,1,0:T(8,128)(2,1)}, bf16[2,2,2,2,2,24,2432]{6,5,4,3,2,1,0:T(8,128)(2,1)S(1)}, u32[]{:S(2)}) copy-start(bf16[2,2,2,2,2,24,2432]{6,5,4,3,2,1,0:T(8,128)(2,1)S(1)} %maximum_select_fusion.2) | copy-start | bytes 11206660
  191.1 6.8 %copy-start.2 = (bf16[2,2,2,2,2,24,3968]{6,5,4,3,2,1,0:T(8,128)(2,1)}, bf16[2,2,2,2,2,24,3968]{6,5,4,3,2,1,0:T(8,128)(2,1)S(1)}, u32[]{:S(2)}) copy-start(bf16[2,2,2,2,2,24,3968]{6,5,4,3,2,1,0:T(8,128)(2,1)S(1)} %maximum_select_fusion) | copy-start | bytes 18284548
  193.5 23.4 %copy-start.9 = (f32[128,768]{1,0:T(8,128)}, f32[128,768]{1,0:T(8,128)S(1)}, u32[]{:S(2)}) copy-start(f32[128,768]{1,0:T(8,128)S(1)} %get-tuple-element.60) | copy-start | bytes 1179652
  197.8 25.2 %copy-start.11 = (f32[128,768]{1,0:T(8,128)}, f32[128,768]{1,0:T(8,128)S(1)}, u32[]{:S(2)}) copy-start(f32[128,768]{1,0:T(8,128)S(1)} %multiply_add_fusion) | copy-start | bytes 1179652
  217.9 5.1 %copy-start.24 = (bf16[128,768]{1,0:T(8,128)(2,1)S(1)}, bf16[128,768]{1,0:T(8,128)(2,1)}, u32[]{:S(2)}) copy-start(bf16[128,768]{1,0:T(8,128)(2,1)} %get-tuple-element.20) | copy-start | bytes 589828
  225.0 5.2 %copy-start.15 = (bf16[1024,768]{1,0:T(8,128)(2,1)S(1)}, bf16[1024,768]{1,0:T(8,128)(2,1)}, u32[]{:S(2)}) copy-start(bf16[1024,768]{1,0:T(8,128)(2,1)} %get-tuple-element.23) | copy-start | bytes 4718596
  236.2 32.1 %collective-permute-start.21 = (bf16[2,2,1,128,768]{4,3,2,1,0:T(8,128)(2,1)}, bf16[2,2,1,128,768]{4,3,2,1,0:T(8,128)(2,1)}, u32[]{:S(2)}, u32[]{:S(2)}) collective-permute-start(bf16[2,2,1,128,768]{4,3,2,1,0:T(8,128)(2,1)} %dynamic-slice_convert_fusion.6), channel_id=1, source_target_pairs={{0,1},{1,0},{2,3},{3,2},{4,5},{5,4},{6,7},{7,6},{8,9},{9,8},{10,11... | collective-permute-start | bytes 2359304 | tf_op jit(solution)/shard_map/ppermute | solution.py:57
  253.0 37.1 %collective-permute-start.24 = (bf16[2,1,2,2,2,24,2432]{6,5,4,3,2,1,0:T(8,128)(2,1)}, bf16[2,1,2,2,2,24,2432]{6,5,4,3,2,1,0:T(8,128)(2,1)}, u32[]{:S(2)}, u32[]{:S(2)}) collective-permute-start(bf16[2,1,2,2,2,24,2432]{6,5,4,3,2,1,0:T(8,128)(2,1)} %dynamic-slice_convert_fusion.2), channel_id=1, source_target_pairs={{0,8},{1,9},{2,10},{3,11},{4,12},{5,13},{6,14},{7,15},{8,0},{9,1},... | collective-permute-start | bytes 5603336 | tf_op jit(solution)/shard_map/ppermute | solution.py:57
  254.5 4.3 %collective-permute-start.39 = (f32[32,128]{0,1:T(8,128)S(1)}, f32[32,128]{0,1:T(8,128)S(1)}, u32[]{:S(2)}, u32[]{:S(2)}) collective-permute-start(f32[32,128]{0,1:T(8,128)S(1)} %pad.14), channel_id=1, source_target_pairs={{0,1},{1,0},{2,3},{3,2},{4,5},{5,4},{6,7},{7,6},{8,9},{9,8},{10,11... | collective-permute-start | bytes 49160 | tf_op jit(solution)/shard_map/ppermute | solution.py:57
  255.6 4.8 %copy-start.7 = (f32[768,768]{1,0:T(8,128)S(1)}, f32[768,768]{1,0:T(8,128)}, u32[]{:S(2)}) copy-start(f32[768,768]{1,0:T(8,128)} %fusion.54) | copy-start | bytes 7077892
  255.6 4.8 %copy-start.16 = (f32[768,128]{1,0:T(8,128)S(1)}, f32[768,128]{1,0:T(8,128)}, u32[]{:S(2)}) copy-start(f32[768,128]{1,0:T(8,128)} %fusion.68) | copy-start | bytes 1179652
  258.4 39.2 %collective-permute-start.34 = (bf16[2,1,2,2,2,96,768]{6,5,4,3,2,1,0:T(8,128)(2,1)S(1)}, bf16[2,1,2,2,2,96,768]{6,5,4,3,2,1,0:T(8,128)(2,1)}, u32[]{:S(2)}, u32[]{:S(2)}) collective-permute-start(bf16[2,1,2,2,2,96,768]{6,5,4,3,2,1,0:T(8,128)(2,1)S(1)} %dynamic-slice_convert_fusion.1), channel_id=1, source_target_pairs={{0,8},{1,9},{2,10},{3,11},{4,12},{5,13},{6,14},{7,15},{8,0},{9,1},... | collective-permute-start | bytes 7077896 | tf_op jit(solution)/shard_map/ppermute | solution.py:57
  258.9 6.0 %collective-permute-start.40 = (f32[32,128]{0,1:T(8,128)S(1)}, f32[32,128]{0,1:T(8,128)S(1)}, u32[]{:S(2)}, u32[]{:S(2)}) collective-permute-start(f32[32,128]{0,1:T(8,128)S(1)} %pad_add_fusion), channel_id=1, source_target_pairs={{0,2},{1,3},{2,0},{3,1},{4,6},{5,7},{6,4},{7,5},{8,10},{9,11},{10,... | collective-permute-start | bytes 49160 | tf_op jit(solution)/shard_map/ppermute | solution.py:57
  264.9 7.0 %collective-permute-start.41 = (f32[32,128]{0,1:T(8,128)S(1)}, f32[32,128]{0,1:T(8,128)S(1)}, u32[]{:S(2)}, u32[]{:S(2)}) collective-permute-start(f32[32,128]{0,1:T(8,128)S(1)} %add.248), channel_id=1, source_target_pairs={{0,4},{1,5},{2,6},{3,7},{4,0},{5,1},{6,2},{7,3},{8,12},{9,13},{10,... | collective-permute-start | bytes 49160 | tf_op jit(solution)/shard_map/ppermute | solution.py:57
  268.3 29.2 %slice-start = ((s8[9437184]{0:T(1024)(128)(4,1)}), s8[1048576]{0:T(1024)(128)(4,1)S(1)}, s32[]{:S(2)}) async-start(s8[9437184]{0:T(1024)(128)(4,1)} %bitcast.213), calls=%async_computation | async-start | bytes 2097152
  269.8 20.1 %collective-permute-start.22 = (bf16[1,2,1,128,768]{4,3,2,1,0:T(8,128)(2,1)S(1)}, bf16[1,2,1,128,768]{4,3,2,1,0:T(8,128)(2,1)S(1)}, u32[]{:S(2)}, u32[]{:S(2)}) collective-permute-start(bf16[1,2,1,128,768]{4,3,2,1,0:T(8,128)(2,1)S(1)} %dynamic-slice_convert_fusion.10), channel_id=1, source_target_pairs={{0,4},{1,5},{2,6},{3,7},{4,0},{5,1},{6,2},{7,3},{8,12},{9,13},{10,... | collective-permute-start | bytes 1179656 | tf_op jit(solution)/shard_map/ppermute | solution.py:57
  269.9 27.7 %slice-start.1 = ((s8[9437184]{0:T(1024)(128)(4,1)}), s8[4194304]{0:T(1024)(128)(4,1)S(1)}, s32[]{:S(2)}) async-start(s8[9437184]{0:T(1024)(128)(4,1)} %bitcast.213), calls=%async_computation.1 | async-start | bytes 8388608
  271.9 2.4 collective-permute-start.42
  273.9 46.5 %collective-permute-start.29 = (bf16[2,1,2,2,2,24,3968]{6,5,4,3,2,1,0:T(8,128)(2,1)S(1)}, bf16[2,1,2,2,2,24,3968]{6,5,4,3,2,1,0:T(8,128)(2,1)}, u32[]{:S(2)}, u32[]{:S(2)}) collective-permute-start(bf16[2,1,2,2,2,24,3968]{6,5,4,3,2,1,0:T(8,128)(2,1)S(1)} %dynamic-slice_convert_fusion), channel_id=1, source_target_pairs={{0,8},{1,9},{2,10},{3,11},{4,12},{5,13},{6,14},{7,15},{8,0},{9,1},... | collective-permute-start | bytes 9142280 | tf_op jit(solution)/shard_map/ppermute | solution.py:57
  274.3 21.5 %collective-permute-start.43 = (f32[32,128]{0,1:T(8,128)S(1)}, f32[32,128]{0,1:T(8,128)S(1)}, u32[]{:S(2)}, u32[]{:S(2)}) collective-permute-start(f32[32,128]{0,1:T(8,128)S(1)} %add.250), channel_id=1, source_target_pairs={{0,16},{1,17},{2,18},{3,19},{4,20},{5,21},{6,22},{7,23},{8,24},{9,... | collective-permute-start | bytes 49160 | tf_op jit(solution)/shard_map/ppermute | solution.py:57
  289.9 7.0 %copy-start.13 = (f32[1,2,1,128,768]{4,3,2,1,0:T(8,128)}, f32[1,2,1,128,768]{4,3,2,1,0:T(8,128)S(1)}, u32[]{:S(2)}) copy-start(f32[1,2,1,128,768]{4,3,2,1,0:T(8,128)S(1)} %convert_add_fusion.10) | copy-start | bytes 2359300
  290.0 7.6 %slice-start.2 = ((s8[9437184]{0:T(1024)(128)(4,1)}), s8[4194304]{0:T(1024)(128)(4,1)S(1)}, s32[]{:S(2)}) async-start(s8[9437184]{0:T(1024)(128)(4,1)} %bitcast.213), calls=%async_computation.2 | async-start | bytes 8388608
  290.0 6.9 %collective-permute-start.23 = (bf16[1,1,1,128,768]{4,3,2,1,0:T(8,128)(2,1)S(1)}, bf16[1,1,1,128,768]{4,3,2,1,0:T(8,128)(2,1)S(1)}, u32[]{:S(2)}, u32[]{:S(2)}) collective-permute-start(bf16[1,1,1,128,768]{4,3,2,1,0:T(8,128)(2,1)S(1)} %dynamic-slice_convert_fusion.14), channel_id=1, source_target_pairs={{0,2},{1,3},{2,0},{3,1},{4,6},{5,7},{6,4},{7,5},{8,10},{9,11},{10,... | collective-permute-start | bytes 589832 | tf_op jit(solution)/shard_map/ppermute | solution.py:57
  294.4 23.9 %collective-permute-start.25 = (bf16[1,1,2,2,2,24,2432]{6,5,4,3,2,1,0:T(8,128)(2,1)}, bf16[1,1,2,2,2,24,2432]{6,5,4,3,2,1,0:T(8,128)(2,1)}, u32[]{:S(2)}, u32[]{:S(2)}) collective-permute-start(bf16[1,1,2,2,2,24,2432]{6,5,4,3,2,1,0:T(8,128)(2,1)} %dynamic-slice_convert_fusion.5), channel_id=1, source_target_pairs={{0,16},{1,17},{2,18},{3,19},{4,20},{5,21},{6,22},{7,23},{8,24},{9,... | collective-permute-start | bytes 2801672 | tf_op jit(solution)/shard_map/ppermute | solution.py:57
  299.9 19.7 %copy-start.3 = (f32[2,1,2,2,2,96,768]{6,5,4,3,2,1,0:T(8,128)}, f32[2,1,2,2,2,96,768]{6,5,4,3,2,1,0:T(8,128)S(1)}, u32[]{:S(2)}) copy-start(f32[2,1,2,2,2,96,768]{6,5,4,3,2,1,0:T(8,128)S(1)} %convert_add_fusion.1) | copy-start | bytes 14155780
  301.2 42.4 %collective-permute-start.35 = (bf16[1,1,2,2,2,96,768]{6,5,4,3,2,1,0:T(8,128)(2,1)}, bf16[1,1,2,2,2,96,768]{6,5,4,3,2,1,0:T(8,128)(2,1)}, u32[]{:S(2)}, u32[]{:S(2)}) collective-permute-start(bf16[1,1,2,2,2,96,768]{6,5,4,3,2,1,0:T(8,128)(2,1)} %dynamic-slice_convert_fusion.4), channel_id=1, source_target_pairs={{0,16},{1,17},{2,18},{3,19},{4,20},{5,21},{6,22},{7,23},{8,24},{9,... | collective-permute-start | bytes 3538952 | tf_op jit(solution)/shard_map/ppermute | solution.py:57
  319.7 11.0 %collective-permute-start.26 = (bf16[1,1,2,2,1,24,2432]{6,5,4,3,2,1,0:T(8,128)(2,1)S(1)}, bf16[1,1,2,2,1,24,2432]{6,5,4,3,2,1,0:T(8,128)(2,1)}, u32[]{:S(2)}, u32[]{:S(2)}) collective-permute-start(bf16[1,1,2,2,1,24,2432]{6,5,4,3,2,1,0:T(8,128)(2,1)S(1)} %dynamic-slice_convert_fusion.9), channel_id=1, source_target_pairs={{0,1},{1,0},{2,3},{3,2},{4,5},{5,4},{6,7},{7,6},{8,9},{9,8},{10,11... | collective-permute-start | bytes 1400840 | tf_op jit(solution)/shard_map/ppermute | solution.py:57
  322.7 10.4 %copy-start.14 = (f32[1,2,1,128,768]{4,3,2,1,0:T(8,128)S(1)}, f32[1,2,1,128,768]{4,3,2,1,0:T(8,128)}, u32[]{:S(2)}) copy-start(f32[1,2,1,128,768]{4,3,2,1,0:T(8,128)} %copy-done.13) | copy-start | bytes 2359300
  322.9 10.2 %copy-start.12 = (f32[128,768]{1,0:T(8,128)S(1)}, f32[128,768]{1,0:T(8,128)}, u32[]{:S(2)}) copy-start(f32[128,768]{1,0:T(8,128)} %copy-done.11) | copy-start | bytes 1179652
  322.9 10.2 %copy-start.19 = (bf16[1,1,1,128,768]{4,3,2,1,0:T(8,128)(2,1)S(1)}, bf16[1,1,1,128,768]{4,3,2,1,0:T(8,128)(2,1)}, u32[]{:S(2)}) copy-start(bf16[1,1,1,128,768]{4,3,2,1,0:T(8,128)(2,1)} %copy-done.18) | copy-start | bytes 589828
  322.9 52.2 %collective-permute-start.30 = (bf16[1,1,2,2,2,24,3968]{6,5,4,3,2,1,0:T(8,128)(2,1)S(1)}, bf16[1,1,2,2,2,24,3968]{6,5,4,3,2,1,0:T(8,128)(2,1)S(1)}, u32[]{:S(2)}, u32[]{:S(2)}) collective-permute-start(bf16[1,1,2,2,2,24,3968]{6,5,4,3,2,1,0:T(8,128)(2,1)S(1)} %dynamic-slice_convert_fusion.3), channel_id=1, source_target_pairs={{0,16},{1,17},{2,18},{3,19},{4,20},{5,21},{6,22},{7,23},{8,24},{9,... | collective-permute-start | bytes 4571144 | tf_op jit(solution)/shard_map/ppermute | solution.py:57
  330.7 12.9 %copy-start.4 = (f32[2,1,2,2,2,96,768]{6,5,4,3,2,1,0:T(8,128)S(1)}, f32[2,1,2,2,2,96,768]{6,5,4,3,2,1,0:T(8,128)}, u32[]{:S(2)}) copy-start(f32[2,1,2,2,2,96,768]{6,5,4,3,2,1,0:T(8,128)} %copy-done.3) | copy-start | bytes 14155780
  332.0 10.8 %collective-permute-start.27 = (bf16[1,1,1,2,1,24,2432]{6,5,4,3,2,1,0:T(8,128)(2,1)S(1)}, bf16[1,1,1,2,1,24,2432]{6,5,4,3,2,1,0:T(8,128)(2,1)S(1)}, u32[]{:S(2)}, u32[]{:S(2)}) collective-permute-start(bf16[1,1,1,2,1,24,2432]{6,5,4,3,2,1,0:T(8,128)(2,1)S(1)} %dynamic-slice_convert_fusion.13), channel_id=1, source_target_pairs={{0,4},{1,5},{2,6},{3,7},{4,0},{5,1},{6,2},{7,3},{8,12},{9,13},{10,... | collective-permute-start | bytes 700424 | tf_op jit(solution)/shard_map/ppermute | solution.py:57
  342.8 33.3 %collective-permute-start.28 = (bf16[1,1,1,1,1,24,2432]{6,5,4,3,2,1,0:T(8,128)(2,1)S(1)}, bf16[1,1,1,1,1,24,2432]{6,5,4,3,2,1,0:T(8,128)(2,1)S(1)}, u32[]{:S(2)}, u32[]{:S(2)}) collective-permute-start(bf16[1,1,1,1,1,24,2432]{6,5,4,3,2,1,0:T(8,128)(2,1)S(1)} %dynamic-slice_convert_fusion.17), channel_id=1, source_target_pairs={{0,2},{1,3},{2,0},{3,1},{4,6},{5,7},{6,4},{7,5},{8,10},{9,11},{10,... | collective-permute-start | bytes 350216 | tf_op jit(solution)/shard_map/ppermute | solution.py:57
  345.2 31.7 %collective-permute-start.36 = (bf16[1,1,2,2,1,96,768]{6,5,4,3,2,1,0:T(8,128)(2,1)S(1)}, bf16[1,1,2,2,1,96,768]{6,5,4,3,2,1,0:T(8,128)(2,1)S(1)}, u32[]{:S(2)}, u32[]{:S(2)}) collective-permute-start(bf16[1,1,2,2,1,96,768]{6,5,4,3,2,1,0:T(8,128)(2,1)S(1)} %dynamic-slice_convert_fusion.8), channel_id=1, source_target_pairs={{0,1},{1,0},{2,3},{3,2},{4,5},{5,4},{6,7},{7,6},{8,9},{9,8},{10,11... | collective-permute-start | bytes 1769480 | tf_op jit(solution)/shard_map/ppermute | solution.py:57
  375.5 18.2 %collective-permute-start.31 = (bf16[1,1,2,2,1,24,3968]{6,5,4,3,2,1,0:T(8,128)(2,1)S(1)}, bf16[1,1,2,2,1,24,3968]{6,5,4,3,2,1,0:T(8,128)(2,1)S(1)}, u32[]{:S(2)}, u32[]{:S(2)}) collective-permute-start(bf16[1,1,2,2,1,24,3968]{6,5,4,3,2,1,0:T(8,128)(2,1)S(1)} %dynamic-slice_convert_fusion.7), channel_id=1, source_target_pairs={{0,1},{1,0},{2,3},{3,2},{4,5},{5,4},{6,7},{7,6},{8,9},{9,8},{10,11... | collective-permute-start | bytes 2285576 | tf_op jit(solution)/shard_map/ppermute | solution.py:57
  377.1 18.7 %collective-permute-start.37 = (bf16[1,1,1,2,1,96,768]{6,5,4,3,2,1,0:T(8,128)(2,1)S(1)}, bf16[1,1,1,2,1,96,768]{6,5,4,3,2,1,0:T(8,128)(2,1)S(1)}, u32[]{:S(2)}, u32[]{:S(2)}) collective-permute-start(bf16[1,1,1,2,1,96,768]{6,5,4,3,2,1,0:T(8,128)(2,1)S(1)} %dynamic-slice_convert_fusion.12), channel_id=1, source_target_pairs={{0,4},{1,5},{2,6},{3,7},{4,0},{5,1},{6,2},{7,3},{8,12},{9,13},{10,... | collective-permute-start | bytes 884744 | tf_op jit(solution)/shard_map/ppermute | solution.py:57
  393.9 18.1 %collective-permute-start.32 = (bf16[1,1,1,2,1,24,3968]{6,5,4,3,2,1,0:T(8,128)(2,1)S(1)}, bf16[1,1,1,2,1,24,3968]{6,5,4,3,2,1,0:T(8,128)(2,1)S(1)}, u32[]{:S(2)}, u32[]{:S(2)}) collective-permute-start(bf16[1,1,1,2,1,24,3968]{6,5,4,3,2,1,0:T(8,128)(2,1)S(1)} %dynamic-slice_convert_fusion.11), channel_id=1, source_target_pairs={{0,4},{1,5},{2,6},{3,7},{4,0},{5,1},{6,2},{7,3},{8,12},{9,13},{10,... | collective-permute-start | bytes 1142792 | tf_op jit(solution)/shard_map/ppermute | solution.py:57
  395.8 16.4 %collective-permute-start.38 = (bf16[1,1,1,1,1,96,768]{6,5,4,3,2,1,0:T(8,128)(2,1)S(1)}, bf16[1,1,1,1,1,96,768]{6,5,4,3,2,1,0:T(8,128)(2,1)S(1)}, u32[]{:S(2)}, u32[]{:S(2)}) collective-permute-start(bf16[1,1,1,1,1,96,768]{6,5,4,3,2,1,0:T(8,128)(2,1)S(1)} %dynamic-slice_convert_fusion.16), channel_id=1, source_target_pairs={{0,2},{1,3},{2,0},{3,1},{4,6},{5,7},{6,4},{7,5},{8,10},{9,11},{10,... | collective-permute-start | bytes 442376 | tf_op jit(solution)/shard_map/ppermute | solution.py:57
  412.0 8.7 %copy-start.1 = (bf16[1,128,128]{2,1,0:T(8,128)(2,1)S(1)}, bf16[1,128,128]{2,1,0:T(8,128)(2,1)}, u32[]{:S(2)}) copy-start(bf16[1,128,128]{2,1,0:T(8,128)(2,1)} %param.29) | copy-start | bytes 98308
  412.1 6.6 %collective-permute-start.33 = (bf16[1,1,1,1,1,24,3968]{6,5,4,3,2,1,0:T(8,128)(2,1)S(1)}, bf16[1,1,1,1,1,24,3968]{6,5,4,3,2,1,0:T(8,128)(2,1)S(1)}, u32[]{:S(2)}, u32[]{:S(2)}) collective-permute-start(bf16[1,1,1,1,1,24,3968]{6,5,4,3,2,1,0:T(8,128)(2,1)S(1)} %dynamic-slice_convert_fusion.15), channel_id=1, source_target_pairs={{0,2},{1,3},{2,0},{3,1},{4,6},{5,7},{6,4},{7,5},{8,10},{9,11},{10,... | collective-permute-start | bytes 571400 | tf_op jit(solution)/shard_map/ppermute | solution.py:57
  (10 other events, 25.2 us)

commit v2 on v1

--- a/solution.py
+++ b/solution.py
@@ -122,14 +122,15 @@
     for t in range(chunk_tiles):
         at = base + t * TILE
         near = tiles_ref[tile_kind(chunk * chunk_tiles + t, own)]
-        allowed = qseg == kseg_ref[:, pl.ds(at, TILE)]
+        allowed = qseg == kseg_ref[pl.ds(chunk * chunk_tiles + t, 1), :]
         tile = jnp.where(allowed, raw[:, t * TILE : (t + 1) * TILE] + near, MASKED)
         s_ref[:, pl.ds(at, TILE)] = tile
         parts.append(tile)
     return parts
 
 
-def attend_kernel(own_ref, q_ref, k_ref, v_ref, qseg_ref, kseg_ref, bias_ref, o_ref, low_ref, lse_ref, tiles_ref, s_ref, *, chunks, chunk_tiles):
+def attend_kernel(own_ref, q_ref, k_ref, v_ref, qseg_ref, kseg_ref, bias_ref, *refs, marks, chunks, chunk_tiles):
+    o_ref, low_ref, lse_ref, tiles_ref, s_ref = refs[marks:]
     pair = pl.program_id(0)
     own = own_ref[0]
     for side in range(2):
@@ -168,8 +169,9 @@
     lse_ref[...] = jnp.broadcast_to(high + jnp.log(total), (2 * TILE, TILE))
 
 
-def attend_back_kernel(own_ref, q_ref, k_ref, v_ref, do_ref, o_ref, lse_ref, qseg_ref, kseg_ref, bias_ref, dq_ref, dk_ref, dv_ref, sums_ref, tiles_ref, s_ref, near_ref, *, chunks, chunk_tiles):
-    pair = pl.program_id(0)
+def attend_back_kernel(own_ref, q_ref, k_ref, v_ref, do_ref, o_ref, lse_ref, qseg_ref, kseg_ref, bias_ref, *refs, first, marks, chunks, chunk_tiles):
+    dq_ref, dk_ref, dv_ref, sums_ref, tiles_ref, s_ref, near_ref = refs[marks:]
+    pair = pl.program_id(0) + first
     own = own_ref[0]
     for side in range(2):
         bias_tiles(bias_ref, tiles_ref, pair * 2 + side, side)
@@ -222,20 +224,24 @@
         sums_ref[0, side : side + 1, WIN:] = jnp.where(lane == 0, far[0], jnp.where(lane == 1, far[1], 0.0))
 
 
-def attention_calls(length, width, heads):
-    pairs = heads // 2
+def attention_calls(length, width, heads, first=0, pairs=None, marks=0):
+    total = heads // 2
+    pairs = pairs or total
     tiles = length // TILE
     chunk_tiles = min(8, tiles)
     chunks = tiles // chunk_tiles
     wide = WIN + TILE
-    lanes = width // pairs
+    lanes = width // total
+    any_spec = pl.BlockSpec(memory_space=pl.ANY)
     own_spec = pl.BlockSpec(memory_space=pltpu.SMEM)
-    q_spec = pl.BlockSpec((TILE, lanes), lambda p: (0, p))
-    k_spec = pl.BlockSpec((length, lanes), lambda p: (0, p))
+    q_spec = pl.BlockSpec((TILE, lanes), lambda p: (0, p + first))
+    k_spec = pl.BlockSpec((length, lanes), lambda p: (0, p + first))
+    dq_spec = pl.BlockSpec((TILE, lanes), lambda p: (0, p))
+    dk_spec = pl.BlockSpec((length, lanes), lambda p: (0, p))
     qseg_spec = pl.BlockSpec((TILE, 1), lambda p: (0, 0))
-    kseg_spec = pl.BlockSpec((1, length), lambda p: (0, 0))
+    kseg_spec = pl.BlockSpec((tiles, TILE), lambda p: (0, 0))
     bias_spec = pl.BlockSpec((heads, wide), lambda p: (0, 0))
-    lse_spec = pl.BlockSpec((2 * TILE, TILE), lambda p: (p, 0))
+    lse_spec = pl.BlockSpec((2 * TILE, TILE), lambda p: (p + first, 0))
     sums_spec = pl.BlockSpec((1, 2, wide), lambda p: (p, 0, 0))
     scratch = [pltpu.VMEM((5, 2 * TILE, TILE), F32), pltpu.VMEM((2 * TILE, length), F32)]
     params = pltpu.CompilerParams(vmem_limit_bytes=VMEM_LIMIT)
@@ -244,28 +250,31 @@
         return jax.ShapeDtypeStruct(dims, kind)
 
     forward = pl.pallas_call(
-        functools.partial(attend_kernel, chunks=chunks, chunk_tiles=chunk_tiles),
+        functools.partial(attend_kernel, marks=marks, chunks=chunks, chunk_tiles=chunk_tiles),
         grid=(pairs,),
-        in_specs=[own_spec, q_spec, k_spec, k_spec, qseg_spec, kseg_spec, bias_spec],
+        in_specs=[own_spec, q_spec, k_spec, k_spec, qseg_spec, kseg_spec, bias_spec] + [any_spec] * marks,
         out_specs=[q_spec, q_spec, lse_spec],
         out_shape=[shape((TILE, width), F32), shape((TILE, width), BF16), shape((pairs * 2 * TILE, TILE), F32)],
         scratch_shapes=scratch,
         compiler_params=params,
+        cost_estimate=pl.CostEstimate(flops=0, transcendentals=0, bytes_accessed=30 << 20),
         name="attend",
     )
     backward = pl.pallas_call(
-        functools.partial(attend_back_kernel, chunks=chunks, chunk_tiles=chunk_tiles),
+        functools.partial(attend_back_kernel, first=first, marks=marks, chunks=chunks, chunk_tiles=chunk_tiles),
         grid=(pairs,),
-        in_specs=[own_spec, q_spec, k_spec, k_spec, q_spec, q_spec, lse_spec, qseg_spec, kseg_spec, bias_spec],
-        out_specs=[q_spec, k_spec, k_spec, sums_spec],
+        in_specs=[own_spec, q_spec, k_spec, k_spec, q_spec, q_spec, lse_spec, qseg_spec, kseg_spec, bias_spec]
+        + [any_spec] * marks,
+        out_specs=[dq_spec, dk_spec, dk_spec, sums_spec],
         out_shape=[
-            shape((TILE, width), BF16),
-            shape((length, width), BF16),
-            shape((length, width), BF16),
+            shape((TILE, pairs * lanes), BF16),
+            shape((length, pairs * lanes), BF16),
+            shape((length, pairs * lanes), BF16),
             shape((pairs, 2, wide), F32),
         ],
         scratch_shapes=scratch + [pltpu.VMEM((4, 2 * TILE, TILE), F32)],
         compiler_params=params,
+        cost_estimate=pl.CostEstimate(flops=0, transcendentals=0, bytes_accessed=48 << 20),
         name="attend_back",
     )
     return forward, backward
@@ -281,7 +290,50 @@
     return (scaled - unit * jnp.mean(scaled * unit, axis=-1, keepdims=True)) * scale
 
 
-def body(inputs, segments, w_query, w_key, w_value, w_out, w_in, w_back, w_proj, gain_attn, gain_ffn, gain_final, rel_table, cotangent):
+def bias_rows(rel_table):
+    onehot = np.zeros((WIN + TILE, rel_table.shape[0]), np.float32)
+    onehot[np.arange(WIN), bucket_np(window_offsets())] = 1.0
+    onehot[WIN, 15] = 1.0
+    onehot[WIN + 1, 31] = 1.0
+    return lax.dot_general(
+        rel_table, jnp.asarray(onehot, BF16), (((0,), (1,)), ((), ())), preferred_element_type=F32
+    )
+
+
+def table_grad(sums, heads, buckets):
+    lane = np.arange(WIN)
+    diagonal = np.zeros((WIN + TILE, buckets), np.float32)
+    diagonal[lane, bucket_np(lane - (2 * TILE - 1))] = 1.0
+    diagonal[WIN, 15] = 1.0
+    diagonal[WIN + 1, 31] = 1.0
+    table = lax.dot_general(
+        jnp.asarray(diagonal),
+        sums.reshape(heads, WIN + TILE),
+        (((0,), (1,)), ((), ())),
+        precision=lax.Precision.HIGHEST,
+    )
+    return jnp.pad(table, ((0, 0), (0, TILE - heads)))
+
+
+def outputs_of(states, input_gradient_rows, reduced_qkv, reduced_mid, reduced_back, table, width, ff, heads):
+    return (
+        states[None],
+        input_gradient_rows[None],
+        reduced_qkv[:, :width],
+        reduced_qkv[:, width : 2 * width],
+        reduced_qkv[:, 2 * width : 3 * width],
+        reduced_mid[:, :width],
+        reduced_mid[:, width : width + ff],
+        reduced_back,
+        reduced_mid[:, width + ff :],
+        reduced_qkv[:, 3 * width],
+        reduced_qkv[:, 3 * width + 1],
+        reduced_qkv[:, 3 * width + 2],
+        table[:, :heads],
+    )
+
+
+def general_body(inputs, segments, w_query, w_key, w_value, w_out, w_in, w_back, w_proj, gain_attn, gain_ffn, gain_final, rel_table, cotangent):
     links = Links()
     bits = links.bits
     tokens, width = inputs.shape[1:]
@@ -311,14 +363,7 @@
     full_in = full_mid[:, width : width + ff]
     full_proj = full_mid[:, width + ff :]
 
-    offsets = bucket_np(window_offsets())
-    onehot = np.zeros((WIN + TILE, buckets), np.float32)
-    onehot[np.arange(WIN), offsets] = 1.0
-    onehot[WIN, 15] = 1.0
-    onehot[WIN + 1, 31] = 1.0
-    bias = lax.dot_general(
-        rel_table, jnp.asarray(onehot, BF16), (((0,), (1,)), ((), ())), preferred_element_type=F32
-    )
+    bias = bias_rows(rel_table)
 
     states_in = own_rows.astype(F32)
     unit_all, scale_all = normed(all_rows.astype(F32))
@@ -330,7 +375,7 @@
     value = dot(hidden_all, full_value).astype(BF16)
     attend, attend_back = attention_calls(length, width, heads)
     qseg = segments.reshape(tokens, 1)
-    kseg = seg_all.reshape(1, length)
+    kseg = seg_all
     attended, attended_low, lse = attend(own, query, key, value, qseg, kseg, bias)
     resid_one = states_in + dot(attended_low, full_out)
     unit_two, scale_two = normed(resid_one)
@@ -384,34 +429,433 @@
     grad_hidden_one = scatter_sum(links, grad_rows, blk_up, links.blk_bits)
     input_gradient_rows = grad_one + norm_back(grad_hidden_one, gain_one, unit_one, scale_one)
 
-    per_head = sums.reshape(heads, WIN + TILE)
-    lane = np.arange(WIN)
-    diagonal = np.zeros((WIN + TILE, buckets), np.float32)
-    reach = lane - (TILE - 1) - TILE
-    diagonal[lane, bucket_np(reach)] = 1.0
-    diagonal[WIN, 15] = 1.0
-    diagonal[WIN + 1, 31] = 1.0
-    table = lax.dot_general(
-        jnp.asarray(diagonal), per_head, (((0,), (1,)), ((), ())), precision=lax.Precision.HIGHEST
-    )
-    table = jnp.pad(table, ((0, 0), (0, TILE - heads)))
+    table = table_grad(sums, heads, rel_table.shape[0])
     for bit in bits:
         table = table + links.swap(table, bit)
-    return (
-        states[None],
-        input_gradient_rows[None],
-        reduced_qkv[:, :width],
-        reduced_qkv[:, width : 2 * width],
-        reduced_qkv[:, 2 * width : 3 * width],
-        reduced_mid[:, :width],
-        reduced_mid[:, width : width + ff],
-        reduced_back,
-        reduced_mid[:, width + ff :],
-        reduced_qkv[:, 3 * width],
-        reduced_qkv[:, 3 * width + 1],
-        reduced_qkv[:, 3 * width + 2],
-        table[:, :heads],
+    return outputs_of(states, input_gradient_rows, reduced_qkv, reduced_mid, reduced_back, table, width, ff, heads)
+
+
+X_BIT, CORE_BIT, Y_BIT = 16, 8, 1
+NEAR_BIT, OVER_BIT = 2, 4
+DEPTH = 4
+PEERS = 32
+
+
+def swap(value, mask, other_mask=None):
+    masks = (mask, mask if other_mask is None else other_mask)
+    return lax.ppermute(value, AXES, [(i, i ^ masks[(i // CORE_BIT) % 2]) for i in range(PEERS)])
+
+
+def depth_mask(place, core):
+    return (0, NEAR_BIT + core * (OVER_BIT - NEAR_BIT), OVER_BIT - core * (OVER_BIT - NEAR_BIT), NEAR_BIT | OVER_BIT)[place]
+
+
+def side_masks(core):
+    return Y_BIT + core * (X_BIT - Y_BIT), X_BIT - core * (X_BIT - Y_BIT)
+
+
+def tied(value, *earlier):
+    whole = functools.reduce(jnp.logical_and, [mark[(0,) * mark.ndim] == mark[(0,) * mark.ndim] for mark in earlier])
+    return jnp.where(whole, value, jnp.zeros_like(value))
+
+
+def gather_depth(own, first=None):
+    first = swap(own, NEAR_BIT, OVER_BIT) if first is None else first
+    pair = jnp.stack([own, first])
+    return jnp.concatenate([pair, swap(pair, OVER_BIT, NEAR_BIT)], 0)
+
+
+def gather_plane(column):
+    half = jnp.concatenate([column, swap(column, Y_BIT, X_BIT)], 0)
+    return half, swap(half, X_BIT, Y_BIT)
+
+
+def y_pairs(half, rest):
+    second = (lax.axis_index("head") % 2) == 1
+    high = (lax.axis_index("blk") % 2) == 1
+    pairs = (
+        (half[:DEPTH], jnp.where(second, rest[:DEPTH], half[DEPTH:])),
+        (jnp.where(second, half[DEPTH:], rest[:DEPTH]), rest[DEPTH:]),
     )
+    return [
+        jnp.where(high, jnp.concatenate([other, mine], 1), jnp.concatenate([mine, other], 1)) for mine, other in pairs
+    ]
+
+
+def gathered_items(core, paired):
+    items = []
+    for c in range(2):
+        here = core if c == 0 else 1 - core
+        first, second = side_masks(here)
+        for b in range(2):
+            for k in range(DEPTH):
+                depth = depth_mask(k, here)
+                if paired:
+                    items.append((2 * c + b, k, (c * CORE_BIT + b * X_BIT) | depth))
+                else:
+                    items += [
+                        (2 * c + b, a * DEPTH + k, (c * CORE_BIT) | (a * first) | (b * second) | depth) for a in range(2)
+                    ]
+    return items
+
+
+def sent_items(core):
+    items = []
+    for c in range(2):
+        here = core if c == 0 else 1 - core
+        minor, major = side_masks(here)
+        for a in range(2):
+            for b in range(2):
+                for k in range(DEPTH):
+                    place = a * 2 * DEPTH + b * DEPTH + k
+                    items.append((c, place, (c * CORE_BIT) | (a * major) | (b * minor) | depth_mask(k, here)))
+    return items
+
+
+def wide(value):
+    return value.astype(F32)
+
+
+def part_of(terms, first, last):
+    return sum(wide(term[first:last]) for term in terms)
+
+
+def next_sent(terms):
+    half = terms[-1].shape[0] // 2
+    return part_of(terms, half, 2 * half).astype(BF16)
+
+
+def halved(terms, masks, sent=None):
+    half = terms[-1].shape[0] // 2
+    return [term[:half] for term in terms] + [swap(next_sent(terms) if sent is None else sent, *masks)]
+
+
+FIRST_SIDE, SECOND_SIDE = (X_BIT, Y_BIT), (Y_BIT, X_BIT)
+FIRST_DEPTH, SECOND_DEPTH = (OVER_BIT, NEAR_BIT), (NEAR_BIT, OVER_BIT)
+
+
+ANY = pl.BlockSpec(memory_space=pl.ANY)
+SMEM = pl.BlockSpec(memory_space=pltpu.SMEM)
+WHOLE = pl.BlockSpec(memory_space=pltpu.VMEM)
+
+
+def load_shards(parts, me, target, sems, rows, paired):
+    copies = []
+    rows = 2 * rows if paired else rows
+    core = lax.rem(me // CORE_BIT, 2)
+    for n, (buffer, place, relative) in enumerate(gathered_items(core, paired)):
+        index = (me ^ relative) // 2 if paired else me ^ relative
+        at = pl.multiple_of(index * rows, 16)
+        copies.append(pltpu.make_async_copy(parts[buffer].at[place], target.at[pl.ds(at, rows), :], sems.at[n]))
+    for copy in copies:
+        copy.start()
+    return copies
+
+
+def store_blocks(source, me, targets, sems):
+    copies = []
+    for n, (side, place, relative) in enumerate(sent_items(lax.rem(me // CORE_BIT, 2))):
+        copies.append(pltpu.make_async_copy(source.at[me ^ relative], targets[side].at[place], sems.at[n]))
+    for copy in copies:
+        copy.start()
+    return copies
+
+
+def put_blocks(target, lanes, value):
+    rows = target.shape[1]
+    for p in range(PEERS):
+        target[p, :, lanes] = value[p * rows : (p + 1) * rows, :].astype(BF16)
+
+
+def wait_all(copies):
+    for copy in copies:
+        copy.wait()
+
+
+def project_kernel(me_ref, *refs, blocks, rows):
+    xs = refs[:2]
+    parts = refs[2:6]
+    h_ref, k_ref, v_ref, q_ref, gains_ref, seg_ref, w_ref, sems = refs[-8:]
+    me = me_ref[0]
+    own = lax.rem(me, blocks)
+    copies = load_shards(parts, me, w_ref, sems, rows, True)
+    width = h_ref.shape[1]
+    wait_all(copies)
+    gains_ref[...] = wide(w_ref[:, 3 * width :]).T[:8]
+    gain = gains_ref[0:1, :]
+    core = lax.rem(me // CORE_BIT, 2)
+    for r in range(blocks):
+        x_ref = xs[r // 4].at[r % 4]
+        unit, scale = normed(wide(x_ref[:TILE, :]))
+        hidden = (unit * gain).astype(BF16)
+        block = own ^ ((r & 1) * Y_BIT | depth_mask(r >> 1, core))
+        at = pl.multiple_of(block * TILE, TILE)
+        h_ref[pl.ds(at, TILE), :] = hidden
+        seg_ref[pl.ds(block, 1), :] = wide(x_ref[TILE : TILE + 1, :TILE])
+        if r == 0:
+            q_ref[...] = dot(hidden, w_ref[:, :width]).astype(BF16)
+    step = 512
+    for start in range(0, h_ref.shape[0], step):
+        at = slice(start, start + step)
+        k_ref[at, :] = dot(h_ref[at, :], w_ref[:, width : 2 * width]).astype(BF16)
+        v_ref[at, :] = dot(h_ref[at, :], w_ref[:, 2 * width : 3 * width]).astype(BF16)
+
+
+GELU_C = math.sqrt(2.0 / math.pi)
+
+
+def ffn_kernel(me_ref, att_ref, x_ref, cot_ref, gains_ref, *refs, ff):
+    mid_parts, back_parts = refs[:4], refs[4:8]
+    states_ref, one_ref, do_ref, gain_grads_ref, back_keep, back_send, mid_keep, mid_send = refs[8:16]
+    mid_ref, back_ref, dmid_ref, dback_ref, mid_sems, back_sems, mid_out_sems, back_out_sems = refs[16:]
+    me = me_ref[0]
+    width = att_ref.shape[1]
+    mid_rows = width // PEERS
+    back_rows = ff // PEERS
+    mid_copies = load_shards(mid_parts, me, mid_ref, mid_sems, mid_rows, True)
+    back_copies = load_shards(back_parts, me, back_ref, back_sems, back_rows, False)
+    gain_two = gains_ref[1:2, :]
+    gain_three = gains_ref[2:3, :]
+    w_out = slice(0, width)
+    w_in = slice(width, width + ff)
+    w_proj = slice(width + ff, mid_ref.shape[1])
+    wait_all(mid_copies)
+    resid_one = wide(x_ref[:TILE, :]) + dot(att_ref[...], mid_ref[:, w_out])
+    unit_two, scale_two = normed(resid_one)
+    hidden_two = (unit_two * gain_two).astype(BF16)
+    up = dot(hidden_two, mid_ref[:, w_in])
+    inner = GELU_C * (up + 0.044715 * (up * up * up))
+    bent = jnp.tanh(inner)
+    active = (0.5 * up * (1.0 + bent)).astype(BF16)
+    slope = 0.5 * (1.0 + bent) + 0.5 * up * (1.0 - bent * bent) * (GELU_C * (1.0 + 3.0 * 0.044715 * (up * up)))
+    wait_all(back_copies)
+    resid_two = resid_one + dot(active, back_ref[...])
+    unit_three, scale_three = normed(resid_two)
+    final = (unit_three * gain_three).astype(BF16)
+    states_ref[...] = dot(final, mid_ref[:, w_proj]).astype(BF16)
+    grad_final = dot_nt(cot_ref[...], mid_ref[:, w_proj])
+    grad_two = norm_back(grad_final, gain_three, unit_three, scale_three)
+    branch = grad_two.astype(BF16)
+    put_blocks(dback_ref, slice(None), dot_tn(active, branch))
+    back_out = store_blocks(dback_ref, me, (back_keep, back_send), back_out_sems)
+    grad_up = (dot_nt(branch, back_ref[...]) * slope).astype(BF16)
+    grad_hidden = dot_nt(grad_up, mid_ref[:, w_in])
+    grad_one = grad_two + norm_back(grad_hidden, gain_two, unit_two, scale_two)
+    one_ref[...] = grad_one
+    grad_attn = grad_one.astype(BF16)
+    do_ref[...] = dot_nt(grad_attn, mid_ref[:, w_out]).astype(BF16)
+    put_blocks(dmid_ref, w_out, dot_tn(att_ref[...], grad_attn))
+    put_blocks(dmid_ref, w_in, dot_tn(hidden_two, grad_up))
+    put_blocks(dmid_ref, w_proj, dot_tn(final, cot_ref[...]))
+    mid_out = store_blocks(dmid_ref, me, (mid_keep, mid_send), mid_out_sems)
+    gain_grads_ref[...] = jnp.zeros_like(gain_grads_ref)
+    gain_grads_ref[1:2, :] = jnp.sum(grad_hidden * unit_two, axis=0, keepdims=True)
+    gain_grads_ref[2:3, :] = jnp.sum(grad_final * unit_three, axis=0, keepdims=True)
+    wait_all(back_out)
+    wait_all(mid_out)
+
+
+def rows_grad_kernel(me_ref, x_ref, rest_ref, *refs, blocks, rows):
+    halves = [refs[3 * i : 3 * i + 3] for i in range(2)]
+    parts = refs[6:10]
+    dh_ref, gain_grad_ref, w_ref, grad_ref, sems = refs[-5:]
+    me = me_ref[0]
+    own = lax.rem(me, blocks)
+    width = grad_ref.shape[1]
+    span = width // 2
+    own_at = pl.ds(pl.multiple_of(own * TILE, TILE), TILE)
+    wait_all(load_shards(parts, me, w_ref, sems, rows, True))
+    for i, (dq_ref, dk_ref, dv_ref) in enumerate(halves):
+        grad = dot_nt(dk_ref[...], w_ref[:, width + i * span : width + (i + 1) * span])
+        grad = grad + dot_nt(dv_ref[...], w_ref[:, 2 * width + i * span : 2 * width + (i + 1) * span])
+        grad_ref[...] = grad if i == 0 else grad_ref[...] + grad
+        grad_ref[own_at, :] = grad_ref[own_at, :] + dot_nt(dq_ref[...], w_ref[:, i * span : (i + 1) * span])
+    gain_grad = jnp.zeros((1, width), F32)
+    core = lax.rem(me // CORE_BIT, 2)
+    for r in range(blocks):
+        block = own ^ ((r & 1) * Y_BIT | depth_mask(r >> 1, core))
+        at = pl.ds(pl.multiple_of(block * TILE, TILE), TILE)
+        grad = grad_ref[at, :]
+        source = rest_ref if r // 4 else x_ref
+        unit, scale = normed(wide(source[r % 4, :TILE, :]))
+        gain_grad = gain_grad + jnp.sum(grad * unit, axis=0, keepdims=True)
+        dh_ref[r] = grad.astype(BF16)
+    gain_grad_ref[...] = jnp.broadcast_to(gain_grad, gain_grad_ref.shape)
+
+
+def qkv_grad_kernel(me_ref, h_ref, gain_grads_ref, gain_grad_ref, *refs, marks, blocks):
+    halves = [refs[3 * i : 3 * i + 3] for i in range(2)]
+    keep, send, dw_ref, out_sems = refs[6 + marks :]
+    me = me_ref[0]
+    own = lax.rem(me, blocks)
+    width = h_ref.shape[1]
+    span = width // 2
+    own_at = pl.ds(pl.multiple_of(own * TILE, TILE), TILE)
+    for i, (dq_ref, dk_ref, dv_ref) in enumerate(halves):
+        put_blocks(dw_ref, slice(i * span, (i + 1) * span), dot_tn(h_ref[own_at, :], dq_ref[...]))
+        put_blocks(dw_ref, slice(width + i * span, width + (i + 1) * span), dot_tn(h_ref[...], dk_ref[...]))
+        put_blocks(dw_ref, slice(2 * width + i * span, 2 * width + (i + 1) * span), dot_tn(h_ref[...], dv_ref[...]))
+    row = lax.broadcasted_iota(jnp.int32, (TILE, width), 0)
+    rows_of = jnp.where(row == 0, gain_grad_ref[:1, :], jnp.where(row == 1, gain_grads_ref[1:2, :], gain_grads_ref[2:3, :]))
+    put_blocks(dw_ref, slice(3 * width, 3 * width + TILE), rows_of.T)
+    wait_all(store_blocks(dw_ref, me, (keep, send), out_sems))
+
+
+def shaped(dims, kind):
+    return jax.ShapeDtypeStruct(dims, kind)
+
+
+def cube_body(inputs, segments, w_query, w_key, w_value, w_out, w_in, w_back, w_proj, gain_attn, gain_ffn, gain_final, rel_table, cotangent):
+    blocks = lax.axis_size("blk")
+    tokens, width = inputs.shape[1:]
+    ff = w_in.shape[1]
+    proj = w_proj.shape[1]
+    heads = rel_table.shape[1]
+    length = tokens * blocks
+    rows = w_query.shape[0]
+    back_rows = w_back.shape[0]
+    own = lax.axis_index("blk").reshape(1).astype(jnp.int32)
+    me = (lax.axis_index("head") * blocks + lax.axis_index("blk")).reshape(1).astype(jnp.int32)
+    params = pltpu.CompilerParams(vmem_limit_bytes=VMEM_LIMIT)
+    dma = pltpu.SemaphoreType.DMA((PEERS,))
+
+    gains = jnp.stack([gain_attn, gain_ffn, gain_final], 1)
+    gains = jnp.pad(gains, ((0, 0), (0, TILE - gains.shape[1])))
+    pack_qkv = jnp.concatenate([w_query, w_key, w_value, gains], 1)
+    pack_mid = jnp.concatenate([w_out, w_in, w_proj], 1)
+    qkv_lanes = pack_qkv.shape[1]
+    mid_lanes = pack_mid.shape[1]
+    seg_row = jnp.pad(segments.astype(BF16), ((0, 7), (0, width - tokens)))
+    own_x = jnp.concatenate([inputs[0], seg_row], 0)
+    x_pair = jnp.stack([own_x, swap(own_x, Y_BIT)])
+    qkv_first = swap(pack_qkv, NEAR_BIT, OVER_BIT)
+    qkv_column = gather_depth(pack_qkv, qkv_first)
+    x_half = jnp.concatenate([x_pair, swap(x_pair, NEAR_BIT, OVER_BIT)], 0)
+    x_rest = swap(x_half, OVER_BIT, NEAR_BIT)
+    qkv_parts = y_pairs(*gather_plane(qkv_column))
+    qkv_parts = qkv_parts + [swap(part, CORE_BIT) for part in qkv_parts]
+    pack_mid = tied(pack_mid, qkv_column)
+    mid_first = swap(pack_mid, NEAR_BIT, OVER_BIT)
+    mid_plane = gather_plane(gather_depth(pack_mid, mid_first))
+    back_column = gather_depth(tied(w_back, mid_first))
+    back_plane = gather_plane(back_column)
+    hidden, key, value, query, gain_rows, kseg = pl.pallas_call(
+        functools.partial(project_kernel, blocks=blocks, rows=rows),
+        in_specs=[SMEM] + [WHOLE] * 2 + [ANY] * 6,
+        out_specs=[WHOLE] * 6,
+        out_shape=[
+            shaped((length, width), BF16),
+            shaped((length, width), BF16),
+            shaped((length, width), BF16),
+            shaped((tokens, width), BF16),
+            shaped((8, width), F32),
+            shaped((blocks, TILE), F32),
+        ],
+        scratch_shapes=[pltpu.VMEM((width, qkv_lanes), BF16), dma],
+        compiler_params=params,
+        cost_estimate=pl.CostEstimate(flops=2 * length * width * 2 * width, transcendentals=0, bytes_accessed=30 << 20),
+        name="project",
+    )(me, x_half, x_rest, *qkv_parts, mid_plane[0], back_column)
+    bias = bias_rows(rel_table)
+    attend, _ = attention_calls(length, width, heads, marks=1)
+    qseg = segments.reshape(tokens, 1).astype(F32)
+    attended, attended_low, lse = attend(own, query, key, value, qseg, kseg, bias, back_plane[0])
+    mid_parts = y_pairs(*(tied(part, attended_low) for part in mid_plane))
+    mid_parts = mid_parts + [swap(part, CORE_BIT) for part in mid_parts]
+    back_parts = [*back_plane, *(swap(part, CORE_BIT) for part in back_plane)]
+    states, grad_one, grad_attended, gain_grads, back_keep, back_send, mid_keep, mid_send = pl.pallas_call(
+        functools.partial(ffn_kernel, ff=ff),
+        in_specs=[SMEM] + [WHOLE] * 4 + [ANY] * 8,
+        out_specs=[WHOLE] * 4 + [ANY] * 4,
+        out_shape=[
+            shaped((tokens, proj), BF16),
+            shaped((tokens, width), F32),
+            shaped((tokens, width), BF16),
+            shaped((8, width), F32),
+            shaped((PEERS // 2, back_rows, width), BF16),
+            shaped((PEERS // 2, back_rows, width), BF16),
+            shaped((PEERS // 2, rows, mid_lanes), BF16),
+            shaped((PEERS // 2, rows, mid_lanes), BF16),
+        ],
+        scratch_shapes=[
+            pltpu.VMEM((width, mid_lanes), BF16),
+            pltpu.VMEM((ff, width), BF16),
+            pltpu.VMEM((PEERS, rows, mid_lanes), BF16),
+            pltpu.VMEM((PEERS, back_rows, width), BF16),
+            dma,
+            dma,
+            dma,
+            dma,
+        ],
+        compiler_params=params,
+        cost_estimate=pl.CostEstimate(flops=6 * 2 * tokens * width * (ff + width), transcendentals=0, bytes_accessed=70 << 20),
+        name="ffn",
+    )(me, attended_low, own_x, cotangent[0], gain_rows, *mid_parts, *back_parts)
+    back_terms = [back_keep, swap(back_send, CORE_BIT)]
+    mid_terms = [mid_keep, swap(mid_send, CORE_BIT)]
+    common = (own, query, key, value, grad_attended, attended, lse, qseg, kseg, bias)
+    _, attend_back = attention_calls(length, width, heads, 0, heads // 4)
+    *first_grads, first_sums = attend_back(*common)
+    back_sent, mid_sent = next_sent(back_terms), next_sent(mid_terms)
+    _, attend_back = attention_calls(length, width, heads, heads // 4, heads // 4, marks=2)
+    *second_grads, second_sums = attend_back(*common, back_sent, mid_sent)
+    back_terms = halved(back_terms, FIRST_SIDE, back_sent)
+    mid_terms = halved(mid_terms, FIRST_SIDE, mid_sent)
+    back_sent, mid_sent = next_sent(back_terms), next_sent(mid_terms)
+    grad_parts = (*first_grads, *second_grads)
+    grad_rows, gain_grad = pl.pallas_call(
+        functools.partial(rows_grad_kernel, blocks=blocks, rows=rows),
+        in_specs=[SMEM] + [WHOLE] * 8 + [ANY] * 5,
+        out_specs=[WHOLE] * 2,
+        out_shape=[shaped((blocks, tokens, width), BF16), shaped((8, width), F32)],
+        scratch_shapes=[pltpu.VMEM((width, qkv_lanes), BF16), pltpu.VMEM((length, width), F32), dma],
+        compiler_params=params,
+        cost_estimate=pl.CostEstimate(flops=2 * 2 * length * width * width, transcendentals=0, bytes_accessed=30 << 20),
+        name="rows_grad",
+    )(me, x_half, x_rest, *grad_parts, *qkv_parts, back_sent)
+    back_terms = halved(back_terms, SECOND_SIDE, back_sent)
+    back_sent = next_sent(back_terms)
+    marks = (mid_sent, back_sent)
+    qkv_keep, qkv_send = pl.pallas_call(
+        functools.partial(qkv_grad_kernel, marks=len(marks), blocks=blocks),
+        in_specs=[SMEM] + [WHOLE] * 9 + [ANY] * len(marks),
+        out_specs=[ANY, ANY],
+        out_shape=[shaped((PEERS // 2, rows, qkv_lanes), BF16), shaped((PEERS // 2, rows, qkv_lanes), BF16)],
+        scratch_shapes=[pltpu.VMEM((PEERS, rows, qkv_lanes), BF16), dma],
+        compiler_params=params,
+        cost_estimate=pl.CostEstimate(flops=2 * 2 * length * width * width, transcendentals=0, bytes_accessed=30 << 20),
+        name="qkv_grad",
+    )(me, hidden, gain_grads, gain_grad, *grad_parts, *marks)
+    mid_terms = halved(mid_terms, SECOND_SIDE, mid_sent)
+    mid_sent = next_sent(mid_terms)
+    back_terms = halved(back_terms, FIRST_DEPTH, back_sent)
+    back_sent = next_sent(back_terms)
+    row_terms = halved([grad_rows], FIRST_DEPTH)
+    row_sent = next_sent(row_terms)
+    qkv_terms = [qkv_keep, swap(qkv_send, CORE_BIT)]
+    qkv_terms = halved(qkv_terms, FIRST_SIDE, tied(next_sent(qkv_terms), mid_sent, back_sent, row_sent))
+    mid_terms = halved(mid_terms, FIRST_DEPTH, mid_sent)
+    mid_sent = next_sent(mid_terms)
+    reduced_back = part_of(halved(back_terms, SECOND_DEPTH, back_sent), 0, 1)[0]
+    row_terms = halved(row_terms, SECOND_DEPTH, row_sent)
+    row_sent = next_sent(row_terms)
+    qkv_terms = halved(qkv_terms, SECOND_SIDE, tied(next_sent(qkv_terms), mid_sent, row_sent))
+    qkv_terms = halved(halved(qkv_terms, FIRST_DEPTH), SECOND_DEPTH)
+    reduced_mid = part_of(halved(mid_terms, SECOND_DEPTH, mid_sent), 0, 1)[0]
+    reduced_qkv = part_of(qkv_terms, 0, 1)[0]
+    grad_hidden = part_of(halved(row_terms, (Y_BIT,), row_sent), 0, 1)[0]
+    sums = jnp.concatenate([first_sums, second_sums], 0)
+    unit, scale = normed(wide(inputs[0]))
+    input_gradient_rows = grad_one + norm_back(grad_hidden, gain_rows[0], unit, scale)
+    table = table_grad(sums, heads, rel_table.shape[0])
+    every = lax.all_to_all(jnp.broadcast_to(table, (PEERS,) + table.shape), AXES, 0, 0)
+    table = jnp.sum(every, axis=0)
+    return outputs_of(states, input_gradient_rows, reduced_qkv, reduced_mid, reduced_back, table, width, ff, heads)
+
+
+def body(*args):
+    cube = lax.axis_size("head") == 4 and lax.axis_size("blk") == 8
+    return (cube_body if cube else general_body)(*args)
 
 
 def solution(mesh):

time: 427 us -> 300 us (0.70)
  waiting for transfers between devices: 234 us -> 94.6 us
  Pallas kernels: 20.8 us -> 71.5 us
  matrix products: 40.8 us -> 1.47 us
  starting transfers between devices: 48.2 us -> 62.8 us
  local copies, waits for them, and re-layouts: 29.1 us -> 17.5 us
  between operations: 2.06 us -> 11.8 us
  other arithmetic: 46.4 us -> 38.8 us
    ppermute x44 -> x39, waiting for transfers between devices: 234 us -> 94.6 us  [swap(): lax.ppermute(value, AXES, [(i, i ^ masks[i // CORE_BIT % 2]) for i in ran...]
    pallas_call x2 -> x7, Pallas kernels: 20.8 us -> 71.5 us  [the longest x1 20.7 us: cube_body(): pl.pallas_call(functools.partial(ffn_kernel, ff=ff), in_specs=[SMEM] + [W...]
    dot_general x23 -> x1, matrix products: 40.8 us -> 0.8 us  [bias_rows(): lax.dot_general(rel_table, jnp.asarray(onehot, BF16), (((0,), (1,)), ((),...]
    convert_element_type x2 -> x13, other arithmetic: 0.61 us -> 16.9 us  [the longest x12 15.6 us: next_sent(): return part_of(terms, half, 2 * half).astype(BF16)]
    add x20 -> x0, other arithmetic: 15.1 us -> none  [the longest x14 14.3 us: scatter_sum(): value = kept.astype(F32) + links.swap(sent, bit).astype(F32)]
    convert_element_type x19 -> x1, local copies, waits for them, and re-layouts: 10.9 us -> 0.74 us  [cube_body(): qseg = segments.reshape(tokens, 1).astype(F32)]
    concatenate x2 -> x0, local copies, waits for them, and re-layouts: 9.53 us -> none  [the longest x1 8.83 us: body(): jnp.concatenate([grad_query, grad_key, grad_value, gain_grads], 1)]
    ppermute x44 -> x39, starting transfers between devices: 48.2 us -> 57.7 us  [swap(): lax.ppermute(value, AXES, [(i, i ^ masks[i // CORE_BIT % 2]) for i in ran...]
  transfers between devices with their start and end apart: 44 -> 40, of which waited for: 24 -> 17; matrix products, arithmetic and copies ran while one was open for 18% -> 16% of each run, Pallas kernels for 2% -> 17%
where the time goes in v2:
time: 300 us; the launch traced here: 298 us
  waiting for transfers between devices  94.6 us (32%)
  Pallas kernels  71.5 us (24%)
  starting transfers between devices  62.8 us (21%)
  other arithmetic  38.8 us (13%)
  local copies, waits for them, and re-layouts  17.5 us (6%)
  between operations  11.8 us (4%)
    ppermute x39, waiting for transfers between devices, swap(): lax.ppermute(value, AXES, [(i, i ^ masks[i // CORE_BIT % 2]) for i in ran...  94.6 us
    ppermute x39, starting transfers between devices, swap(): lax.ppermute(value, AXES, [(i, i ^ masks[i // CORE_BIT % 2]) for i in ran...  57.7 us
    pallas_call x1, Pallas kernels, cube_body(): pl.pallas_call(functools.partial(ffn_kernel, ff=ff), in_specs=[SMEM] + [W...  20.7 us
    convert_element_type x12, other arithmetic, next_sent(): return part_of(terms, half, 2 * half).astype(BF16)  15.6 us
    pallas_call x1, Pallas kernels, cube_body(): pl.pallas_call(functools.partial(rows_grad_kernel, blocks=blocks, rows=ro...  10.3 us
    pallas_call x1, Pallas kernels, cube_body(): pl.pallas_call(functools.partial(project_kernel, blocks=blocks, rows=rows...  9.01 us
    pallas_call x1, Pallas kernels, cube_body(): pl.pallas_call(functools.partial(qkv_grad_kernel, marks=len(marks), block...  8.38 us
    pallas_call x1, Pallas kernels, cube_body(): attend(own, query, key, value, qseg, kseg, bias, back_plane[0])  7.97 us
  transfers between devices with their start and end apart: 40, of which 17 were waited for; matrix products, arithmetic and copies ran while one was open for 16% of the time, Pallas kernels for 17%

profile of v2, /device:TPU:0, one launch (start us, length us, event | category | flops | bytes accessed | tf_op | source)
XLA Modules:
  0.0 298.4 jit_solution(3373135038447714417)
XLA Ops:
  2.4 3.1 %collective-permute-start.3 = (bf16[24,2432]{1,0:T(8,128)(2,1)S(1)}, bf16[24,2432]{1,0:T(8,128)(2,1)S(1)}, u32[]{:S(2)}, u32[]{:S(2)}) collective-permute-start(bf16[24,2432]{1,0:T(8,128)(2,1)S(1)} %fusion.13), channel_id=1, source_target_pairs={{0,2},{1,3},{2,0},{3,1},{4,6},{5,7},{6,4},{7,5},{8,12},{9,13},{10,... | collective-permute-start | bytes 350216 | tf_op jit(solution)/shard_map/ppermute | solution.py:446
  9.1 1.2 convert_bitcast_fusion
  11.4 2.0 collective-permute-start
  13.4 2.7 collective-permute-start.4
  16.1 5.9 %collective-permute-done.4 = bf16[2,24,2432]{2,1,0:T(8,128)(2,1)S(1)} collective-permute-done((bf16[2,24,2432]{2,1,0:T(8,128)(2,1)S(1)}, bf16[2,24,2432]{2,1,0:T(8,128)(2,1)S(1)}, u32[]{:S(2)}, u32[]{:S(2)}) %collective-permute-start.4) | collective-permute-done | bytes 233504 | tf_op jit(solution)/shard_map/ppermute | solution.py:446
  22.6 1.9 collective-permute-start.10
  26.3 3.5 %collective-permute-start.12 = (bf16[96,768]{1,0:T(8,128)(2,1)S(1)}, bf16[96,768]{1,0:T(8,128)(2,1)S(1)}, u32[]{:S(2)}, u32[]{:S(2)}) collective-permute-start(bf16[96,768]{1,0:T(8,128)(2,1)S(1)} %broadcast_select_fusion.6), channel_id=1, source_target_pairs={{0,2},{1,3},{2,0},{3,1},{4,6},{5,7},{6,4},{7,5},{8,12},{9,13},{10,... | collective-permute-start | bytes 442376 | tf_op jit(solution)/shard_map/ppermute | solution.py:446
  30.9 1.6 collective-permute-start.6
  32.5 2.5 collective-permute-start.1
  35.0 1.8 collective-permute-done.12
  36.9 4.7 %collective-permute-start.13 = (bf16[2,96,768]{2,1,0:T(8,128)(2,1)S(1)}, bf16[2,96,768]{2,1,0:T(8,128)(2,1)S(1)}, u32[]{:S(2)}, u32[]{:S(2)}) collective-permute-start(bf16[2,96,768]{2,1,0:T(8,128)(2,1)S(1)} %pad_maximum_fusion.9), channel_id=1, source_target_pairs={{0,4},{1,5},{2,6},{3,7},{4,0},{5,1},{6,2},{7,3},{8,10},{9,11},{10,... | collective-permute-start | bytes 884744 | tf_op jit(solution)/shard_map/ppermute | solution.py:446
  41.6 2.4 collective-permute-done.10
  44.1 1.6 collective-permute-start.11
  45.7 5.4 %collective-permute-done.1 = bf16[2,136,768]{2,1,0:T(8,128)(2,1)S(1)} collective-permute-done((bf16[2,136,768]{2,1,0:T(8,128)(2,1)S(1)}, bf16[2,136,768]{2,1,0:T(8,128)(2,1)S(1)}, u32[]{:S(2)}, u32[]{:S(2)}) %collective-permute-start.1) | collective-permute-done | bytes 417824 | tf_op jit(solution)/shard_map/ppermute | solution.py:446
  51.2 7.5 %collective-permute-start.2 = (bf16[4,136,768]{2,1,0:T(8,128)(2,1)S(1)}, bf16[4,136,768]{2,1,0:T(8,128)(2,1)}, u32[]{:S(2)}, u32[]{:S(2)}) collective-permute-start(bf16[4,136,768]{2,1,0:T(8,128)(2,1)S(1)} %pad_maximum_fusion.3.refs_0_.x_ref), channel_id=1, source_target_pairs={{0,4},{1,5},{2,6},{3,7},{4,0},{5,1},{6,2},{7,3},{8,10},{9,11},{10,... | collective-permute-start | bytes 2506760 | tf_op jit(solution)/shard_map/ppermute | solution.py:446
  60.1 1.6 pad_maximum_fusion.refs_6_
  61.7 1.2 collective-permute-start.15
  65.5 15.0 %collective-permute-done.14 = bf16[4,96,768]{2,1,0:T(8,128)(2,1)} collective-permute-done((bf16[4,96,768]{2,1,0:T(8,128)(2,1)}, bf16[4,96,768]{2,1,0:T(8,128)(2,1)}, u32[]{:S(2)}, u32[]{:S(2)}) %collective-permute-start.14) | collective-permute-done | bytes 589856 | tf_op jit(solution)/shard_map/ppermute | solution.py:446
  80.5 2.4 pad_maximum_fusion.1.refs_0_.refs_4_
  83.8 9.0 %project.1 = (bf16[1024,768]{1,0:T(8,128)(2,1)}, bf16[1024,768]{1,0:T(8,128)(2,1)}, bf16[1024,768]{1,0:T(8,128)(2,1)}, bf16[128,768]{1,0:T(8,128)(2,1)}, f32[8,768]{1,0:T(8,128)}, /*index=5*/f32[8,128]{1,0:T(8,128)}) custom-call(s32[1]{0:T(128)} %bitcast.me_ref, bf16[4,136,768]{2,1,0:T(8,128)(2,1)} %copy-done.6, ...), custom_call_target="tpu_custom_call" | custom-call | flops 2415919104 | bytes 31457280 | tf_op jit(solution)/shard_map/project/pallas_call | solution.py:742
  92.8 8.0 %attend.1 = (f32[128,768]{1,0:T(8,128)}, bf16[128,768]{1,0:T(8,128)(2,1)}, f32[1536,128]{1,0:T(8,128)}) custom-call(s32[1]{0:T(128)} %bitcast.1.own_ref, bf16[128,768]{1,0:T(8,128)(2,1)} %get-tuple-element.42.q_ref, bf16[1024,768]{1,0:T(8,128)(2,1)} %get-tuple-element.43.k_ref, bf16[1024,768]{1,0:T(8,128)(2,1)} %get-tuple-element.44.v_ref, ...), custom_call_target="tpu_custom_call" | custom-call | bytes 31457280 | tf_op jit(solution)/shard_map/attend/pallas_call | solution.py:762
  100.8 1.1 slice.380
  103.5 1.5 broadcast_select_fusion.1
  106.9 5.6 %collective-permute-done.19.refs_6_ = bf16[8,96,768]{2,1,0:T(8,128)(2,1)S(1)} collective-permute-done((bf16[8,96,768]{2,1,0:T(8,128)(2,1)}, bf16[8,96,768]{2,1,0:T(8,128)(2,1)S(1)}, u32[]{:S(2)}, u32[]{:S(2)}) %collective-permute-start.19) | collective-permute-done | bytes 1179680 | tf_op jit(solution)/shard_map/ppermute | solution.py:446
  112.5 2.2 collective-permute-done.20.refs_7_
  114.7 1.0 copy-done.39
  116.8 20.7 %ffn.1 = (bf16[128,128]{1,0:T(8,128)(2,1)}, f32[128,768]{1,0:T(8,128)}, bf16[128,768]{1,0:T(8,128)(2,1)}, f32[8,768]{1,0:T(8,128)}, bf16[16,96,768]{2,1,0:T(8,12...) custom-call(s32[1]{0:T(128)} %bitcast.me_ref, ...), custom_call_target="tpu_custom_call" | custom-call | flops 4529848320 | bytes 73400320 | tf_op jit(solution)/shard_map/ffn/pallas_call | solution.py:766
  138.1 8.6 %collective-permute-done.21 = bf16[16,96,768]{2,1,0:T(8,128)(2,1)S(1)} collective-permute-done((bf16[16,96,768]{2,1,0:T(8,128)(2,1)}, bf16[16,96,768]{2,1,0:T(8,128)(2,1)S(1)}, u32[]{:S(2)}, u32[]{:S(2)}) %collective-permute-start.21) | collective-permute-done | bytes 2359328 | tf_op jit(solution)/shard_map/ppermute | solution.py:446
  146.7 2.5 add_convert_fusion.1.refs_0_
  149.2 1.2 collective-permute-start.23
  150.9 1.2 copy-done.12
  152.9 12.6 %collective-permute-done.23 = bf16[8,96,768]{2,1,0:T(8,128)(2,1)} collective-permute-done((bf16[8,96,768]{2,1,0:T(8,128)(2,1)S(1)}, bf16[8,96,768]{2,1,0:T(8,128)(2,1)}, u32[]{:S(2)}, u32[]{:S(2)}) %collective-permute-start.23) | collective-permute-done | bytes 1179680 | tf_op jit(solution)/shard_map/ppermute | solution.py:446
  165.6 1.5 add_convert_fusion.4.refs_10_
  167.1 7.5 %attend_back.2 = (bf16[128,384]{1,0:T(8,128)(2,1)}, bf16[1024,384]{1,0:T(8,128)(2,1)}, bf16[1024,384]{1,0:T(8,128)(2,1)}, f32[3,2,640]{2,1,0:T(2,128)}) custom-call(s32[1]{0:T(128)} %bitcast.1.own_ref, bf16[128,768]{1,0:T(8,128)(2,1)} %get-tuple-element.42.q_ref, bf16[1024,768]{1,0:T(8,128)(2,1)} %get-tuple-element.43.k_ref, ...), custom_call_target="tpu_custom_call" | custom-call | bytes 50331648 | tf_op jit(solution)/shard_map/attend_back/pallas_call | solution.py:798
  174.6 7.7 %attend_back.3 = (bf16[128,384]{1,0:T(8,128)(2,1)}, bf16[1024,384]{1,0:T(8,128)(2,1)}, bf16[1024,384]{1,0:T(8,128)(2,1)}, f32[3,2,640]{2,1,0:T(2,128)}) custom-call(s32[1]{0:T(128)} %bitcast.1.own_ref, bf16[128,768]{1,0:T(8,128)(2,1)} %get-tuple-element.42.q_ref, bf16[1024,768]{1,0:T(8,128)(2,1)} %get-tuple-element.43.k_ref, ...), custom_call_target="tpu_custom_call" | custom-call | bytes 50331648 | tf_op jit(solution)/shard_map/attend_back/pallas_call | solution.py:801
  184.7 5.1 %all-to-all-start = ((f32[32,32,128]{2,1,0:T(8,128)}), f32[32,32,128]{2,1,0:T(8,128)S(1)}, u32[]{:S(2)}, u32[]{:S(2)}) async-start(f32[32,32,128]{2,1,0:T(8,128)} %broadcast_in_dim.32), calls=%async_computation | async-start | bytes 1048576 | tf_op jit(solution)/shard_map/all_to_all | solution.py:851
  189.8 10.3 %rows_grad.1 = (bf16[8,128,768]{2,1,0:T(8,128)(2,1)}, f32[8,768]{1,0:T(8,128)}) custom-call(s32[1]{0:T(128)} %bitcast.me_ref, bf16[4,136,768]{2,1,0:T(8,128)(2,1)} %copy-done.6, bf16[4,136,768]{2,1,0:T(8,128)(2,1)} %collective-permute-done.2.refs_1_.rest_ref, bf16[128,384]{1,0:T(8,128)(2,1)} %get-tuple-element.53.refs_0_, ...), custom_call_target="tpu_custom_call" | custom-call | flops 2415919104 | bytes 31457280 | tf_op jit(solution)/shard_map/rows_grad/pallas_call | solution.py:806
  200.1 2.1 slice.393
  202.2 2.5 collective-permute-start.24
  204.6 2.1 add_convert_fusion.8.refs_7_
  206.7 2.7 add_convert_fusion.3.refs_6_
  209.5 8.4 %qkv_grad.1 = (bf16[16,24,2432]{2,1,0:T(8,128)(2,1)}, bf16[16,24,2432]{2,1,0:T(8,128)(2,1)}) custom-call(s32[1]{0:T(128)} %bitcast.me_ref, bf16[1024,768]{1,0:T(8,128)(2,1)} %get-tuple-element.64.h_ref, f32[8,768]{1,0:T(8,128)} %get-tuple-element.65.gain_grads_ref, f32[8,768]{1,0:T(8,128)} %get-tuple-element.66.gain_grad_ref, ...), custom_call_target="tpu_custom_call" | custom-call | flops 2415919104 | bytes 31457280 | tf_op jit(solution)/shard_map/qkv_grad/pallas_call | solution.py:819
  218.1 1.5 collective-permute-start.30
  219.6 1.4 collective-permute-start.31
  222.9 2.5 collective-permute-start.25
  227.2 9.3 %collective-permute-done.31 = bf16[2,96,768]{2,1,0:T(8,128)(2,1)} collective-permute-done((bf16[2,96,768]{2,1,0:T(8,128)(2,1)}, bf16[2,96,768]{2,1,0:T(8,128)(2,1)}, u32[]{:S(2)}, u32[]{:S(2)}) %collective-permute-start.31) | collective-permute-done | bytes 294944 | tf_op jit(solution)/shard_map/ppermute | solution.py:446
  236.5 1.3 add_convert_fusion.12
  237.8 2.0 collective-permute-start.38
  241.6 1.5 add_convert_fusion.7
  243.1 4.9 %collective-permute-start.33 = (bf16[2,24,3968]{2,1,0:T(8,128)(2,1)S(1)}, bf16[2,24,3968]{2,1,0:T(8,128)(2,1)S(1)}, u32[]{:S(2)}, u32[]{:S(2)}) collective-permute-start(bf16[2,24,3968]{2,1,0:T(8,128)(2,1)S(1)} %add_convert_fusion.7), channel_id=1, source_target_pairs={{0,4},{1,5},{2,6},{3,7},{4,0},{5,1},{6,2},{7,3},{8,10},{9,11},{10,... | collective-permute-start | bytes 1142792 | tf_op jit(solution)/shard_map/ppermute | solution.py:446
  249.8 1.5 fusion
  251.3 1.4 collective-permute-start.32
  253.4 2.0 collective-permute-start.26
  257.2 1.3 add_convert_fusion.11
  260.3 9.7 %collective-permute-done.32 = bf16[8,24,2432]{2,1,0:T(8,128)(2,1)S(1)} collective-permute-done((bf16[8,24,2432]{2,1,0:T(8,128)(2,1)S(1)}, bf16[8,24,2432]{2,1,0:T(8,128)(2,1)S(1)}, u32[]{:S(2)}, u32[]{:S(2)}) %collective-permute-start.32) | collective-permute-done | bytes 933920 | tf_op jit(solution)/shard_map/ppermute | solution.py:446
  270.0 1.2 fusion.3
  271.2 1.5 collective-permute-start.34
  272.7 2.0 add_bitcast_fusion.1
  275.0 4.9 %collective-permute-done.34 = bf16[4,24,2432]{2,1,0:T(8,128)(2,1)S(1)} collective-permute-done((bf16[4,24,2432]{2,1,0:T(8,128)(2,1)S(1)}, bf16[4,24,2432]{2,1,0:T(8,128)(2,1)S(1)}, u32[]{:S(2)}, u32[]{:S(2)}) %collective-permute-start.34) | collective-permute-done | bytes 466976 | tf_op jit(solution)/shard_map/ppermute | solution.py:446
  279.8 1.1 add_convert_fusion.9
  282.1 8.0 %collective-permute-done.35 = bf16[2,24,2432]{2,1,0:T(8,128)(2,1)S(1)} collective-permute-done((bf16[2,24,2432]{2,1,0:T(8,128)(2,1)S(1)}, bf16[2,24,2432]{2,1,0:T(8,128)(2,1)S(1)}, u32[]{:S(2)}, u32[]{:S(2)}) %collective-permute-start.35) | collective-permute-done | bytes 233504 | tf_op jit(solution)/shard_map/ppermute | solution.py:446
  291.2 1.4 add_bitcast_fusion
  294.5 1.5 collective-permute-done.36
  296.0 1.0 add_bitcast_fusion.2
  (178 shorter events, 30.8 us)
Async XLA Ops:
  0.6 64.1 %copy-start = (bf16[32,12]{0,1:T(8,128)(2,1)S(1)}, bf16[32,12]{0,1:T(8,128)(2,1)}, u32[]{:S(2)}) copy-start(bf16[32,12]{0,1:T(8,128)(2,1)} %param.28) | copy-start | bytes 2308
  0.7 15.4 %copy-start.32 = (bf16[24,768]{1,0:T(8,128)(2,1)S(1)}, bf16[24,768]{1,0:T(8,128)(2,1)}, u32[]{:S(2)}) copy-start(bf16[24,768]{1,0:T(8,128)(2,1)} %param.21) | copy-start | bytes 110596
  0.7 15.4 %copy-start.26 = (bf16[24,3072]{1,0:T(8,128)(2,1)S(1)}, bf16[24,3072]{1,0:T(8,128)(2,1)}, u32[]{:S(2)}) copy-start(bf16[24,3072]{1,0:T(8,128)(2,1)} %param.22) | copy-start | bytes 442372
  0.7 15.4 %copy-start.33 = (bf16[24,128]{1,0:T(8,128)(2,1)S(1)}, bf16[24,128]{1,0:T(8,128)(2,1)}, u32[]{:S(2)}) copy-start(bf16[24,128]{1,0:T(8,128)(2,1)} %param.24) | copy-start | bytes 18436
  2.4 11.0 %collective-permute-start.3 = (bf16[24,2432]{1,0:T(8,128)(2,1)S(1)}, bf16[24,2432]{1,0:T(8,128)(2,1)S(1)}, u32[]{:S(2)}, u32[]{:S(2)}) collective-permute-start(bf16[24,2432]{1,0:T(8,128)(2,1)S(1)} %fusion.13), channel_id=1, source_target_pairs={{0,2},{1,3},{2,0},{3,1},{4,6},{5,7},{6,4},{7,5},{8,12},{9,13},{10,... | collective-permute-start | bytes 350216 | tf_op jit(solution)/shard_map/ppermute | solution.py:446
  9.0 13.5 %collective-permute-start.9 = (bf16[24,3968]{1,0:T(8,128)(2,1)S(1)}, bf16[24,3968]{1,0:T(8,128)(2,1)S(1)}, u32[]{:S(2)}, u32[]{:S(2)}) collective-permute-start(bf16[24,3968]{1,0:T(8,128)(2,1)S(1)} %maximum_select_fusion.5), channel_id=1, source_target_pairs={{0,2},{1,3},{2,0},{3,1},{4,6},{5,7},{6,4},{7,5},{8,12},{9,13},{10,... | collective-permute-start | bytes 571400 | tf_op jit(solution)/shard_map/ppermute | solution.py:446
  10.4 15.9 %copy-start.27 = (bf16[96,768]{1,0:T(8,128)(2,1)S(1)}, bf16[96,768]{1,0:T(8,128)(2,1)}, u32[]{:S(2)}) copy-start(bf16[96,768]{1,0:T(8,128)(2,1)} %param.23) | copy-start | bytes 442372
  11.4 19.5 %copy-start.30 = (bf16[136,768]{1,0:T(8,128)(2,1)}, bf16[136,768]{1,0:T(8,128)(2,1)S(1)}, u32[]{:S(2)}) copy-start(bf16[136,768]{1,0:T(8,128)(2,1)S(1)} %get-tuple-element.98.x_ref) | copy-start | bytes 626692
  11.4 21.1 %collective-permute-start = (bf16[136,768]{1,0:T(8,128)(2,1)S(1)}, bf16[136,768]{1,0:T(8,128)(2,1)S(1)}, u32[]{:S(2)}, u32[]{:S(2)}) collective-permute-start(bf16[136,768]{1,0:T(8,128)(2,1)S(1)} %get-tuple-element.98.x_ref), channel_id=1, source_target_pairs={{0,1},{1,0},{2,3},{3,2},{4,5},{5,4},{6,7},{7,6},{8,9},{9,8},{10,11... | collective-permute-start | bytes 626696 | tf_op jit(solution)/shard_map/ppermute | solution.py:446
  13.4 17.5 %copy-start.19 = (bf16[24,2432]{1,0:T(8,128)(2,1)}, bf16[24,2432]{1,0:T(8,128)(2,1)S(1)}, u32[]{:S(2)}) copy-start(bf16[24,2432]{1,0:T(8,128)(2,1)S(1)} %collective-permute-done.3) | copy-start | bytes 350212
  13.4 8.6 %collective-permute-start.4 = (bf16[2,24,2432]{2,1,0:T(8,128)(2,1)S(1)}, bf16[2,24,2432]{2,1,0:T(8,128)(2,1)S(1)}, u32[]{:S(2)}, u32[]{:S(2)}) collective-permute-start(bf16[2,24,2432]{2,1,0:T(8,128)(2,1)S(1)} %pad_maximum_fusion.10), channel_id=1, source_target_pairs={{0,4},{1,5},{2,6},{3,7},{4,0},{5,1},{6,2},{7,3},{8,10},{9,11},{10,... | collective-permute-start | bytes 700424 | tf_op jit(solution)/shard_map/ppermute | solution.py:446
  22.1 8.6 %collective-permute-start.5 = (bf16[4,24,2432]{2,1,0:T(8,128)(2,1)S(1)}, bf16[4,24,2432]{2,1,0:T(8,128)(2,1)S(1)}, u32[]{:S(2)}, u32[]{:S(2)}) collective-permute-start(bf16[4,24,2432]{2,1,0:T(8,128)(2,1)S(1)} %pad_maximum_fusion.6), channel_id=1, source_target_pairs={{0,1},{1,0},{2,3},{3,2},{4,5},{5,4},{6,7},{7,6},{8,24},{9,25},{10,... | collective-permute-start | bytes 1400840 | tf_op jit(solution)/shard_map/ppermute | solution.py:446
  22.5 21.4 %copy-start.8 = (bf16[24,3968]{1,0:T(8,128)(2,1)}, bf16[24,3968]{1,0:T(8,128)(2,1)S(1)}, u32[]{:S(2)}) copy-start(bf16[24,3968]{1,0:T(8,128)(2,1)S(1)} %collective-permute-done.9) | copy-start | bytes 571396
  22.6 21.4 %collective-permute-start.10 = (bf16[2,24,3968]{2,1,0:T(8,128)(2,1)S(1)}, bf16[2,24,3968]{2,1,0:T(8,128)(2,1)S(1)}, u32[]{:S(2)}, u32[]{:S(2)}) collective-permute-start(bf16[2,24,3968]{2,1,0:T(8,128)(2,1)S(1)} %pad_maximum_fusion.8), channel_id=1, source_target_pairs={{0,4},{1,5},{2,6},{3,7},{4,0},{5,1},{6,2},{7,3},{8,10},{9,11},{10,... | collective-permute-start | bytes 1142792 | tf_op jit(solution)/shard_map/ppermute | solution.py:446
  26.3 10.5 %collective-permute-start.12 = (bf16[96,768]{1,0:T(8,128)(2,1)S(1)}, bf16[96,768]{1,0:T(8,128)(2,1)S(1)}, u32[]{:S(2)}, u32[]{:S(2)}) collective-permute-start(bf16[96,768]{1,0:T(8,128)(2,1)S(1)} %broadcast_select_fusion.6), channel_id=1, source_target_pairs={{0,2},{1,3},{2,0},{3,1},{4,6},{5,7},{6,4},{7,5},{8,12},{9,13},{10,... | collective-permute-start | bytes 442376 | tf_op jit(solution)/shard_map/ppermute | solution.py:446
  30.9 27.9 %collective-permute-start.6 = (bf16[8,24,2432]{2,1,0:T(8,128)(2,1)S(1)}, bf16[8,24,2432]{2,1,0:T(8,128)(2,1)S(1)}, u32[]{:S(2)}, u32[]{:S(2)}) collective-permute-start(bf16[8,24,2432]{2,1,0:T(8,128)(2,1)S(1)} %pad_maximum_fusion.2), channel_id=1, source_target_pairs={{0,16},{1,17},{2,18},{3,19},{4,20},{5,21},{6,22},{7,23},{8,9},{9,8... | collective-permute-start | bytes 2801672 | tf_op jit(solution)/shard_map/ppermute | solution.py:446
  32.5 30.5 %copy-start.15 = (bf16[1,96,768]{2,1,0:T(8,128)(2,1)}, bf16[1,96,768]{2,1,0:T(8,128)(2,1)S(1)}, u32[]{:S(2)}) copy-start(bf16[1,96,768]{2,1,0:T(8,128)(2,1)S(1)} %fusion.21) | copy-start | bytes 442372
  32.5 18.6 %collective-permute-start.1 = (bf16[2,136,768]{2,1,0:T(8,128)(2,1)S(1)}, bf16[2,136,768]{2,1,0:T(8,128)(2,1)S(1)}, u32[]{:S(2)}, u32[]{:S(2)}) collective-permute-start(bf16[2,136,768]{2,1,0:T(8,128)(2,1)S(1)} %pad_maximum_fusion.7), channel_id=1, source_target_pairs={{0,2},{1,3},{2,0},{3,1},{4,6},{5,7},{6,4},{7,5},{8,12},{9,13},{10,... | collective-permute-start | bytes 1253384 | tf_op jit(solution)/shard_map/ppermute | solution.py:446
  36.8 26.1 %copy-start.24 = (bf16[96,768]{1,0:T(8,128)(2,1)}, bf16[96,768]{1,0:T(8,128)(2,1)S(1)}, u32[]{:S(2)}) copy-start(bf16[96,768]{1,0:T(8,128)(2,1)S(1)} %collective-permute-done.12) | copy-start | bytes 442372
  36.9 26.1 %collective-permute-start.13 = (bf16[2,96,768]{2,1,0:T(8,128)(2,1)S(1)}, bf16[2,96,768]{2,1,0:T(8,128)(2,1)S(1)}, u32[]{:S(2)}, u32[]{:S(2)}) collective-permute-start(bf16[2,96,768]{2,1,0:T(8,128)(2,1)S(1)} %pad_maximum_fusion.9), channel_id=1, source_target_pairs={{0,4},{1,5},{2,6},{3,7},{4,0},{5,1},{6,2},{7,3},{8,10},{9,11},{10,... | collective-permute-start | bytes 884744 | tf_op jit(solution)/shard_map/ppermute | solution.py:446
  44.1 16.0 %collective-permute-start.11 = (bf16[4,24,3968]{2,1,0:T(8,128)(2,1)S(1)}, bf16[4,24,3968]{2,1,0:T(8,128)(2,1)S(1)}, u32[]{:S(2)}, u32[]{:S(2)}) collective-permute-start(bf16[4,24,3968]{2,1,0:T(8,128)(2,1)S(1)} %pad_maximum_fusion.4), channel_id=1, source_target_pairs={{0,1},{1,0},{2,3},{3,2},{4,5},{5,4},{6,7},{7,6},{8,24},{9,25},{10,... | collective-permute-start | bytes 2285576 | tf_op jit(solution)/shard_map/ppermute | solution.py:446
  51.2 7.8 %copy-start.6 = (bf16[4,136,768]{2,1,0:T(8,128)(2,1)}, bf16[4,136,768]{2,1,0:T(8,128)(2,1)S(1)}, u32[]{:S(2)}) copy-start(bf16[4,136,768]{2,1,0:T(8,128)(2,1)S(1)} %pad_maximum_fusion.3.refs_0_.x_ref) | copy-start | bytes 2506756
  51.2 32.5 %collective-permute-start.2 = (bf16[4,136,768]{2,1,0:T(8,128)(2,1)S(1)}, bf16[4,136,768]{2,1,0:T(8,128)(2,1)}, u32[]{:S(2)}, u32[]{:S(2)}) collective-permute-start(bf16[4,136,768]{2,1,0:T(8,128)(2,1)S(1)} %pad_maximum_fusion.3.refs_0_.x_ref), channel_id=1, source_target_pairs={{0,4},{1,5},{2,6},{3,7},{4,0},{5,1},{6,2},{7,3},{8,10},{9,11},{10,... | collective-permute-start | bytes 2506760 | tf_op jit(solution)/shard_map/ppermute | solution.py:446
  59.1 24.7 %collective-permute-start.8 = (bf16[4,48,2432]{2,1,0:T(8,128)(2,1)S(1)}, bf16[4,48,2432]{2,1,0:T(8,128)(2,1)}, u32[]{:S(2)}, u32[]{:S(2)}) collective-permute-start(bf16[4,48,2432]{2,1,0:T(8,128)(2,1)S(1)} %maximum_select_fusion.3.refs_3_.refs_7_), channel_id=1, source_target_pairs={{0,8},{1,9},{2,10},{3,11},{4,12},{5,13},{6,14},{7,15},{8,0},{9,1},... | collective-permute-start | bytes 2801672 | tf_op jit(solution)/shard_map/ppermute | solution.py:446
  60.0 23.8 %collective-permute-start.7 = (bf16[4,48,2432]{2,1,0:T(8,128)(2,1)S(1)}, bf16[4,48,2432]{2,1,0:T(8,128)(2,1)}, u32[]{:S(2)}, u32[]{:S(2)}) collective-permute-start(bf16[4,48,2432]{2,1,0:T(8,128)(2,1)S(1)} %maximum_select_fusion.2.refs_2_.refs_6_), channel_id=1, source_target_pairs={{0,8},{1,9},{2,10},{3,11},{4,12},{5,13},{6,14},{7,15},{8,0},{9,1},... | collective-permute-start | bytes 2801672 | tf_op jit(solution)/shard_map/ppermute | solution.py:446
  61.7 41.8 %collective-permute-start.15 = (bf16[8,24,3968]{2,1,0:T(8,128)(2,1)}, bf16[8,24,3968]{2,1,0:T(8,128)(2,1)}, u32[]{:S(2)}, u32[]{:S(2)}) collective-permute-start(bf16[8,24,3968]{2,1,0:T(8,128)(2,1)} %pad_maximum_fusion.refs_6_), channel_id=1, source_target_pairs={{0,16},{1,17},{2,18},{3,19},{4,20},{5,21},{6,22},{7,23},{8,9},{9,8... | collective-permute-start | bytes 4571144 | tf_op jit(solution)/shard_map/ppermute | solution.py:446
  63.9 16.6 %collective-permute-start.14 = (bf16[4,96,768]{2,1,0:T(8,128)(2,1)}, bf16[4,96,768]{2,1,0:T(8,128)(2,1)}, u32[]{:S(2)}, u32[]{:S(2)}) collective-permute-start(bf16[4,96,768]{2,1,0:T(8,128)(2,1)} %pad_maximum_fusion.5.refs_7_), channel_id=1, source_target_pairs={{0,1},{1,0},{2,3},{3,2},{4,5},{5,4},{6,7},{7,6},{8,24},{9,25},{10,... | collective-permute-start | bytes 1769480 | tf_op jit(solution)/shard_map/ppermute | solution.py:446
  82.9 23.6 %collective-permute-start.18 = (bf16[8,96,768]{2,1,0:T(8,128)(2,1)}, bf16[8,96,768]{2,1,0:T(8,128)(2,1)}, u32[]{:S(2)}, u32[]{:S(2)}) collective-permute-start(bf16[8,96,768]{2,1,0:T(8,128)(2,1)} %pad_maximum_fusion.1.refs_0_.refs_4_), channel_id=1, source_target_pairs={{0,16},{1,17},{2,18},{3,19},{4,20},{5,21},{6,22},{7,23},{8,9},{9,8... | collective-permute-start | bytes 3538952 | tf_op jit(solution)/shard_map/ppermute | solution.py:446
  92.8 10.4 %copy-start.10 = (bf16[24,3968]{1,0:T(8,128)(2,1)S(1)}, bf16[24,3968]{1,0:T(8,128)(2,1)}, u32[]{:S(2)}) copy-start(bf16[24,3968]{1,0:T(8,128)(2,1)} %copy-done.8) | copy-start | bytes 571396
  92.8 10.4 %copy-start.14 = (bf16[4,24,3968]{2,1,0:T(8,128)(2,1)S(1)}, bf16[4,24,3968]{2,1,0:T(8,128)(2,1)}, u32[]{:S(2)}) copy-start(bf16[4,24,3968]{2,1,0:T(8,128)(2,1)} %copy-done.13) | copy-start | bytes 2285572
  105.5 10.2 %copy-start.22 = (bf16[4,48,3968]{2,1,0:T(8,128)(2,1)}, bf16[4,48,3968]{2,1,0:T(8,128)(2,1)S(1)}, u32[]{:S(2)}) copy-start(bf16[4,48,3968]{2,1,0:T(8,128)(2,1)S(1)} %maximum_select_fusion.1.refs_1_) | copy-start | bytes 4571140
  105.5 9.2 %collective-permute-start.17 = (bf16[4,48,3968]{2,1,0:T(8,128)(2,1)S(1)}, bf16[4,48,3968]{2,1,0:T(8,128)(2,1)S(1)}, u32[]{:S(2)}, u32[]{:S(2)}) collective-permute-start(bf16[4,48,3968]{2,1,0:T(8,128)(2,1)S(1)} %maximum_select_fusion.1.refs_1_), channel_id=1, source_target_pairs={{0,8},{1,9},{2,10},{3,11},{4,12},{5,13},{6,14},{7,15},{8,0},{9,1},... | collective-permute-start | bytes 4571144 | tf_op jit(solution)/shard_map/ppermute | solution.py:446
  105.9 9.8 %copy-start.23 = (bf16[4,48,3968]{2,1,0:T(8,128)(2,1)}, bf16[4,48,3968]{2,1,0:T(8,128)(2,1)S(1)}, u32[]{:S(2)}) copy-start(bf16[4,48,3968]{2,1,0:T(8,128)(2,1)S(1)} %maximum_select_fusion.refs_0_) | copy-start | bytes 4571140
  105.9 8.8 %collective-permute-start.16 = (bf16[4,48,3968]{2,1,0:T(8,128)(2,1)S(1)}, bf16[4,48,3968]{2,1,0:T(8,128)(2,1)S(1)}, u32[]{:S(2)}, u32[]{:S(2)}) collective-permute-start(bf16[4,48,3968]{2,1,0:T(8,128)(2,1)S(1)} %maximum_select_fusion.refs_0_), channel_id=1, source_target_pairs={{0,8},{1,9},{2,10},{3,11},{4,12},{5,13},{6,14},{7,15},{8,0},{9,1},... | collective-permute-start | bytes 4571144 | tf_op jit(solution)/shard_map/ppermute | solution.py:446
  106.4 6.1 %collective-permute-start.19 = (bf16[8,96,768]{2,1,0:T(8,128)(2,1)}, bf16[8,96,768]{2,1,0:T(8,128)(2,1)S(1)}, u32[]{:S(2)}, u32[]{:S(2)}) collective-permute-start(bf16[8,96,768]{2,1,0:T(8,128)(2,1)} %pad_maximum_fusion.1.refs_0_.refs_4_), channel_id=1, source_target_pairs={{0,8},{1,9},{2,10},{3,11},{4,12},{5,13},{6,14},{7,15},{8,0},{9,1},... | collective-permute-start | bytes 3538952 | tf_op jit(solution)/shard_map/ppermute | solution.py:446
  106.5 8.2 %collective-permute-start.20 = (bf16[8,96,768]{2,1,0:T(8,128)(2,1)}, bf16[8,96,768]{2,1,0:T(8,128)(2,1)S(1)}, u32[]{:S(2)}, u32[]{:S(2)}) collective-permute-start(bf16[8,96,768]{2,1,0:T(8,128)(2,1)} %collective-permute-done.18.refs_5_), channel_id=1, source_target_pairs={{0,8},{1,9},{2,10},{3,11},{4,12},{5,13},{6,14},{7,15},{8,0},{9,1},... | collective-permute-start | bytes 3538952 | tf_op jit(solution)/shard_map/ppermute | solution.py:446
  137.5 12.9 %collective-permute-start.22 = (bf16[16,24,3968]{2,1,0:T(8,128)(2,1)}, bf16[16,24,3968]{2,1,0:T(8,128)(2,1)S(1)}, u32[]{:S(2)}, u32[]{:S(2)}) collective-permute-start(bf16[16,24,3968]{2,1,0:T(8,128)(2,1)} %get-tuple-element.59), channel_id=1, source_target_pairs={{0,8},{1,9},{2,10},{3,11},{4,12},{5,13},{6,14},{7,15},{8,0},{9,1},... | collective-permute-start | bytes 9142280 | tf_op jit(solution)/shard_map/ppermute | solution.py:446
  137.7 9.0 %collective-permute-start.21 = (bf16[16,96,768]{2,1,0:T(8,128)(2,1)}, bf16[16,96,768]{2,1,0:T(8,128)(2,1)S(1)}, u32[]{:S(2)}, u32[]{:S(2)}) collective-permute-start(bf16[16,96,768]{2,1,0:T(8,128)(2,1)} %get-tuple-element.57), channel_id=1, source_target_pairs={{0,8},{1,9},{2,10},{3,11},{4,12},{5,13},{6,14},{7,15},{8,0},{9,1},... | collective-permute-start | bytes 7077896 | tf_op jit(solution)/shard_map/ppermute | solution.py:446
  146.7 18.9 %copy-start.17 = (bf16[16,96,768]{2,1,0:T(8,128)(2,1)}, bf16[16,96,768]{2,1,0:T(8,128)(2,1)S(1)}, u32[]{:S(2)}) copy-start(bf16[16,96,768]{2,1,0:T(8,128)(2,1)S(1)} %collective-permute-done.21) | copy-start | bytes 7077892
  149.2 16.4 %collective-permute-start.23 = (bf16[8,96,768]{2,1,0:T(8,128)(2,1)S(1)}, bf16[8,96,768]{2,1,0:T(8,128)(2,1)}, u32[]{:S(2)}, u32[]{:S(2)}) collective-permute-start(bf16[8,96,768]{2,1,0:T(8,128)(2,1)S(1)} %add_convert_fusion.1.refs_0_), channel_id=1, source_target_pairs={{0,16},{1,17},{2,18},{3,19},{4,20},{5,21},{6,22},{7,23},{8,9},{9,8... | collective-permute-start | bytes 3538952 | tf_op jit(solution)/shard_map/ppermute | solution.py:446
  152.1 22.5 %copy-start.2 = (bf16[8,24,3968]{2,1,0:T(8,128)(2,1)}, bf16[8,24,3968]{2,1,0:T(8,128)(2,1)S(1)}, u32[]{:S(2)}) copy-start(bf16[8,24,3968]{2,1,0:T(8,128)(2,1)S(1)} %add_convert_fusion.refs_1_) | copy-start | bytes 4571140
  152.1 54.7 %collective-permute-start.27 = (bf16[8,24,3968]{2,1,0:T(8,128)(2,1)S(1)}, bf16[8,24,3968]{2,1,0:T(8,128)(2,1)}, u32[]{:S(2)}, u32[]{:S(2)}) collective-permute-start(bf16[8,24,3968]{2,1,0:T(8,128)(2,1)S(1)} %add_convert_fusion.refs_1_), channel_id=1, source_target_pairs={{0,16},{1,17},{2,18},{3,19},{4,20},{5,21},{6,22},{7,23},{8,9},{9,8... | collective-permute-start | bytes 4571144 | tf_op jit(solution)/shard_map/ppermute | solution.py:446
  167.0 37.6 %collective-permute-start.28 = (bf16[4,96,768]{2,1,0:T(8,128)(2,1)S(1)}, bf16[4,96,768]{2,1,0:T(8,128)(2,1)}, u32[]{:S(2)}, u32[]{:S(2)}) collective-permute-start(bf16[4,96,768]{2,1,0:T(8,128)(2,1)S(1)} %add_convert_fusion.4.refs_10_), channel_id=1, source_target_pairs={{0,1},{1,0},{2,3},{3,2},{4,5},{5,4},{6,7},{7,6},{8,24},{9,25},{10,... | collective-permute-start | bytes 1769480 | tf_op jit(solution)/shard_map/ppermute | solution.py:446
  174.6 7.7 %copy-start.34 = (f32[3,2,640]{2,1,0:T(2,128)S(1)}, f32[3,2,640]{2,1,0:T(2,128)}, u32[]{:S(2)}) copy-start(f32[3,2,640]{2,1,0:T(2,128)} %get-tuple-element.69) | copy-start | bytes 46084
  174.6 8.5 %copy-start.29 = (f32[640,32]{1,0:T(8,128)S(1)}, f32[640,32]{1,0:T(8,128)}, u32[]{:S(2)}) copy-start(f32[640,32]{1,0:T(8,128)} %constant.54.clone) | copy-start | bytes 245764
  184.7 37.1 %all-to-all-start = ((f32[32,32,128]{2,1,0:T(8,128)}), f32[32,32,128]{2,1,0:T(8,128)S(1)}, u32[]{:S(2)}, u32[]{:S(2)}) async-start(f32[32,32,128]{2,1,0:T(8,128)} %broadcast_in_dim.32), calls=%async_computation | async-start | bytes 1048576 | tf_op jit(solution)/shard_map/all_to_all | solution.py:851
  202.2 20.6 %collective-permute-start.24 = (bf16[4,128,768]{2,1,0:T(8,128)(2,1)}, bf16[4,128,768]{2,1,0:T(8,128)(2,1)S(1)}, u32[]{:S(2)}, u32[]{:S(2)}) collective-permute-start(bf16[4,128,768]{2,1,0:T(8,128)(2,1)} %slice.393), channel_id=1, source_target_pairs={{0,4},{1,5},{2,6},{3,7},{4,0},{5,1},{6,2},{7,3},{8,10},{9,11},{10,... | collective-permute-start | bytes 2359304 | tf_op jit(solution)/shard_map/ppermute | solution.py:446
  209.5 8.5 %copy-start.7 = (bf16[1,128,768]{2,1,0:T(8,128)(2,1)S(1)}, bf16[1,128,768]{2,1,0:T(8,128)(2,1)}, u32[]{:S(2)}) copy-start(bf16[1,128,768]{2,1,0:T(8,128)(2,1)} %param.16) | copy-start | bytes 589828
  209.5 13.3 %copy-start.18 = (bf16[8,128,768]{2,1,0:T(8,128)(2,1)S(1)}, bf16[8,128,768]{2,1,0:T(8,128)(2,1)}, u32[]{:S(2)}) copy-start(bf16[8,128,768]{2,1,0:T(8,128)(2,1)} %get-tuple-element.63) | copy-start | bytes 4718596
  217.9 32.0 %collective-permute-start.29 = (bf16[16,24,2432]{2,1,0:T(8,128)(2,1)}, bf16[16,24,2432]{2,1,0:T(8,128)(2,1)}, u32[]{:S(2)}, u32[]{:S(2)}) collective-permute-start(bf16[16,24,2432]{2,1,0:T(8,128)(2,1)} %get-tuple-element.68), channel_id=1, source_target_pairs={{0,8},{1,9},{2,10},{3,11},{4,12},{5,13},{6,14},{7,15},{8,0},{9,1},... | collective-permute-start | bytes 5603336 | tf_op jit(solution)/shard_map/ppermute | solution.py:446
  218.1 23.5 %collective-permute-start.30 = (bf16[4,24,3968]{2,1,0:T(8,128)(2,1)}, bf16[4,24,3968]{2,1,0:T(8,128)(2,1)}, u32[]{:S(2)}, u32[]{:S(2)}) collective-permute-start(bf16[4,24,3968]{2,1,0:T(8,128)(2,1)} %add_convert_fusion.3.refs_6_), channel_id=1, source_target_pairs={{0,1},{1,0},{2,3},{3,2},{4,5},{5,4},{6,7},{7,6},{8,24},{9,25},{10,... | collective-permute-start | bytes 2285576 | tf_op jit(solution)/shard_map/ppermute | solution.py:446
  219.6 16.9 %collective-permute-start.31 = (bf16[2,96,768]{2,1,0:T(8,128)(2,1)}, bf16[2,96,768]{2,1,0:T(8,128)(2,1)}, u32[]{:S(2)}, u32[]{:S(2)}) collective-permute-start(bf16[2,96,768]{2,1,0:T(8,128)(2,1)} %add_convert_fusion.8.refs_7_), channel_id=1, source_target_pairs={{0,4},{1,5},{2,6},{3,7},{4,0},{5,1},{6,2},{7,3},{8,10},{9,11},{10,... | collective-permute-start | bytes 884744 | tf_op jit(solution)/shard_map/ppermute | solution.py:446
  222.9 26.9 %copy-start.21 = (bf16[16,24,2432]{2,1,0:T(8,128)(2,1)S(1)}, bf16[16,24,2432]{2,1,0:T(8,128)(2,1)}, u32[]{:S(2)}) copy-start(bf16[16,24,2432]{2,1,0:T(8,128)(2,1)} %get-tuple-element.67) | copy-start | bytes 5603332
  222.9 29.9 %collective-permute-start.25 = (bf16[2,128,768]{2,1,0:T(8,128)(2,1)S(1)}, bf16[2,128,768]{2,1,0:T(8,128)(2,1)S(1)}, u32[]{:S(2)}, u32[]{:S(2)}) collective-permute-start(bf16[2,128,768]{2,1,0:T(8,128)(2,1)S(1)} %add_convert_fusion.6), channel_id=1, source_target_pairs={{0,2},{1,3},{2,0},{3,1},{4,6},{5,7},{6,4},{7,5},{8,12},{9,13},{10,... | collective-permute-start | bytes 1179656 | tf_op jit(solution)/shard_map/ppermute | solution.py:446
  237.8 34.9 %collective-permute-start.38 = (bf16[1,96,768]{2,1,0:T(8,128)(2,1)S(1)}, bf16[1,96,768]{2,1,0:T(8,128)(2,1)S(1)}, u32[]{:S(2)}, u32[]{:S(2)}) collective-permute-start(bf16[1,96,768]{2,1,0:T(8,128)(2,1)S(1)} %add_convert_fusion.12), channel_id=1, source_target_pairs={{0,2},{1,3},{2,0},{3,1},{4,6},{5,7},{6,4},{7,5},{8,12},{9,13},{10,... | collective-permute-start | bytes 442376 | tf_op jit(solution)/shard_map/ppermute | solution.py:446
  243.1 14.0 %collective-permute-start.33 = (bf16[2,24,3968]{2,1,0:T(8,128)(2,1)S(1)}, bf16[2,24,3968]{2,1,0:T(8,128)(2,1)S(1)}, u32[]{:S(2)}, u32[]{:S(2)}) collective-permute-start(bf16[2,24,3968]{2,1,0:T(8,128)(2,1)S(1)} %add_convert_fusion.7), channel_id=1, source_target_pairs={{0,4},{1,5},{2,6},{3,7},{4,0},{5,1},{6,2},{7,3},{8,10},{9,11},{10,... | collective-permute-start | bytes 1142792 | tf_op jit(solution)/shard_map/ppermute | solution.py:446
  251.3 18.6 %collective-permute-start.32 = (bf16[8,24,2432]{2,1,0:T(8,128)(2,1)S(1)}, bf16[8,24,2432]{2,1,0:T(8,128)(2,1)S(1)}, u32[]{:S(2)}, u32[]{:S(2)}) collective-permute-start(bf16[8,24,2432]{2,1,0:T(8,128)(2,1)S(1)} %fusion), channel_id=1, source_target_pairs={{0,16},{1,17},{2,18},{3,19},{4,20},{5,21},{6,22},{7,23},{8,9},{9,8... | collective-permute-start | bytes 2801672 | tf_op jit(solution)/shard_map/ppermute | solution.py:446
  253.4 21.3 %collective-permute-start.26 = (bf16[1,128,768]{2,1,0:T(8,128)(2,1)S(1)}, bf16[1,128,768]{2,1,0:T(8,128)(2,1)S(1)}, u32[]{:S(2)}, u32[]{:S(2)}) collective-permute-start(bf16[1,128,768]{2,1,0:T(8,128)(2,1)S(1)} %add_convert_fusion.10), channel_id=1, source_target_pairs={{0,1},{1,0},{2,3},{3,2},{4,5},{5,4},{6,7},{7,6},{8,9},{9,8},{10,11... | collective-permute-start | bytes 589832 | tf_op jit(solution)/shard_map/ppermute | solution.py:446
  271.2 9.9 %copy-start.28 = (f32[128,768]{1,0:T(8,128)S(1)}, f32[128,768]{1,0:T(8,128)}, u32[]{:S(2)}) copy-start(f32[128,768]{1,0:T(8,128)} %get-tuple-element.49) | copy-start | bytes 1179652
  271.2 8.6 %collective-permute-start.34 = (bf16[4,24,2432]{2,1,0:T(8,128)(2,1)S(1)}, bf16[4,24,2432]{2,1,0:T(8,128)(2,1)S(1)}, u32[]{:S(2)}, u32[]{:S(2)}) collective-permute-start(bf16[4,24,2432]{2,1,0:T(8,128)(2,1)S(1)} %fusion.3), channel_id=1, source_target_pairs={{0,1},{1,0},{2,3},{3,2},{4,5},{5,4},{6,7},{7,6},{8,24},{9,25},{10,... | collective-permute-start | bytes 1400840 | tf_op jit(solution)/shard_map/ppermute | solution.py:446
  280.9 9.2 %collective-permute-start.35 = (bf16[2,24,2432]{2,1,0:T(8,128)(2,1)S(1)}, bf16[2,24,2432]{2,1,0:T(8,128)(2,1)S(1)}, u32[]{:S(2)}, u32[]{:S(2)}) collective-permute-start(bf16[2,24,2432]{2,1,0:T(8,128)(2,1)S(1)} %add_convert_fusion.9), channel_id=1, source_target_pairs={{0,4},{1,5},{2,6},{3,7},{4,0},{5,1},{6,2},{7,3},{8,10},{9,11},{10,... | collective-permute-start | bytes 700424 | tf_op jit(solution)/shard_map/ppermute | solution.py:446
  282.0 9.1 %collective-permute-start.37 = (bf16[1,24,3968]{2,1,0:T(8,128)(2,1)S(1)}, bf16[1,24,3968]{2,1,0:T(8,128)(2,1)S(1)}, u32[]{:S(2)}, u32[]{:S(2)}) collective-permute-start(bf16[1,24,3968]{2,1,0:T(8,128)(2,1)S(1)} %add_convert_fusion.11), channel_id=1, source_target_pairs={{0,2},{1,3},{2,0},{3,1},{4,6},{5,7},{6,4},{7,5},{8,12},{9,13},{10,... | collective-permute-start | bytes 571400 | tf_op jit(solution)/shard_map/ppermute | solution.py:446
  290.1 8.3 %copy-start.1 = (bf16[32,12]{0,1:T(8,128)(2,1)S(1)}, bf16[32,12]{0,1:T(8,128)(2,1)}, u32[]{:S(2)}) copy-start(bf16[32,12]{0,1:T(8,128)(2,1)} %param.28) | copy-start | bytes 2308
  291.1 4.9 %collective-permute-start.36 = (bf16[1,24,2432]{2,1,0:T(8,128)(2,1)S(1)}, bf16[1,24,2432]{2,1,0:T(8,128)(2,1)S(1)}, u32[]{:S(2)}, u32[]{:S(2)}) collective-permute-start(bf16[1,24,2432]{2,1,0:T(8,128)(2,1)S(1)} %add_convert_fusion.13), channel_id=1, source_target_pairs={{0,2},{1,3},{2,0},{3,1},{4,6},{5,7},{6,4},{7,5},{8,12},{9,13},{10,... | collective-permute-start | bytes 350216 | tf_op jit(solution)/shard_map/ppermute | solution.py:446
  (16 other events, 43.6 us)
